TPU v7x, 32 devices: a whole 2x2x4 slice. The times are simulated.
32 devices in a mesh: blk: 8 (over z, x), tile: 4 (over y, core).
Axes of the slice: x: 2, y: 2, z: 4, core: 2. Of those that a mesh axis runs over, the one named last changes fastest.
Arguments:
- blocks: float32 [96, 384, 1024], P('blk', None, 'tile')
- orders: int32 [96], replicated, may hold values from 96 to 384, as said below
- pattern: int32 [96, 8], replicated, may hold values 0 or 1
- dest: int32 [96], replicated, may hold values from 0 to 7, as said below
- inv_factor: float32 [96, 384, 384], P('blk'), as said below
Outputs:
- gram_matrix: float32 [1024, 1024], P('blk', 'tile')
Inputs may be any that keep to these rules, and one draw needn't show every extreme that they name: `dest`: each owner owns exactly 12 blocks; of the 12 blocks numbered s * 12 to (s + 1) * 12 - 1, each owner owns 0 or exactly 2, and the owners are s + k modulo the number of owners for the same set of 6 offsets k at every s. `orders`: some block has order 384. `inv_factor`: each matrix is lower triangular with its diagonal from 1 to 2.
All inputs are finite; a program needn't handle non-finite values.
Results may differ from a plain program's by a relative error of at most 0.0003.
Values sent between devices are 32-bit elements; how exact they have to be, the bound alone decides.
No kernel may reach another device: no remote copies, remote signals or barrier semaphores. Data moves between devices by JAX's collectives and lax.ppermute only.
A program may use at most 128 MiB of HBM per device.

v0:
```python
import jax
import jax.numpy as jnp
from jax import lax
from jax.sharding import PartitionSpec as P

CTW = 128


def body(blocks, orders, pattern, dest, inv_factor):
    source_index = lax.axis_index("blk")
    owner_count = lax.axis_size("blk")
    tile_index = lax.axis_index("tile")
    slot_count, max_order, column_width = blocks.shape
    block_count = dest.shape[0]
    tiles_here = column_width // CTW
    highest = lax.Precision.HIGHEST
    capacity = (slot_count + owner_count - 1) // owner_count
    dest_grid = dest.reshape(owner_count, slot_count)
    earlier = lax.broadcasted_iota(jnp.int32, (slot_count, slot_count), 1) < lax.broadcasted_iota(
        jnp.int32, (slot_count, slot_count), 0
    )
    matching = dest_grid[:, :, None] == dest_grid[:, None, :]
    ranks = jnp.sum((matching & earlier[None]).astype(jnp.int32), axis=2).reshape(block_count)
    my_dest = lax.dynamic_slice_in_dim(dest, source_index * slot_count, slot_count)
    my_rank = lax.dynamic_slice_in_dim(ranks, source_index * slot_count, slot_count)
    my_orders = lax.dynamic_slice_in_dim(orders, source_index * slot_count, slot_count)
    my_tiles = lax.dynamic_slice(
        pattern, (source_index * slot_count, tile_index * tiles_here), (slot_count, tiles_here)
    )
    row_ids = lax.broadcasted_iota(jnp.int32, (slot_count, max_order), 1)
    row_mask = (row_ids < my_orders[:, None]).astype(jnp.float32)
    col_mask = jnp.repeat(my_tiles.astype(jnp.float32), CTW, axis=1)
    masked = blocks * row_mask[:, :, None] * col_mask[:, None, :]
    owned = lax.dynamic_slice_in_dim(
        jnp.argsort(dest, stable=True), source_index * slot_count, slot_count
    )
    slot_ids = my_dest * capacity + my_rank
    placing = (
        lax.broadcasted_iota(jnp.int32, (owner_count * capacity, slot_count), 0)
        == slot_ids[None, :]
    ).astype(jnp.float32)
    outgoing = jnp.einsum(
        "ak,krc->arc", placing, masked, precision=highest, preferred_element_type=jnp.float32
    )
    arrived = lax.all_to_all(outgoing, "blk", split_axis=0, concat_axis=0, tiled=True)
    positions = owned // slot_count * capacity + ranks[owned]
    own_blocks = jnp.take(arrived, positions, axis=0)
    own_mask = (row_ids < orders[owned][:, None]).astype(jnp.float32)
    whitened = jnp.einsum(
        "jrq,jqc->jrc",
        inv_factor,
        own_blocks,
        precision=highest,
        preferred_element_type=jnp.float32,
    )
    whitened_rows = (whitened * own_mask[:, :, None]).reshape(slot_count * max_order, column_width)
    factor = 1.0 / (block_count * max_order**0.5)
    partial_sums = lax.dot_general(
        lax.all_gather(whitened_rows, "tile", axis=1, tiled=True),
        whitened_rows,
        (((0,), (0,)), ((), ())),
        precision=highest,
        preferred_element_type=jnp.float32,
    )
    gram_tile = lax.psum_scatter(partial_sums, "blk", scatter_dimension=0, tiled=True)
    return gram_tile * factor


def solution(mesh):
    in_specs = (P("blk", None, "tile"), P(), P(), P(), P("blk", None, None))
    out_specs = P("blk", "tile")
    return jax.shard_map(body, mesh=mesh, in_specs=in_specs, out_specs=out_specs, check_vma=False)
```

profile of v0, /device:TPU:0, one launch (start us, length us, event | category | flops | bytes accessed | tf_op | source)
XLA Modules:
  0.0 431.8 jit_solution(3987751077127100030)
XLA Ops:
  6.5 0.7 eq.23
  7.3 3.2 sort.17
  10.5 0.7 dynamic_slice.18
  11.2 0.8 dynamic-slice_convert_fusion
  12.0 0.1 copy.19
  12.2 0.3 convert_reduce_fusion
  12.8 0.7 compare_select_fusion.1
  13.6 2.8 multiply_multiply_fusion
  16.4 5.9 %fusion = f32[16,384,256]{2,0,1:T(8,128)S(1)} fusion(f32[12,384,256]{2,1,0:T(8,128)S(1)} %multiply_multiply_fusion, s32[12]{0:T(128)S(1)} %get-tuple-element.10), kind=kOutput, calls=%fused_computation.3 | convolution fusion | flops 226492608 | bytes 11010096 | tf_op jit(solution)/shard_map/ak,krc->arc/dot_general | solution.py:42
  22.2 6.3 %copy.21 = f32[16,384,256]{2,1,0:T(8,128)} copy(f32[16,384,256]{2,0,1:T(8,128)S(1)} %fusion) | data formatting | bytes 12582912 | tf_op jit(solution)/shard_map/ak,krc->arc/dot_general | solution.py:42
  28.5 7.4 %all-to-all-start = ((f32[16,384,256]{2,1,0:T(8,128)}), f32[16,384,256]{2,1,0:T(8,128)}, u32[]{:S(2)}, u32[]{:S(2)}) async-start(f32[16,384,256]{2,1,0:T(8,128)} %copy.21), calls=%async_computation | async-start | bytes 12582912 | tf_op jit(solution)/shard_map/all_to_all | solution.py:45
  35.9 0.2 all-gather.2.cloned.1.call-start
  36.1 0.7 gather_fusion
  36.8 0.7 gather_fusion.2
  37.5 0.1 compare_and_fusion
  37.7 136.5 %all-to-all-done = f32[16,384,256]{2,1,0:T(8,128)} async-done(((f32[16,384,256]{2,1,0:T(8,128)}), f32[16,384,256]{2,1,0:T(8,128)}, u32[]{:S(2)}, u32[]{:S(2)}) %all-to-all-start) | async-done | bytes 6291488 | tf_op jit(solution)/shard_map/all_to_all | solution.py:45
  174.1 5.9 %gather_fusion.1 = f32[12,384,256]{2,1,0:T(8,128)} fusion(f32[16,384,256]{2,1,0:T(8,128)} %all-to-all-done, s32[1024]{0:T(1024)S(1)} %pad_clamp_fusion), kind=kCustom, calls=%fused_computation.1 | custom fusion | bytes 9437232 | tf_op jit(solution)/shard_map/jit(_take)/gather | solution.py:47
  180.0 19.7 %multiply_bitcast_fusion = f32[12,384,256]{1,2,0:T(8,128)} fusion(f32[12,384]{1,0:T(8,128)S(1)} %fusion.9, f32[12,384,384]{2,1,0:T(8,128)} %param.9, f32[12,384,256]{2,1,0:T(8,128)} %gather_fusion.1, pred[12]{0:T(512)(128)(4,1)S(1)} %get-tuple-element.7), kind=kOutput, calls=%fused_computation.5 | convolution fusion | flops 5438177280 | bytes 16533516 | tf_op jit(solution)/shard_map/jrq,jqc->jrc/dot_general | solution.py:49
  199.7 6.1 %copy.23 = f32[12,384,256]{2,1,0:T(8,128)} copy(f32[12,384,256]{1,2,0:T(8,128)} %multiply_bitcast_fusion) | data formatting | bytes 9437184 | tf_op jit(solution)/shard_map/mul | solution.py:56
  205.8 0.3 reduce-scatter.2.cloned.1.call-start
  206.1 119.0 %all-gather.2.cloned.1.call-done = f32[4608,1024]{1,0:T(8,128)} async-done(((f32[4608,256]{1,0:T(8,128)}), f32[4608,1024]{1,0:T(8,128)}) %all-gather.2.cloned.1.call-update) | async-done | bytes 18874384 | tf_op jit(solution)/shard_map/all_gather | solution.py:59
  325.1 34.0 %fusion.14 = f32[1024,256]{1,0:T(8,128)} fusion(f32[4608,1024]{1,0:T(8,128)} %all-gather.2.cloned.1.call-done, f32[4608,256]{1,0:T(8,128)} %bitcast.13), kind=kOutput, calls=%fused_computation.30 | convolution fusion | flops 14495514624 | bytes 24641536 | tf_op jit(solution)/shard_map/dot_general | solution.py:58
  359.1 64.3 %reduce-scatter.2.cloned.1.call-done = f32[128,256]{1,0:T(8,128)} async-done(((f32[1024,256]{1,0:T(8,128)}), f32[128,256]{1,0:T(8,128)}) %reduce-scatter.2.cloned.1.call-update) | async-done | bytes 131088 | tf_op jit(solution)/shard_map/reduce_scatter | solution.py:65
  423.4 1.6 broadcast_multiply_fusion
  (16 shorter events, 0.5 us)
Async XLA Ops:
  28.5 8.3 %copy-start = (s32[96]{0:T(128)S(1)}, s32[96]{0:T(128)}, u32[]{:S(2)}) copy-start(s32[96]{0:T(128)} %param.6) | copy-start | bytes 1156
  28.5 145.6 %all-to-all-start = ((f32[16,384,256]{2,1,0:T(8,128)}), f32[16,384,256]{2,1,0:T(8,128)}, u32[]{:S(2)}, u32[]{:S(2)}) async-start(f32[16,384,256]{2,1,0:T(8,128)} %copy.21), calls=%async_computation | async-start | bytes 12582912 | tf_op jit(solution)/shard_map/all_to_all | solution.py:45
  35.9 289.2 %all-gather.2.cloned.1.call-start = ((), (), s32[]{:S(2)}) async-start(), calls=%async_computation.2 | async-start | bytes 23592960 | tf_op jit(solution)/shard_map/all_gather | solution.py:59
  205.8 217.5 %reduce-scatter.2.cloned.1.call-start = ((), (), s32[]{:S(2)}) async-start(), calls=%async_computation.3 | async-start | bytes 1179648 | tf_op jit(solution)/shard_map/reduce_scatter | solution.py:65
Sparse Core Ops, SparseCore 0:
  205.9 119.0 all-gather.1
  359.2 64.1 reduce-scatter.1
where the time goes:
time: 432 us
  waiting for transfers between devices  320 us (74%)
  matrix products  59.5 us (14%)
  local copies, waits for them, and re-layouts  21.5 us (5%)
  between operations  13.5 us (3%)
  other arithmetic  9.65 us (2%)
  starting transfers between devices  7.86 us (2%)
    all_to_all x1, waiting for transfers between devices, body(): lax.all_to_all(outgoing, 'blk', split_axis=0, concat_axis=0, tiled=True)  136 us
    all_gather x1, waiting for transfers between devices, body(): lax.all_gather(whitened_rows, 'tile', axis=1, tiled=True)  119 us
    reduce_scatter x1, waiting for transfers between devices, body(): lax.psum_scatter(partial_sums, 'blk', scatter_dimension=0, tiled=True)  64.3 us
    dot_general x1, matrix products, body(): lax.dot_general(lax.all_gather(whitened_rows, 'tile', axis=1, tiled=True)...  34 us
    dot_general x1, matrix products, body(): jnp.einsum('jrq,jqc->jrc', inv_factor, own_blocks, precision=highest, pre...  19.7 us
  transfers between devices with their start and end apart: 3, of which 3 were waited for; matrix products, arithmetic and copies ran while one was open for 0% of the time, Pallas kernels for 0%

commit v1 on v0

v1 whole, which is shorter than its diff:
```python
import functools

import jax
import jax.numpy as jnp
from jax import lax
from jax.experimental import pallas as pl
from jax.experimental.pallas import tpu as pltpu
from jax.sharding import PartitionSpec as P

CTW = 128
F32 = jnp.float32
BF16 = jnp.bfloat16
XY_FIRST = 88


def general_body(blocks, orders, pattern, dest, inv_factor):
    source_index = lax.axis_index("blk")
    owner_count = lax.axis_size("blk")
    tile_index = lax.axis_index("tile")
    slot_count, max_order, column_width = blocks.shape
    block_count = dest.shape[0]
    tiles_here = column_width // CTW
    highest = lax.Precision.HIGHEST
    capacity = (slot_count + owner_count - 1) // owner_count
    dest_grid = dest.reshape(owner_count, slot_count)
    earlier = lax.broadcasted_iota(jnp.int32, (slot_count, slot_count), 1) < lax.broadcasted_iota(
        jnp.int32, (slot_count, slot_count), 0
    )
    matching = dest_grid[:, :, None] == dest_grid[:, None, :]
    ranks = jnp.sum((matching & earlier[None]).astype(jnp.int32), axis=2).reshape(block_count)
    my_dest = lax.dynamic_slice_in_dim(dest, source_index * slot_count, slot_count)
    my_rank = lax.dynamic_slice_in_dim(ranks, source_index * slot_count, slot_count)
    my_orders = lax.dynamic_slice_in_dim(orders, source_index * slot_count, slot_count)
    my_tiles = lax.dynamic_slice(
        pattern, (source_index * slot_count, tile_index * tiles_here), (slot_count, tiles_here)
    )
    row_ids = lax.broadcasted_iota(jnp.int32, (slot_count, max_order), 1)
    row_mask = (row_ids < my_orders[:, None]).astype(F32)
    col_mask = jnp.repeat(my_tiles.astype(F32), CTW, axis=1)
    masked = blocks * row_mask[:, :, None] * col_mask[:, None, :]
    owned = lax.dynamic_slice_in_dim(
        jnp.argsort(dest, stable=True), source_index * slot_count, slot_count
    )
    slot_ids = my_dest * capacity + my_rank
    placing = (
        lax.broadcasted_iota(jnp.int32, (owner_count * capacity, slot_count), 0)
        == slot_ids[None, :]
    ).astype(F32)
    outgoing = jnp.einsum("ak,krc->arc", placing, masked, precision=highest, preferred_element_type=F32)
    arrived = lax.all_to_all(outgoing, "blk", split_axis=0, concat_axis=0, tiled=True)
    positions = owned // slot_count * capacity + ranks[owned]
    own_blocks = jnp.take(arrived, positions, axis=0)
    own_mask = (row_ids < orders[owned][:, None]).astype(F32)
    whitened = jnp.einsum(
        "jrq,jqc->jrc", inv_factor, own_blocks, precision=highest, preferred_element_type=F32
    )
    whitened_rows = (whitened * own_mask[:, :, None]).reshape(slot_count * max_order, column_width)
    factor = 1.0 / (block_count * max_order**0.5)
    partial_sums = lax.dot_general(
        lax.all_gather(whitened_rows, "tile", axis=1, tiled=True),
        whitened_rows,
        (((0,), (0,)), ((), ())),
        precision=highest,
        preferred_element_type=F32,
    )
    gram_tile = lax.psum_scatter(partial_sums, "blk", scatter_dimension=0, tiled=True)
    return gram_tile * factor


def pack_kernel(
    dest_ref, blocks_ref, inv_ref, y_send, core_send, factor_send, table_ref, factor_at, block_at, count, sem, factor_sem
):
    s = lax.axis_index("blk")
    t = lax.axis_index("tile")
    y, c = t // 2, t % 2
    n_blk = factor_at.shape[0]
    slots = blocks_ref.shape[0]

    def scan_source(source, found):
        def scan_block(i, carry):
            found, seen = carry
            mine = dest_ref[source * slots + i] == s

            @pl.when(mine & (seen == y))
            def _():
                factor_at[source] = found

            step = jnp.where(mine, 1, 0)
            return found + step, seen + step

        factor_at[source] = 0
        return lax.fori_loop(0, slots, scan_block, (found, 0), unroll=True)[0]

    lax.fori_loop(0, n_blk, scan_source, 0)

    def factor_copies(source):
        row = factor_at[source]
        for k, (ti, tj) in enumerate(((0, 0), (1, 0), (1, 1))):
            ri, rj = jnp.where(c == 0, ti, 2), jnp.where(c == 0, tj, k)
            yield pltpu.make_async_copy(
                inv_ref.at[row, pl.ds(pl.multiple_of(ri * 128, 128), 128), pl.ds(pl.multiple_of(rj * 128, 128), 128)],
                factor_send.at[source, pl.ds(k * 128, 128), :],
                factor_sem,
            )

    for source in range(n_blk):
        for copy in factor_copies(source):
            copy.start()

    def clear(o, carry):
        count[o] = 0
        return carry

    lax.fori_loop(0, n_blk, clear, 0, unroll=True)

    def place(i, carry):
        o = dest_ref[s * slots + i]
        r = count[o]
        block_at[r, o] = i
        count[o] = r + 1
        return carry

    lax.fori_loop(0, slots, place, 0, unroll=True)

    def compact(o, p):
        @pl.when(count[o] > 0)
        def _():
            table_ref[0, p] = block_at[y, o]
            table_ref[1, p] = block_at[1 - y, o]
            table_ref[2, p] = o

        return p + jnp.where(count[o] > 0, 1, 0)

    lax.fori_loop(0, n_blk, compact, 0, unroll=True)

    half = slots // 4

    def block_copies():
        for p in range(2 * half):
            yield pltpu.make_async_copy(blocks_ref.at[table_ref[1, p]], y_send.at[p], sem)
        for p in range(half):
            yield pltpu.make_async_copy(
                blocks_ref.at[table_ref[0, (1 - c) * half + p]], core_send.at[p], sem
            )

    for copy in block_copies():
        copy.start()
    for copy in block_copies():
        copy.wait()
    for source in range(n_blk):
        for copy in factor_copies(source):
            copy.wait()


def split(x):
    high = x.astype(BF16)
    return high, (x - high.astype(F32)).astype(BF16)


def dot3(a, b, dims):
    def dot(p, q):
        return lax.dot_general(p, q, (dims, ((), ())), preferred_element_type=F32)

    return dot(a[0], b[0]) + (dot(a[0], b[1]) + dot(a[1], b[0]))


def gram_kernel(
    table_ref,
    orders_ref,
    pattern_ref,
    blocks_ref,
    core_recv,
    y_recv,
    yc_recv,
    factor_ref,
    factor_other,
    send_out,
    keep_out,
    xs,
    fs,
    w_high,
    w_low,
    wt_high,
    wt_low,
    gram,
    sems,
    out_sem,
):
    s = lax.axis_index("blk")
    t = lax.axis_index("tile")
    c = t % 2
    slots, max_order, width = blocks_ref.shape
    half = slots // 4
    base = c * half

    def loads(p):
        at = base + p
        owner = table_ref[2, at]
        for m, src in enumerate(
            (blocks_ref.at[table_ref[0, at]], core_recv.at[p], y_recv.at[at], yc_recv.at[p])
        ):
            q = t ^ m
            yield pltpu.make_async_copy(
                src, xs.at[p, :, pl.ds(pl.multiple_of(q * width, width), width)], sems.at[p]
            )
        for which, src in ((c, factor_ref), (1 - c, factor_other)):
            yield pltpu.make_async_copy(src.at[owner], fs.at[p, which], sems.at[p])

    for p in range(half):
        for copy in loads(p):
            copy.start()

    row_ids = lax.broadcasted_iota(jnp.int32, (max_order, CTW), 0)
    for p in range(half):
        for copy in loads(p):
            copy.wait()
        number = s * slots + table_ref[0, base + p]
        order = orders_ref[number]
        row_on = row_ids < order
        top, low = fs[p, 0], fs[p, 1]
        f00, f10, f11 = top[:128], top[128:256], top[256:]
        f2 = jnp.concatenate([low[:128], low[128:256], low[256:]], axis=1)
        f1 = jnp.concatenate([jnp.concatenate([f00, jnp.zeros_like(f00)], axis=1), jnp.concatenate([f10, f11], axis=1)], axis=0)
        f1s, f2s = split(f1), split(f2)
        for q in range(4):
            parts = []
            for e in range(width // CTW):
                ct = q * (width // CTW) + e
                on = row_on & (pattern_ref[number * 8 + ct] != 0)
                parts.append(jnp.where(on, xs[p, :, ct * CTW : (ct + 1) * CTW], 0.0))
            x = split(jnp.concatenate(parts, axis=1))
            w = jnp.concatenate(
                [
                    dot3(f1s, (x[0][:256], x[1][:256]), ((1,), (0,))),
                    dot3(f2s, x, ((1,), (0,))),
                ],
                axis=0,
            )
            w = jnp.where(jnp.concatenate([row_on, row_on], axis=1), w, 0.0)
            rows, cols = pl.ds(p * max_order, max_order), pl.ds(q * width, width)
            w_high[rows, cols], w_low[rows, cols] = split(w)
            wt_high[cols, rows], wt_low[cols, rows] = split(w.T)

    for q1 in range(4):
        rows = pl.ds(q1 * width, width)
        lhs = wt_high[rows, :], wt_low[rows, :]
        for q2 in range(q1 + 1):
            cols = pl.ds(q2 * width, width)
            g = dot3(lhs, (w_high[:, cols], w_low[:, cols]), ((1,), (0,)))
            gram[q1, q2] = g
            if q1 != q2:
                gram[q2, q1] = g.T

    z, x = s // 2, s % 2

    def stores():
        for m in range(4):
            out = send_out if m % 2 else keep_out
            for n in range(4):
                for a in range(2):
                    yield pltpu.make_async_copy(
                        gram.at[z ^ n, t ^ m, pl.ds(pl.multiple_of((x ^ a) * 128, 128), 128), :],
                        out.at[n, a, m // 2],
                        out_sem,
                    )

    for copy in stores():
        copy.start()
    for copy in stores():
        copy.wait()


def paired_body(blocks, orders, pattern, dest, inv_factor):
    slots, max_order, width = blocks.shape
    n_blk = lax.axis_size("blk")
    n_tile = lax.axis_size("tile")
    half = slots // 4
    block_count = dest.shape[0]
    axes = ("blk", "tile")

    def exchange(value, blk_bits, tile_bits):
        perm = [
            (b * n_tile + t, (b ^ blk_bits) * n_tile + (t ^ tile_bits)) for b in range(n_blk) for t in range(n_tile)
        ]
        return lax.ppermute(value, axes, perm)

    hbm = pl.BlockSpec(memory_space=pl.ANY)
    smem = pl.BlockSpec(memory_space=pltpu.SMEM)
    shape = jax.ShapeDtypeStruct
    y_send, core_send, factor_send, table = pl.pallas_call(
        pack_kernel,
        out_shape=(
            shape((2 * half, max_order, width), F32),
            shape((half, max_order, width), F32),
            shape((n_blk, max_order, CTW), F32),
            shape((3, 8), jnp.int32),
        ),
        in_specs=[smem, hbm, hbm],
        out_specs=(hbm, hbm, hbm, smem),
        scratch_shapes=[
            pltpu.SMEM((n_blk,), jnp.int32),
            pltpu.SMEM((2, n_blk), jnp.int32),
            pltpu.SMEM((n_blk,), jnp.int32),
            pltpu.SemaphoreType.DMA,
            pltpu.SemaphoreType.DMA,
        ],
        name="pack",
    )(dest, blocks, inv_factor)

    factors = lax.all_to_all(factor_send, "blk", split_axis=0, concat_axis=0, tiled=True)
    y_recv = exchange(y_send, 0, 2)
    core_recv = exchange(core_send, 0, 1)
    factors_other = exchange(factors, 0, 1)
    core = lax.axis_index("tile") % 2
    yc_recv = exchange(lax.dynamic_slice_in_dim(y_recv, (1 - core) * half, half), 0, 1)

    pieces = (4, 2, 2, 128, width)
    send, keep = pl.pallas_call(
        gram_kernel,
        out_shape=(shape(pieces, F32), shape(pieces, F32)),
        in_specs=[smem, smem, smem] + [hbm] * 6,
        out_specs=(hbm, hbm),
        scratch_shapes=[
            pltpu.VMEM((half, max_order, 4 * width), F32),
            pltpu.VMEM((half, 2, max_order, CTW), F32),
            pltpu.VMEM((half * max_order, 4 * width), BF16),
            pltpu.VMEM((half * max_order, 4 * width), BF16),
            pltpu.VMEM((4 * width, half * max_order), BF16),
            pltpu.VMEM((4 * width, half * max_order), BF16),
            pltpu.VMEM((4, 4, width, width), F32),
            pltpu.SemaphoreType.DMA((half,)),
            pltpu.SemaphoreType.DMA,
        ],
        compiler_params=pltpu.CompilerParams(vmem_limit_bytes=48 << 20),
        name="gram",
    )(table, orders, pattern.reshape(-1), blocks, core_recv, y_recv, yc_recv, factors, factors_other)

    total = keep + exchange(send, 0, 1)
    first, second = total[..., :XY_FIRST, :], total[..., XY_FIRST:, :]
    plane = [(a, b) for a in range(2) for b in range(2) if a or b]
    plane_in = [exchange(first[:, a, b], a, 2 * b) for a, b in plane]
    line_in = [exchange(second[n], 2 * n, 0) for n in range(1, 4)]
    first = first[:, 0, 0] + sum(plane_in)
    second = second[0] + sum(line_in)
    line_in = [exchange(first[n], 2 * n, 0) for n in range(1, 4)]
    plane_in = [exchange(second[a, b], a, 2 * b) for a, b in plane]
    gram_tile = jnp.concatenate([first[0] + sum(line_in), second[0, 0] + sum(plane_in)], axis=0)
    return gram_tile * (1.0 / (block_count * max_order**0.5))


def solution(mesh):
    in_specs = (P("blk", None, "tile"), P(), P(), P(), P("blk", None, None))
    out_specs = P("blk", "tile")
    paired = mesh.shape["blk"] == 8 and mesh.shape["tile"] == 4
    body = paired_body if paired else general_body
    return jax.shard_map(body, mesh=mesh, in_specs=in_specs, out_specs=out_specs, check_vma=False)
```

time: 432 us -> 277 us (0.64)
  waiting for transfers between devices: 320 us -> 72.9 us
  Pallas kernels: 0 us -> 170 us
  matrix products: 59.5 us -> 0 us
  starting transfers between devices: 7.86 us -> 28 us
  local copies, waits for them, and re-layouts: 21.5 us -> 2.73 us
  between operations: 13.5 us -> 0.12 us
  other arithmetic: 9.65 us -> 2.89 us
    pallas_call x0 -> x2, Pallas kernels: none -> 170 us  [the longest x1 158 us: paired_body(): pl.pallas_call(pack_kernel, out_shape=(shape((2 * half, max_order, width)...]
    all_gather x1 -> x0, waiting for transfers between devices: 119 us -> none  [body(): lax.all_gather(whitened_rows, 'tile', axis=1, tiled=True)]
    all_to_all x1, waiting for transfers between devices: 136 us -> 35.5 us  [paired_body(): lax.all_to_all(factor_send, 'blk', split_axis=0, concat_axis=0, tiled=True)]
    reduce_scatter x1 -> x0, waiting for transfers between devices: 64.3 us -> none  [body(): lax.psum_scatter(partial_sums, 'blk', scatter_dimension=0, tiled=True)]
    dot_general x3 -> x0, matrix products: 59.5 us -> none  [the longest x1 34 us: body(): lax.dot_general(lax.all_gather(whitened_rows, 'tile', axis=1, tiled=True)...]
    ppermute x0 -> x17, waiting for transfers between devices: none -> 37.4 us  [exchange(): return lax.ppermute(value, axes, perm)]
    ppermute x0 -> x17, starting transfers between devices: none -> 20.6 us  [exchange(): return lax.ppermute(value, axes, perm)]
    gather x3 -> x0, local copies, waits for them, and re-layouts: 7.17 us -> none  [the longest x1 5.85 us: body(): own_blocks = jnp.take(arrived, positions, axis=0)]
  transfers between devices with their start and end apart: 3 -> 18, of which waited for: 3 -> 9; matrix products, arithmetic and copies ran while one was open for 0% -> 1% of each run, Pallas kernels for 0% -> 0%
where the time goes in v1:
time: 277 us
  Pallas kernels  170 us (61%)
  waiting for transfers between devices  72.9 us (26%)
  starting transfers between devices  28 us (10%)
  other arithmetic  2.89 us (1%)
    pallas_call x1, Pallas kernels, paired_body(): pl.pallas_call(pack_kernel, out_shape=(shape((2 * half, max_order, width)...  158 us
    ppermute x17, waiting for transfers between devices, exchange(): return lax.ppermute(value, axes, perm)  37.4 us
    all_to_all x1, waiting for transfers between devices, paired_body(): lax.all_to_all(factor_send, 'blk', split_axis=0, concat_axis=0, tiled=True)  35.5 us
    ppermute x17, starting transfers between devices, exchange(): return lax.ppermute(value, axes, perm)  20.6 us
    pallas_call x1, Pallas kernels, paired_body(): pl.pallas_call(gram_kernel, out_shape=(shape(pieces, F32), shape(pieces,...  12.8 us
    all_to_all x1, starting transfers between devices, paired_body(): lax.all_to_all(factor_send, 'blk', split_axis=0, concat_axis=0, tiled=True)  7.4 us
  transfers between devices with their start and end apart: 18, of which 9 were waited for; matrix products, arithmetic and copies ran while one was open for 1% of the time, Pallas kernels for 0%

profile of v1, /device:TPU:0, one launch (start us, length us, event | category | flops | bytes accessed | tf_op | source)
XLA Modules:
  0.0 276.9 jit_solution(533852981444077188)
XLA Ops:
  0.0 157.5 %pack.1 = (f32[6,384,256]{2,1,0:T(8,128)}, f32[3,384,256]{2,1,0:T(8,128)}, f32[8,384,128]{2,1,0:T(8,128)}, s32[3,8]{1,0:T(4,128)}) custom-call(s32[96]{0:T(128)} %dest_ref.1, f32[12,384,256]{2,1,0:T(8,128)} %blocks_ref.3, f32[12,384,384]{2,1,0:T(8,128)} %inv_ref.1), custom_call_target="tpu_custom_call" | custom-call | tf_op jit(solution)/shard_map/pack/pallas_call | solution.py:290
  157.6 7.4 %all-to-all-start = ((f32[8,384,128]{2,1,0:T(8,128)}), f32[8,384,128]{2,1,0:T(8,128)S(1)}, u32[]{:S(2)}, u32[]{:S(2)}) async-start(f32[8,384,128]{2,1,0:T(8,128)} %get-tuple-element.14), calls=%async_computation | async-start | bytes 3145728 | tf_op jit(solution)/shard_map/all_to_all | solution.py:310
  165.0 1.5 collective-permute-start.1
  166.5 35.5 %all-to-all-done.factor_ref = f32[8,384,128]{2,1,0:T(8,128)S(1)} async-done(((f32[8,384,128]{2,1,0:T(8,128)}), f32[8,384,128]{2,1,0:T(8,128)S(1)}, u32[]{:S(2)}, u32[]{:S(2)}) %all-to-all-start) | async-done | bytes 1572896 | tf_op jit(solution)/shard_map/all_to_all | solution.py:310
  202.5 15.5 %collective-permute-done.1.y_recv = f32[6,384,256]{2,1,0:T(8,128)} collective-permute-done((f32[6,384,256]{2,1,0:T(8,128)}, f32[6,384,256]{2,1,0:T(8,128)}, u32[]{:S(2)}, u32[]{:S(2)}) %collective-permute-start.1) | collective-permute-done | bytes 2359328 | tf_op jit(solution)/shard_map/ppermute | solution.py:285
  218.0 2.4 constant_dynamic-slice_fusion
  220.5 3.0 %collective-permute-done.2.yc_recv = f32[3,384,256]{2,1,0:T(8,128)} collective-permute-done((f32[3,384,256]{2,1,0:T(8,128)}, f32[3,384,256]{2,1,0:T(8,128)}, u32[]{:S(2)}, u32[]{:S(2)}) %collective-permute-start.2) | collective-permute-done | bytes 1179680 | tf_op jit(solution)/shard_map/ppermute | solution.py:285
  223.5 12.8 %gram.1 = (f32[4,2,2,128,256]{4,3,2,1,0:T(8,128)}, f32[4,2,2,128,256]{4,3,2,1,0:T(8,128)}) custom-call(s32[3,8]{1,0:T(4,128)S(1)} %copy-done, s32[96]{0:T(128)S(1)} %copy-done.1, s32[768]{0:T(1024)S(1)} %reshape.3.pattern_ref, f32[12,384,256]{2,1,0:T(8,128)} %blocks_ref.3, f32[3,384,256]{2,1,0:T(8,128)} %collective-permute-done.core_recv, ...), custom_call_target="tpu_custom_call" | custom-call | tf_op jit(solution)/shard_map/gram/pallas_call | solution.py:318
  236.6 4.2 %collective-permute-done.4 = f32[4,2,2,128,256]{4,3,2,1,0:T(8,128)S(1)} collective-permute-done((f32[4,2,2,128,256]{4,3,2,1,0:T(8,128)}, f32[4,2,2,128,256]{4,3,2,1,0:T(8,128)S(1)}, u32[]{:S(2)}, u32[]{:S(2)}) %collective-permute-start.4) | collective-permute-done | bytes 2097184 | tf_op jit(solution)/shard_map/ppermute | solution.py:285
  240.8 2.0 add.48
  242.9 2.7 collective-permute-start.12
  245.6 1.5 collective-permute-start.11
  247.4 1.8 collective-permute-start.6
  249.2 1.5 collective-permute-start.5
  250.8 4.0 %collective-permute-done.12 = f32[2,2,40,256]{3,2,1,0:T(8,128)S(1)} collective-permute-done((f32[2,2,40,256]{3,2,1,0:T(8,128)S(1)}, f32[2,2,40,256]{3,2,1,0:T(8,128)S(1)}, u32[]{:S(2)}, u32[]{:S(2)}) %collective-permute-start.12) | collective-permute-done | bytes 163872 | tf_op jit(solution)/shard_map/ppermute | solution.py:285
  254.8 3.1 %collective-permute-start.7 = (f32[4,88,256]{2,1,0:T(8,128)S(1)}, f32[4,88,256]{2,1,0:T(8,128)S(1)}, u32[]{:S(2)}, u32[]{:S(2)}) collective-permute-start(f32[4,88,256]{2,1,0:T(8,128)S(1)} %get-tuple-element.19), channel_id=1, source_target_pairs={{0,6},{1,7},{2,4},{3,5},{4,2},{5,3},{6,0},{7,1},{8,14},{9,15},{10,... | collective-permute-start | bytes 1081352 | tf_op jit(solution)/shard_map/ppermute | solution.py:285
  258.5 1.5 collective-permute-start.15
  260.0 1.5 collective-permute-start.16
  262.1 4.9 %collective-permute-done.5 = f32[4,88,256]{2,1,0:T(8,128)S(1)} collective-permute-done((f32[4,88,256]{2,1,0:T(8,128)S(1)}, f32[4,88,256]{2,1,0:T(8,128)S(1)}, u32[]{:S(2)}, u32[]{:S(2)}) %collective-permute-start.5) | collective-permute-done | bytes 360480 | tf_op jit(solution)/shard_map/ppermute | solution.py:285
  267.1 1.1 collective-permute-start.9
  268.2 2.4 collective-permute-start.10
  271.1 4.3 %collective-permute-done.9 = f32[88,256]{1,0:T(8,128)S(1)} collective-permute-done((f32[88,256]{1,0:T(8,128)S(1)}, f32[88,256]{1,0:T(8,128)S(1)}, u32[]{:S(2)}, u32[]{:S(2)}) %collective-permute-start.9) | collective-permute-done | bytes 90144 | tf_op jit(solution)/shard_map/ppermute | solution.py:285
  275.5 0.7 collective-permute-done.8
  276.2 0.7 maximum_multiply_fusion
  (33 shorter events, 3.2 us)
Async XLA Ops:
  157.5 62.8 %copy-start.2 = (s32[96,8]{0,1:T(8,128)S(1)}, s32[96,8]{0,1:T(8,128)}, u32[]{:S(2)}) copy-start(s32[96,8]{0,1:T(8,128)} %param.7) | copy-start | bytes 9220
  157.5 66.0 %copy-start = (s32[3,8]{1,0:T(4,128)S(1)}, s32[3,8]{1,0:T(4,128)}, u32[]{:S(2)}) copy-start(s32[3,8]{1,0:T(4,128)} %get-tuple-element.11.table_ref) | copy-start | bytes 292
  157.5 66.0 %copy-start.1 = (s32[96]{0:T(128)S(1)}, s32[96]{0:T(128)}, u32[]{:S(2)}) copy-start(s32[96]{0:T(128)} %orders_ref.1) | copy-start | bytes 1156
  157.6 44.4 %all-to-all-start = ((f32[8,384,128]{2,1,0:T(8,128)}), f32[8,384,128]{2,1,0:T(8,128)S(1)}, u32[]{:S(2)}, u32[]{:S(2)}) async-start(f32[8,384,128]{2,1,0:T(8,128)} %get-tuple-element.14), calls=%async_computation | async-start | bytes 3145728 | tf_op jit(solution)/shard_map/all_to_all | solution.py:310
  165.0 53.0 %collective-permute-start.1 = (f32[6,384,256]{2,1,0:T(8,128)}, f32[6,384,256]{2,1,0:T(8,128)}, u32[]{:S(2)}, u32[]{:S(2)}) collective-permute-start(f32[6,384,256]{2,1,0:T(8,128)} %get-tuple-element.13), channel_id=1, source_target_pairs={{0,2},{1,3},{2,0},{3,1},{4,6},{5,7},{6,4},{7,5},{8,10},{9,11},{10,... | collective-permute-start | bytes 7077896 | tf_op jit(solution)/shard_map/ppermute | solution.py:285
  202.0 21.6 %collective-permute-start.3 = (f32[8,384,128]{2,1,0:T(8,128)S(1)}, f32[8,384,128]{2,1,0:T(8,128)S(1)}, u32[]{:S(2)}, u32[]{:S(2)}) collective-permute-start(f32[8,384,128]{2,1,0:T(8,128)S(1)} %all-to-all-done.factor_ref), channel_id=1, source_target_pairs={{0,1},{1,0},{2,3},{3,2},{4,5},{5,4},{6,7},{7,6},{8,9},{9,8},{10,11... | collective-permute-start | bytes 4718600 | tf_op jit(solution)/shard_map/ppermute | solution.py:285
  202.0 18.6 %collective-permute-start = (f32[3,384,256]{2,1,0:T(8,128)}, f32[3,384,256]{2,1,0:T(8,128)}, u32[]{:S(2)}, u32[]{:S(2)}) collective-permute-start(f32[3,384,256]{2,1,0:T(8,128)} %get-tuple-element.12), channel_id=1, source_target_pairs={{0,1},{1,0},{2,3},{3,2},{4,5},{5,4},{6,7},{7,6},{8,9},{9,8},{10,11... | collective-permute-start | bytes 3538952 | tf_op jit(solution)/shard_map/ppermute | solution.py:285
  220.3 3.2 %collective-permute-start.2 = (f32[3,384,256]{2,1,0:T(8,128)}, f32[3,384,256]{2,1,0:T(8,128)}, u32[]{:S(2)}, u32[]{:S(2)}) collective-permute-start(f32[3,384,256]{2,1,0:T(8,128)} %constant_dynamic-slice_fusion), channel_id=1, source_target_pairs={{0,1},{1,0},{2,3},{3,2},{4,5},{5,4},{6,7},{7,6},{8,9},{9,8},{10,11... | collective-permute-start | bytes 3538952 | tf_op jit(solution)/shard_map/ppermute | solution.py:285
  236.4 4.4 %collective-permute-start.4 = (f32[4,2,2,128,256]{4,3,2,1,0:T(8,128)}, f32[4,2,2,128,256]{4,3,2,1,0:T(8,128)S(1)}, u32[]{:S(2)}, u32[]{:S(2)}) collective-permute-start(f32[4,2,2,128,256]{4,3,2,1,0:T(8,128)} %get-tuple-element.16), channel_id=1, source_target_pairs={{0,1},{1,0},{2,3},{3,2},{4,5},{5,4},{6,7},{7,6},{8,9},{9,8},{10,11... | collective-permute-start | bytes 6291464 | tf_op jit(solution)/shard_map/ppermute | solution.py:285
  242.9 11.9 %collective-permute-start.12 = (f32[2,2,40,256]{3,2,1,0:T(8,128)S(1)}, f32[2,2,40,256]{3,2,1,0:T(8,128)S(1)}, u32[]{:S(2)}, u32[]{:S(2)}) collective-permute-start(f32[2,2,40,256]{3,2,1,0:T(8,128)S(1)} %get-tuple-element.20), channel_id=1, source_target_pairs={{0,16},{1,17},{2,18},{3,19},{4,20},{5,21},{6,22},{7,23},{8,24},{9,... | collective-permute-start | bytes 491528 | tf_op jit(solution)/shard_map/ppermute | solution.py:285
  245.6 12.3 %collective-permute-start.11 = (f32[2,2,40,256]{3,2,1,0:T(8,128)S(1)}, f32[2,2,40,256]{3,2,1,0:T(8,128)S(1)}, u32[]{:S(2)}, u32[]{:S(2)}) collective-permute-start(f32[2,2,40,256]{3,2,1,0:T(8,128)S(1)} %get-tuple-element.21), channel_id=1, source_target_pairs={{0,8},{1,9},{2,10},{3,11},{4,12},{5,13},{6,14},{7,15},{8,0},{9,1},... | collective-permute-start | bytes 491528 | tf_op jit(solution)/shard_map/ppermute | solution.py:285
  247.0 11.4 %collective-permute-start.13 = (f32[2,2,40,256]{3,2,1,0:T(8,128)S(1)}, f32[2,2,40,256]{3,2,1,0:T(8,128)S(1)}, u32[]{:S(2)}, u32[]{:S(2)}) collective-permute-start(f32[2,2,40,256]{3,2,1,0:T(8,128)S(1)} %get-tuple-element.22), channel_id=1, source_target_pairs={{0,24},{1,25},{2,26},{3,27},{4,28},{5,29},{6,30},{7,31},{8,16},{9,... | collective-permute-start | bytes 491528 | tf_op jit(solution)/shard_map/ppermute | solution.py:285
  247.4 14.1 %collective-permute-start.6 = (f32[4,88,256]{2,1,0:T(8,128)S(1)}, f32[4,88,256]{2,1,0:T(8,128)S(1)}, u32[]{:S(2)}, u32[]{:S(2)}) collective-permute-start(f32[4,88,256]{2,1,0:T(8,128)S(1)} %get-tuple-element.17), channel_id=1, source_target_pairs={{0,4},{1,5},{2,6},{3,7},{4,0},{5,1},{6,2},{7,3},{8,12},{9,13},{10,... | collective-permute-start | bytes 1081352 | tf_op jit(solution)/shard_map/ppermute | solution.py:285
  249.2 17.8 %collective-permute-start.5 = (f32[4,88,256]{2,1,0:T(8,128)S(1)}, f32[4,88,256]{2,1,0:T(8,128)S(1)}, u32[]{:S(2)}, u32[]{:S(2)}) collective-permute-start(f32[4,88,256]{2,1,0:T(8,128)S(1)} %get-tuple-element.18), channel_id=1, source_target_pairs={{0,2},{1,3},{2,0},{3,1},{4,6},{5,7},{6,4},{7,5},{8,10},{9,11},{10,... | collective-permute-start | bytes 1081352 | tf_op jit(solution)/shard_map/ppermute | solution.py:285
  254.8 12.2 %collective-permute-start.7 = (f32[4,88,256]{2,1,0:T(8,128)S(1)}, f32[4,88,256]{2,1,0:T(8,128)S(1)}, u32[]{:S(2)}, u32[]{:S(2)}) collective-permute-start(f32[4,88,256]{2,1,0:T(8,128)S(1)} %get-tuple-element.19), channel_id=1, source_target_pairs={{0,6},{1,7},{2,4},{3,5},{4,2},{5,3},{6,0},{7,1},{8,14},{9,15},{10,... | collective-permute-start | bytes 1081352 | tf_op jit(solution)/shard_map/ppermute | solution.py:285
  258.5 12.1 %collective-permute-start.15 = (f32[40,256]{1,0:T(8,128)S(1)}, f32[40,256]{1,0:T(8,128)S(1)}, u32[]{:S(2)}, u32[]{:S(2)}) collective-permute-start(f32[40,256]{1,0:T(8,128)S(1)} %get-tuple-element.26), channel_id=1, source_target_pairs={{0,4},{1,5},{2,6},{3,7},{4,0},{5,1},{6,2},{7,3},{8,12},{9,13},{10,... | collective-permute-start | bytes 122888 | tf_op jit(solution)/shard_map/ppermute | solution.py:285
  260.0 11.1 %collective-permute-start.16 = (f32[40,256]{1,0:T(8,128)S(1)}, f32[40,256]{1,0:T(8,128)S(1)}, u32[]{:S(2)}, u32[]{:S(2)}) collective-permute-start(f32[40,256]{1,0:T(8,128)S(1)} %get-tuple-element.27), channel_id=1, source_target_pairs={{0,6},{1,7},{2,4},{3,5},{4,2},{5,3},{6,0},{7,1},{8,14},{9,15},{10,... | collective-permute-start | bytes 122888 | tf_op jit(solution)/shard_map/ppermute | solution.py:285
  261.5 9.6 %collective-permute-start.14 = (f32[40,256]{1,0:T(8,128)S(1)}, f32[40,256]{1,0:T(8,128)S(1)}, u32[]{:S(2)}, u32[]{:S(2)}) collective-permute-start(f32[40,256]{1,0:T(8,128)S(1)} %get-tuple-element.28), channel_id=1, source_target_pairs={{0,2},{1,3},{2,0},{3,1},{4,6},{5,7},{6,4},{7,5},{8,10},{9,11},{10,... | collective-permute-start | bytes 122888 | tf_op jit(solution)/shard_map/ppermute | solution.py:285
  267.1 8.3 %collective-permute-start.9 = (f32[88,256]{1,0:T(8,128)S(1)}, f32[88,256]{1,0:T(8,128)S(1)}, u32[]{:S(2)}, u32[]{:S(2)}) collective-permute-start(f32[88,256]{1,0:T(8,128)S(1)} %get-tuple-element.23), channel_id=1, source_target_pairs={{0,16},{1,17},{2,18},{3,19},{4,20},{5,21},{6,22},{7,23},{8,24},{9,... | collective-permute-start | bytes 270344 | tf_op jit(solution)/shard_map/ppermute | solution.py:285
  268.2 7.2 %collective-permute-start.10 = (f32[88,256]{1,0:T(8,128)S(1)}, f32[88,256]{1,0:T(8,128)S(1)}, u32[]{:S(2)}, u32[]{:S(2)}) collective-permute-start(f32[88,256]{1,0:T(8,128)S(1)} %get-tuple-element.24), channel_id=1, source_target_pairs={{0,24},{1,25},{2,26},{3,27},{4,28},{5,29},{6,30},{7,31},{8,16},{9,... | collective-permute-start | bytes 270344 | tf_op jit(solution)/shard_map/ppermute | solution.py:285
  270.6 5.6 %collective-permute-start.8 = (f32[88,256]{1,0:T(8,128)S(1)}, f32[88,256]{1,0:T(8,128)S(1)}, u32[]{:S(2)}, u32[]{:S(2)}) collective-permute-start(f32[88,256]{1,0:T(8,128)S(1)} %get-tuple-element.25), channel_id=1, source_target_pairs={{0,8},{1,9},{2,10},{3,11},{4,12},{5,13},{6,14},{7,15},{8,0},{9,1},... | collective-permute-start | bytes 270344 | tf_op jit(solution)/shard_map/ppermute | solution.py:285

commit v2 on v0

v2 whole, which is shorter than its diff:
```python
import jax
import jax.numpy as jnp
from jax import lax
from jax.experimental import pallas as pl
from jax.experimental.pallas import tpu as pltpu
from jax.sharding import PartitionSpec as P

CTW = 128
F32 = jnp.float32
BF16 = jnp.bfloat16
XY_FIRST = 88


def general_body(blocks, orders, pattern, dest, inv_factor):
    source_index = lax.axis_index("blk")
    owner_count = lax.axis_size("blk")
    tile_index = lax.axis_index("tile")
    slot_count, max_order, column_width = blocks.shape
    block_count = dest.shape[0]
    tiles_here = column_width // CTW
    highest = lax.Precision.HIGHEST
    capacity = (slot_count + owner_count - 1) // owner_count
    dest_grid = dest.reshape(owner_count, slot_count)
    earlier = lax.broadcasted_iota(jnp.int32, (slot_count, slot_count), 1) < lax.broadcasted_iota(
        jnp.int32, (slot_count, slot_count), 0
    )
    matching = dest_grid[:, :, None] == dest_grid[:, None, :]
    ranks = jnp.sum((matching & earlier[None]).astype(jnp.int32), axis=2).reshape(block_count)
    my_dest = lax.dynamic_slice_in_dim(dest, source_index * slot_count, slot_count)
    my_rank = lax.dynamic_slice_in_dim(ranks, source_index * slot_count, slot_count)
    my_orders = lax.dynamic_slice_in_dim(orders, source_index * slot_count, slot_count)
    my_tiles = lax.dynamic_slice(
        pattern, (source_index * slot_count, tile_index * tiles_here), (slot_count, tiles_here)
    )
    row_ids = lax.broadcasted_iota(jnp.int32, (slot_count, max_order), 1)
    row_mask = (row_ids < my_orders[:, None]).astype(F32)
    col_mask = jnp.repeat(my_tiles.astype(F32), CTW, axis=1)
    masked = blocks * row_mask[:, :, None] * col_mask[:, None, :]
    owned = lax.dynamic_slice_in_dim(
        jnp.argsort(dest, stable=True), source_index * slot_count, slot_count
    )
    slot_ids = my_dest * capacity + my_rank
    placing = (
        lax.broadcasted_iota(jnp.int32, (owner_count * capacity, slot_count), 0)
        == slot_ids[None, :]
    ).astype(F32)
    outgoing = jnp.einsum("ak,krc->arc", placing, masked, precision=highest, preferred_element_type=F32)
    arrived = lax.all_to_all(outgoing, "blk", split_axis=0, concat_axis=0, tiled=True)
    positions = owned // slot_count * capacity + ranks[owned]
    own_blocks = jnp.take(arrived, positions, axis=0)
    own_mask = (row_ids < orders[owned][:, None]).astype(F32)
    whitened = jnp.einsum(
        "jrq,jqc->jrc", inv_factor, own_blocks, precision=highest, preferred_element_type=F32
    )
    whitened_rows = (whitened * own_mask[:, :, None]).reshape(slot_count * max_order, column_width)
    factor = 1.0 / (block_count * max_order**0.5)
    partial_sums = lax.dot_general(
        lax.all_gather(whitened_rows, "tile", axis=1, tiled=True),
        whitened_rows,
        (((0,), (0,)), ((), ())),
        precision=highest,
        preferred_element_type=F32,
    )
    gram_tile = lax.psum_scatter(partial_sums, "blk", scatter_dimension=0, tiled=True)
    return gram_tile * factor


MINE, OTHERS, OWNER, ROW_AT = 0, 1, 2, 3


def round8(order):
    return (order + 7) // 8 * 8


def pack_rows(dest_ref, orders_ref, pattern_ref, blocks_ref, rows_out, table_ref, block_at, count, staged, packed, sems, out_sem):
    s = lax.axis_index("blk")
    t = lax.axis_index("tile")
    y = t // 2
    slots, max_order, width = blocks_ref.shape
    n_blk = count.shape[0]
    tiles = width // CTW

    def clear(o, carry):
        count[o] = 0
        return carry

    lax.fori_loop(0, n_blk, clear, 0, unroll=True)

    def place(i, carry):
        o = dest_ref[s * slots + i]
        r = count[o]
        block_at[r, o] = i
        count[o] = r + 1
        return carry

    lax.fori_loop(0, slots, place, 0, unroll=True)

    def compact(o, p):
        @pl.when(count[o] > 0)
        def _():
            table_ref[MINE, p] = block_at[y, o]
            table_ref[OTHERS, p] = block_at[1 - y, o]
            table_ref[OWNER, p] = o

        return p + jnp.where(count[o] > 0, 1, 0)

    lax.fori_loop(0, n_blk, compact, 0, unroll=True)

    def loads():
        for p in range(slots // 2):
            yield pltpu.make_async_copy(blocks_ref.at[table_ref[OTHERS, p]], staged.at[p], sems.at[p])

    for copy in loads():
        copy.start()

    for k in range(2):
        at = jnp.int32(0)
        for p in range(slots // 2):
            number = s * slots + table_ref[MINE, p]
            for e in range(tiles):
                table_ref[ROW_AT + k, p * tiles + e] = jnp.minimum(at, rows_out.shape[0] - max_order)
                on = pattern_ref[number * 8 + (t ^ (2 + k)) * tiles + e] != 0
                at = at + jnp.where(on, round8(orders_ref[number]), 0)

    at = jnp.int32(0)
    for p, copy in enumerate(loads()):
        copy.wait()
        number = s * slots + table_ref[OTHERS, p]
        for e in range(tiles):
            on = pattern_ref[number * 8 + t * tiles + e] != 0

            @pl.when(on)
            def _(at=at, p=p, e=e):
                packed[pl.ds(pl.multiple_of(at, 8), max_order), :] = staged[p, :, e * CTW : (e + 1) * CTW]

            at = at + jnp.where(on, round8(orders_ref[number]), 0)
    out = pltpu.make_async_copy(packed.at[pl.ds(0, rows_out.shape[0])], rows_out, out_sem)
    out.start()
    out.wait()


def pack_own(table_ref, dest_ref, blocks_ref, inv_ref, own_out, factor_out, factor_at, own, factor, own_sems, factor_sems, out_sem):
    s = lax.axis_index("blk")
    t = lax.axis_index("tile")
    y, c = t // 2, t % 2
    slots = blocks_ref.shape[0]
    n_blk = factor_at.shape[0]

    def scan_source(source, found):
        def scan_block(i, carry):
            found, seen = carry
            mine = dest_ref[source * slots + i] == s

            @pl.when(mine & (seen == y))
            def _():
                factor_at[source] = found

            step = jnp.where(mine, 1, 0)
            return found + step, seen + step

        factor_at[source] = 0
        return lax.fori_loop(0, slots, scan_block, (found, 0), unroll=True)[0]

    lax.fori_loop(0, n_blk, scan_source, 0)

    def factor_loads(source):
        row = factor_at[source]
        for k, (ti, tj) in enumerate(((0, 0), (1, 0), (1, 1))):
            ri, rj = jnp.where(c == 0, ti, 2), jnp.where(c == 0, tj, k)
            yield pltpu.make_async_copy(
                inv_ref.at[row, pl.ds(pl.multiple_of(ri * 128, 128), 128), pl.ds(pl.multiple_of(rj * 128, 128), 128)],
                factor.at[source, pl.ds(k * 128, 128), :],
                factor_sems.at[source],
            )

    def own_load(p):
        return pltpu.make_async_copy(blocks_ref.at[table_ref[MINE, p]], own.at[p], own_sems.at[p])

    def outs():
        for source in range(n_blk):
            yield pltpu.make_async_copy(factor.at[source], factor_out.at[source], out_sem)
        for p in range(slots // 2):
            yield pltpu.make_async_copy(own.at[p], own_out.at[p], out_sem)

    for source in range(n_blk):
        for copy in factor_loads(source):
            copy.start()
    for p in range(slots // 2):
        own_load(p).start()
    for i, out in enumerate(outs()):
        if i < n_blk:
            for copy in factor_loads(i):
                copy.wait()
        else:
            own_load(i - n_blk).wait()
        out.start()
    for out in outs():
        out.wait()


def split(x):
    high = x.astype(BF16)
    return high, (x - high.astype(F32)).astype(BF16)


def dot3(a, b):
    def dot(p, q):
        return jnp.dot(p, q, preferred_element_type=F32)

    return dot(a[0], b[0]) + (dot(a[0], b[1]) + dot(a[1], b[0]))


def whiten(tiles, number, upper, lower, orders_ref, pattern_ref, tile_ids):
    row_on = lax.broadcasted_iota(jnp.int32, tiles[0].shape, 0) < orders_ref[number]
    parts = [
        jnp.where(row_on & (pattern_ref[number * 8 + ct] != 0), tile, 0.0) for tile, ct in zip(tiles, tile_ids)
    ]
    x = split(jnp.concatenate(parts, axis=1))
    w = jnp.concatenate([dot3(upper, (x[0][:256], x[1][:256])), dot3(lower, x)], axis=0)
    return [jnp.where(row_on, w[:, i * CTW : (i + 1) * CTW], 0.0) for i in range(len(tiles))]


def gram_own(
    table_ref, orders_ref, pattern_ref, own_ref, core_ref, factor_ref, factor_other,
    upper_high, upper_low, lower_high, lower_low, w0_high, w0_low, w1t_high, w1t_low, g_out,
    xs, fs, w0t_high, w0t_low, sems,
):
    s = lax.axis_index("blk")
    t = lax.axis_index("tile")
    c = t % 2
    half, max_order, width = own_ref.shape

    def loads(p):
        yield pltpu.make_async_copy(own_ref.at[p], xs.at[p, 0], sems.at[p])
        yield pltpu.make_async_copy(core_ref.at[p], xs.at[p, 1], sems.at[p])
        for which, src in ((c, factor_ref), (1 - c, factor_other)):
            yield pltpu.make_async_copy(src.at[table_ref[OWNER, p]], fs.at[p, which], sems.at[p])

    for p in range(half):
        for copy in loads(p):
            copy.start()
    for p in range(half):
        for copy in loads(p):
            copy.wait()
        top, low = fs[p, 0], fs[p, 1]
        f00, f10, f11 = top[:128], top[128:256], top[256:]
        upper = split(
            jnp.concatenate(
                [jnp.concatenate([f00, jnp.zeros_like(f00)], axis=1), jnp.concatenate([f10, f11], axis=1)], axis=0
            )
        )
        lower = split(jnp.concatenate([low[:128], low[128:256], low[256:]], axis=1))
        upper_high[p], upper_low[p] = upper
        lower_high[p], lower_low[p] = lower
        tiles = [xs[p, m, :, e * CTW : (e + 1) * CTW] for m in range(2) for e in range(2)]
        tile_ids = [(t ^ m) * 2 + e for m in range(2) for e in range(2)]
        number = s * 2 * half + table_ref[MINE, p]
        w = whiten(tiles, number, upper, lower, orders_ref, pattern_ref, tile_ids)
        rows = pl.ds(p * max_order, max_order)
        w0, w1 = jnp.concatenate(w[:2], axis=1), jnp.concatenate(w[2:], axis=1)
        w0_high[rows, :], w0_low[rows, :] = split(w0)
        w0t_high[:, rows], w0t_low[:, rows] = split(w0.T)
        w1t_high[:, rows], w1t_low[:, rows] = split(w1.T)
    w0 = w0_high[...], w0_low[...]
    g_out[0] = dot3((w0t_high[...], w0t_low[...]), w0)
    g_out[1] = dot3((w1t_high[...], w1t_low[...]), w0)


def gram_rest(
    table_ref, orders_ref, pattern_ref, y_ref, yc_ref,
    upper_high, upper_low, lower_high, lower_low, w0_high, w0_low, w1t_high, w1t_low, g_own,
    *refs,
):
    firsts, seconds = refs[:4], refs[4:8]
    xs, w2_high, w2_low, w2t_high, w2t_low, w3t_high, w3t_low, gram, sems, out_sem = refs[8:]
    s = lax.axis_index("blk")
    t = lax.axis_index("tile")
    half, tiles, max_order, _ = xs.shape
    width = w0_high.shape[1]

    def loads(p):
        for k, src in enumerate((y_ref, yc_ref)):
            for e in range(2):
                at = pl.multiple_of(table_ref[ROW_AT + k, p * 2 + e], 8)
                yield pltpu.make_async_copy(src.at[pl.ds(at, max_order), :], xs.at[p, k * 2 + e], sems.at[p])

    for p in range(half):
        for copy in loads(p):
            copy.start()
    for p in range(half):
        for copy in loads(p):
            copy.wait()
        tile_ids = [(t ^ (2 + k)) * 2 + e for k in range(2) for e in range(2)]
        number = s * 2 * half + table_ref[MINE, p]
        upper, lower = (upper_high[p], upper_low[p]), (lower_high[p], lower_low[p])
        w = whiten([xs[p, i] for i in range(tiles)], number, upper, lower, orders_ref, pattern_ref, tile_ids)
        rows = pl.ds(p * max_order, max_order)
        w2, w3 = jnp.concatenate(w[:2], axis=1), jnp.concatenate(w[2:], axis=1)
        w2_high[rows, :], w2_low[rows, :] = split(w2)
        w2t_high[:, rows], w2t_low[:, rows] = split(w2.T)
        w3t_high[:, rows], w3t_low[:, rows] = split(w3.T)

    w0, w2 = (w0_high[...], w0_low[...]), (w2_high[...], w2_low[...])
    w1t, w2t, w3t = (w1t_high[...], w1t_low[...]), (w2t_high[...], w2t_low[...]), (w3t_high[...], w3t_low[...])
    gram[0, 0] = g_own[0]
    gram[0, 1] = g_own[1]
    g20 = dot3(w2t, w0)
    gram[0, 2] = g20
    gram[1, 0] = g20.T
    gram[0, 3] = dot3(w3t, w0)
    gram[1, 1] = dot3(w1t, w2)
    gram[1, 2] = dot3(w2t, w2)
    gram[1, 3] = dot3(w3t, w2)

    z, x = s // 2, s % 2

    def stores():
        for n in range(4):
            for a in range(2):
                for b in range(2):
                    m, at = (z ^ n) ^ t, (x ^ a) * 128
                    first, second = firsts[2 * a + b], seconds[n]
                    yield pltpu.make_async_copy(
                        gram.at[b, m, pl.ds(pl.multiple_of(at, 8), XY_FIRST), :], first.at[n], out_sem
                    )
                    yield pltpu.make_async_copy(
                        gram.at[b, m, pl.ds(pl.multiple_of(at + XY_FIRST, 8), 128 - XY_FIRST), :],
                        second.at[a, b],
                        out_sem,
                    )

    for copy in stores():
        copy.start()
    for copy in stores():
        copy.wait()


def paired_body(blocks, orders, pattern, dest, inv_factor):
    slots, max_order, width = blocks.shape
    n_blk = lax.axis_size("blk")
    n_tile = lax.axis_size("tile")
    half = slots // 2
    tiles = width // CTW
    block_count = dest.shape[0]
    axes = ("blk", "tile")
    pattern = pattern.reshape(-1)

    def exchange(value, blk_bits, tile_bits):
        perm = [
            (b * n_tile + t, (b ^ blk_bits) * n_tile + (t ^ tile_bits)) for b in range(n_blk) for t in range(n_tile)
        ]
        return lax.ppermute(value, axes, perm)

    hbm = pl.BlockSpec(memory_space=pltpu.HBM)
    smem = pl.BlockSpec(memory_space=pltpu.SMEM)
    vmem = pl.BlockSpec(memory_space=pltpu.VMEM)
    shape = jax.ShapeDtypeStruct
    params = pltpu.CompilerParams(vmem_limit_bytes=48 << 20)
    dma = pltpu.SemaphoreType.DMA
    row_count = half * tiles * max_order

    y_rows, table = pl.pallas_call(
        pack_rows,
        out_shape=(pltpu.HBM((row_count, CTW), F32), shape((5, half * tiles), jnp.int32)),
        in_specs=[smem, smem, smem, hbm],
        out_specs=(hbm, smem),
        scratch_shapes=[
            pltpu.SMEM((2, n_blk), jnp.int32),
            pltpu.SMEM((n_blk,), jnp.int32),
            pltpu.VMEM((half, max_order, width), F32),
            pltpu.VMEM((row_count, CTW), F32),
            dma((half,)),
            dma,
        ],
        compiler_params=params,
        name="pack_rows",
    )(dest, orders, pattern, blocks)
    y_recv = exchange(y_rows, 0, 2)

    own, factor_send = pl.pallas_call(
        pack_own,
        out_shape=(pltpu.HBM((half, max_order, width), F32), pltpu.HBM((n_blk, max_order, CTW), F32)),
        in_specs=[smem, smem, hbm, hbm],
        out_specs=(hbm, hbm),
        scratch_shapes=[
            pltpu.SMEM((n_blk,), jnp.int32),
            pltpu.VMEM((half, max_order, width), F32),
            pltpu.VMEM((n_blk, max_order, CTW), F32),
            dma((half,)),
            dma((n_blk,)),
            dma,
        ],
        compiler_params=params,
        name="pack_own",
    )(table, dest, blocks, inv_factor)
    factors = lax.all_to_all(factor_send, "blk", split_axis=0, concat_axis=0, tiled=True)
    core_recv = exchange(own, 0, 1)
    factors_other = exchange(factors, 0, 1)

    depth = half * max_order
    own_results = pl.pallas_call(
        gram_own,
        out_shape=(
            shape((half, 256, 256), BF16),
            shape((half, 256, 256), BF16),
            shape((half, 128, 384), BF16),
            shape((half, 128, 384), BF16),
            shape((depth, width), BF16),
            shape((depth, width), BF16),
            shape((width, depth), BF16),
            shape((width, depth), BF16),
            shape((2, width, width), F32),
        ),
        in_specs=[smem] * 3 + [hbm] * 4,
        out_specs=(vmem,) * 9,
        scratch_shapes=[
            pltpu.VMEM((half, 2, max_order, width), F32),
            pltpu.VMEM((half, 2, max_order, CTW), F32),
            pltpu.VMEM((width, depth), BF16),
            pltpu.VMEM((width, depth), BF16),
            dma((half,)),
        ],
        compiler_params=params,
        name="gram_own",
    )(table, orders, pattern, own, core_recv, factors, factors_other)

    y_recv, own_results = lax.optimization_barrier((y_recv, own_results))
    yc_recv = exchange(y_recv, 0, 1)
    first_shape, second_shape = (4, XY_FIRST, width), (2, 2, 128 - XY_FIRST, width)
    pieces = pl.pallas_call(
        gram_rest,
        out_shape=(shape(first_shape, F32),) * 4 + (shape(second_shape, F32),) * 4,
        in_specs=[smem] * 3 + [hbm] * 2 + [vmem] * 9,
        out_specs=(hbm,) * 8,
        scratch_shapes=[
            pltpu.VMEM((half, 2 * tiles, max_order, CTW), F32),
            pltpu.VMEM((depth, width), BF16),
            pltpu.VMEM((depth, width), BF16),
            pltpu.VMEM((width, depth), BF16),
            pltpu.VMEM((width, depth), BF16),
            pltpu.VMEM((width, depth), BF16),
            pltpu.VMEM((width, depth), BF16),
            pltpu.VMEM((2, 4, width, width), F32),
            dma((half,)),
            dma,
        ],
        compiler_params=params,
        name="gram_rest",
    )(table, orders, pattern, y_recv, yc_recv, *own_results)
    firsts, seconds = pieces[:4], pieces[4:]

    plane = [(a, b) for a in range(2) for b in range(2) if a or b]
    plane_in = [exchange(firsts[2 * a + b], a, 2 * b) for a, b in plane]
    line_in = [exchange(seconds[n], 2 * n, 0) for n in range(1, 4)]
    first = firsts[0] + sum(plane_in)
    second = seconds[0] + sum(line_in)
    line_in = [exchange(first[n], 2 * n, 0) for n in range(1, 4)]
    plane_in = [exchange(second[a, b], a, 2 * b) for a, b in plane]
    gram_tile = jnp.concatenate([first[0] + sum(line_in), second[0, 0] + sum(plane_in)], axis=0)
    return gram_tile * (1.0 / (block_count * max_order**0.5))


def solution(mesh):
    in_specs = (P("blk", None, "tile"), P(), P(), P(), P("blk", None, None))
    out_specs = P("blk", "tile")
    paired = mesh.shape["blk"] == 8 and mesh.shape["tile"] == 4
    body = paired_body if paired else general_body
    return jax.shard_map(body, mesh=mesh, in_specs=in_specs, out_specs=out_specs, check_vma=False)
```

time: 432 us -> 132 us (0.31)
  waiting for transfers between devices: 320 us -> 59.5 us
  matrix products: 59.5 us -> 0 us
  Pallas kernels: 0 us -> 35 us
  starting transfers between devices: 7.86 us -> 27.4 us
  between operations: 13.5 us -> 0.13 us
  local copies, waits for them, and re-layouts: 21.5 us -> 9.23 us
  other arithmetic: 9.65 us -> 0.87 us
    all_gather x1 -> x0, waiting for transfers between devices: 119 us -> none  [body(): lax.all_gather(whitened_rows, 'tile', axis=1, tiled=True)]
    all_to_all x1, waiting for transfers between devices: 136 us -> 35.4 us  [paired_body(): lax.all_to_all(factor_send, 'blk', split_axis=0, concat_axis=0, tiled=True)]
    reduce_scatter x1 -> x0, waiting for transfers between devices: 64.3 us -> none  [body(): lax.psum_scatter(partial_sums, 'blk', scatter_dimension=0, tiled=True)]
    dot_general x3 -> x0, matrix products: 59.5 us -> none  [the longest x1 34 us: body(): lax.dot_general(lax.all_gather(whitened_rows, 'tile', axis=1, tiled=True)...]
    pallas_call x0 -> x4, Pallas kernels: none -> 35 us  [the longest x1 17.4 us: paired_body(): pl.pallas_call(gram_rest, out_shape=(shape(first_shape, F32),) * 4 + (sha...]
    ppermute x0 -> x16, waiting for transfers between devices: none -> 24.1 us  [exchange(): return lax.ppermute(value, axes, perm)]
    ppermute x0 -> x16, starting transfers between devices: none -> 20.1 us  [exchange(): return lax.ppermute(value, axes, perm)]
    unnamed x4 -> x21, local copies, waits for them, and re-layouts: 0.01 us -> 9.11 us
  transfers between devices with their start and end apart: 3 -> 17, of which waited for: 3 -> 10; matrix products, arithmetic and copies ran while one was open for 0% -> 0% of each run, Pallas kernels for 0% -> 7%
where the time goes in v2:
time: 132 us
  waiting for transfers between devices  59.5 us (45%)
  Pallas kernels  35 us (27%)
  starting transfers between devices  27.4 us (21%)
  local copies, waits for them, and re-layouts  9.23 us (7%)
    all_to_all x1, waiting for transfers between devices, paired_body(): lax.all_to_all(factor_send, 'blk', split_axis=0, concat_axis=0, tiled=True)  35.4 us
    ppermute x16, waiting for transfers between devices, exchange(): return lax.ppermute(value, axes, perm)  24.1 us
    ppermute x16, starting transfers between devices, exchange(): return lax.ppermute(value, axes, perm)  20.1 us
    pallas_call x1, Pallas kernels, paired_body(): pl.pallas_call(gram_rest, out_shape=(shape(first_shape, F32),) * 4 + (sha...  17.4 us
    unnamed x21, local copies, waits for them, and re-layouts  9.11 us
    pallas_call x1, Pallas kernels, paired_body(): pl.pallas_call(gram_own, out_shape=(shape((half, 256, 256), BF16), shape(...  9.02 us
    all_to_all x1, starting transfers between devices, paired_body(): lax.all_to_all(factor_send, 'blk', split_axis=0, concat_axis=0, tiled=True)  7.27 us
    pallas_call x1, Pallas kernels, paired_body(): pl.pallas_call(pack_rows, out_shape=(pltpu.HBM((row_count, CTW), F32), sh...  4.43 us
  transfers between devices with their start and end apart: 17, of which 10 were waited for; matrix products, arithmetic and copies ran while one was open for 0% of the time, Pallas kernels for 7%

profile of v2, /device:TPU:0, one launch (start us, length us, event | category | flops | bytes accessed | tf_op | source)
XLA Modules:
  0.0 132.2 jit_solution(12809809307954416352)
XLA Ops:
  0.9 2.3 %copy-done = f32[12,384,256]{2,1,0:T(8,128)S(1)} copy-done((f32[12,384,256]{2,1,0:T(8,128)S(1)}, f32[12,384,256]{2,1,0:T(8,128)}, u32[]{:S(2)}) %copy-start) | copy-done | bytes 4718616
  4.5 4.4 %pack_rows.1 = (f32[4608,128]{1,0:T(8,128)}, s32[5,12]{1,0:T(8,128)S(1)}) custom-call(s32[96]{0:T(128)S(1)} %copy-done.6, s32[96]{0:T(128)S(1)} %copy-done.4, s32[768]{0:T(1024)S(1)} %reshape.3.pattern_ref, f32[12,384,256]{2,1,0:T(8,128)S(1)} %copy-done), custom_call_target="tpu_custom_call" | custom-call | tf_op jit(solution)/shard_map/pack_rows/pallas_call | solution.py:362
  9.0 4.2 %pack_own.1 = (f32[6,384,256]{2,1,0:T(8,128)}, f32[8,384,128]{2,1,0:T(8,128)}) custom-call(s32[5,12]{1,0:T(8,128)S(1)} %get-tuple-element.36.table_ref, s32[96]{0:T(128)S(1)} %copy-done.6, f32[12,384,256]{2,1,0:T(8,128)S(1)} %copy-done.1, f32[12,384,384]{2,1,0:T(8,128)} %inv_ref.1), custom_call_target="tpu_custom_call" | custom-call | tf_op jit(solution)/shard_map/pack_own/pallas_call | solution.py:380
  13.2 7.3 %all-to-all-start = ((f32[8,384,128]{2,1,0:T(8,128)}), f32[8,384,128]{2,1,0:T(8,128)S(1)}, u32[]{:S(2)}, u32[]{:S(2)}) async-start(f32[8,384,128]{2,1,0:T(8,128)} %get-tuple-element.39), calls=%async_computation | async-start | bytes 3145728 | tf_op jit(solution)/shard_map/all_to_all | solution.py:396
  20.4 1.6 %collective-permute-start = (f32[4608,128]{1,0:T(8,128)}, f32[4608,128]{1,0:T(8,128)}, u32[]{:S(2)}, u32[]{:S(2)}) collective-permute-start(f32[4608,128]{1,0:T(8,128)} %get-tuple-element.37), channel_id=1, source_target_pairs={{0,2},{1,3},{2,0},{3,1},{4,6},{5,7},{6,4},{7,5},{8,10},{9,11},{10,... | collective-permute-start | bytes 7077896 | tf_op jit(solution)/shard_map/ppermute | solution.py:352
  22.0 35.4 %all-to-all-done.factor_ref = f32[8,384,128]{2,1,0:T(8,128)S(1)} async-done(((f32[8,384,128]{2,1,0:T(8,128)}), f32[8,384,128]{2,1,0:T(8,128)S(1)}, u32[]{:S(2)}, u32[]{:S(2)}) %all-to-all-start) | async-done | bytes 1572896 | tf_op jit(solution)/shard_map/all_to_all | solution.py:396
  57.5 3.4 %collective-permute-done.2.factor_other = f32[8,384,128]{2,1,0:T(8,128)S(1)} collective-permute-done((f32[8,384,128]{2,1,0:T(8,128)S(1)}, f32[8,384,128]{2,1,0:T(8,128)S(1)}, u32[]{:S(2)}, u32[]{:S(2)}) %collective-permute-start.2) | collective-permute-done | bytes 1572896 | tf_op jit(solution)/shard_map/ppermute | solution.py:352
  62.1 9.0 %gram_own.1 = (bf16[6,256,256]{2,1,0:T(8,128)(2,1)S(1)}, bf16[6,256,256]{2,1,0:T(8,128)(2,1)S(1)}, bf16[6,128,384]{2,1,0:T(8,128)(2,1)S(1)}, bf16[6,128,384]{2,1...) custom-call(s32[5,12]{1,0:T(8,128)S(1)} %get-tuple-element.36.table_, ...), custom_call_target="tpu_custom_call" | custom-call | tf_op jit(solution)/shard_map/gram_own/pallas_call | solution.py:401
  74.4 4.7 %collective-permute-done.3.yc_ref = f32[4608,128]{1,0:T(8,128)S(1)} collective-permute-done((f32[4608,128]{1,0:T(8,128)}, f32[4608,128]{1,0:T(8,128)S(1)}, u32[]{:S(2)}, u32[]{:S(2)}) %collective-permute-start.3) | collective-permute-done | bytes 2359328 | tf_op jit(solution)/shard_map/ppermute | solution.py:352
  79.2 1.4 %copy-done.8 = f32[4608,128]{1,0:T(8,128)} copy-done((f32[4608,128]{1,0:T(8,128)}, f32[4608,128]{1,0:T(8,128)S(1)}, u32[]{:S(2)}) %copy-start.8) | copy-done | bytes 2359320
  80.6 17.4 %gram_rest.1 = (f32[4,88,256]{2,1,0:T(8,128)S(1)}, f32[4,88,256]{2,1,0:T(8,128)S(1)}, f32[4,88,256]{2,1,0:T(8,128)S(1)}, f32[4,88,256]{2,1,0:T(8,128)S(1)}, f32[...) custom-call(s32[5,12]{1,0:T(8,128)S(1)} %get-tuple-element.36.table_, ...), custom_call_target="tpu_custom_call" | custom-call | tf_op jit(solution)/shard_map/gram_rest/pallas_call | solution.py:430
  98.0 2.2 %collective-permute-start.10 = (f32[2,2,40,256]{3,2,1,0:T(8,128)S(1)}, f32[2,2,40,256]{3,2,1,0:T(8,128)S(1)}, u32[]{:S(2)}, u32[]{:S(2)}) collective-permute-start(f32[2,2,40,256]{3,2,1,0:T(8,128)S(1)} %get-tuple-element.64), channel_id=1, source_target_pairs={{0,8},{1,9},{2,10},{3,11},{4,12},{5,13},{6,14},{7,15},{8,0},{9,1},... | collective-permute-start | bytes 491528 | tf_op jit(solution)/shard_map/ppermute | solution.py:352
  100.2 2.3 %collective-permute-start.11 = (f32[2,2,40,256]{3,2,1,0:T(8,128)S(1)}, f32[2,2,40,256]{3,2,1,0:T(8,128)S(1)}, u32[]{:S(2)}, u32[]{:S(2)}) collective-permute-start(f32[2,2,40,256]{3,2,1,0:T(8,128)S(1)} %get-tuple-element.65), channel_id=1, source_target_pairs={{0,16},{1,17},{2,18},{3,19},{4,20},{5,21},{6,22},{7,23},{8,24},{9,... | collective-permute-start | bytes 491528 | tf_op jit(solution)/shard_map/ppermute | solution.py:352
  102.6 1.5 %collective-permute-start.4 = (f32[4,88,256]{2,1,0:T(8,128)S(1)}, f32[4,88,256]{2,1,0:T(8,128)S(1)}, u32[]{:S(2)}, u32[]{:S(2)}) collective-permute-start(f32[4,88,256]{2,1,0:T(8,128)S(1)} %get-tuple-element.60), channel_id=1, source_target_pairs={{0,2},{1,3},{2,0},{3,1},{4,6},{5,7},{6,4},{7,5},{8,10},{9,11},{10,... | collective-permute-start | bytes 1081352 | tf_op jit(solution)/shard_map/ppermute | solution.py:352
  104.1 1.9 %collective-permute-start.5 = (f32[4,88,256]{2,1,0:T(8,128)S(1)}, f32[4,88,256]{2,1,0:T(8,128)S(1)}, u32[]{:S(2)}, u32[]{:S(2)}) collective-permute-start(f32[4,88,256]{2,1,0:T(8,128)S(1)} %get-tuple-element.61), channel_id=1, source_target_pairs={{0,4},{1,5},{2,6},{3,7},{4,0},{5,1},{6,2},{7,3},{8,12},{9,13},{10,... | collective-permute-start | bytes 1081352 | tf_op jit(solution)/shard_map/ppermute | solution.py:352
  106.0 1.3 %collective-permute-done.10 = f32[2,2,40,256]{3,2,1,0:T(8,128)S(1)} collective-permute-done((f32[2,2,40,256]{3,2,1,0:T(8,128)S(1)}, f32[2,2,40,256]{3,2,1,0:T(8,128)S(1)}, u32[]{:S(2)}, u32[]{:S(2)}) %collective-permute-start.10) | collective-permute-done | bytes 163872 | tf_op jit(solution)/shard_map/ppermute | solution.py:352
  107.3 2.8 %collective-permute-start.6 = (f32[4,88,256]{2,1,0:T(8,128)S(1)}, f32[4,88,256]{2,1,0:T(8,128)S(1)}, u32[]{:S(2)}, u32[]{:S(2)}) collective-permute-start(f32[4,88,256]{2,1,0:T(8,128)S(1)} %get-tuple-element.62), channel_id=1, source_target_pairs={{0,6},{1,7},{2,4},{3,5},{4,2},{5,3},{6,0},{7,1},{8,14},{9,15},{10,... | collective-permute-start | bytes 1081352 | tf_op jit(solution)/shard_map/ppermute | solution.py:352
  110.2 5.0 %collective-permute-done.11 = f32[2,2,40,256]{3,2,1,0:T(8,128)S(1)} collective-permute-done((f32[2,2,40,256]{3,2,1,0:T(8,128)S(1)}, f32[2,2,40,256]{3,2,1,0:T(8,128)S(1)}, u32[]{:S(2)}, u32[]{:S(2)}) %collective-permute-start.11) | collective-permute-done | bytes 163872 | tf_op jit(solution)/shard_map/ppermute | solution.py:352
  115.2 1.5 %collective-permute-start.14 = (f32[40,256]{1,0:T(8,128)S(1)}, f32[40,256]{1,0:T(8,128)S(1)}, u32[]{:S(2)}, u32[]{:S(2)}) collective-permute-start(f32[40,256]{1,0:T(8,128)S(1)} %get-tuple-element.70), channel_id=1, source_target_pairs={{0,4},{1,5},{2,6},{3,7},{4,0},{5,1},{6,2},{7,3},{8,12},{9,13},{10,... | collective-permute-start | bytes 122888 | tf_op jit(solution)/shard_map/ppermute | solution.py:352
  116.8 1.5 %collective-permute-start.15 = (f32[40,256]{1,0:T(8,128)S(1)}, f32[40,256]{1,0:T(8,128)S(1)}, u32[]{:S(2)}, u32[]{:S(2)}) collective-permute-start(f32[40,256]{1,0:T(8,128)S(1)} %get-tuple-element.71), channel_id=1, source_target_pairs={{0,6},{1,7},{2,4},{3,5},{4,2},{5,3},{6,0},{7,1},{8,14},{9,15},{10,... | collective-permute-start | bytes 122888 | tf_op jit(solution)/shard_map/ppermute | solution.py:352
  118.8 3.5 %collective-permute-done.6 = f32[4,88,256]{2,1,0:T(8,128)S(1)} collective-permute-done((f32[4,88,256]{2,1,0:T(8,128)S(1)}, f32[4,88,256]{2,1,0:T(8,128)S(1)}, u32[]{:S(2)}, u32[]{:S(2)}) %collective-permute-start.6) | collective-permute-done | bytes 360480 | tf_op jit(solution)/shard_map/ppermute | solution.py:352
  122.4 1.8 %collective-permute-start.8 = (f32[88,256]{1,0:T(8,128)S(1)}, f32[88,256]{1,0:T(8,128)S(1)}, u32[]{:S(2)}, u32[]{:S(2)}) collective-permute-start(f32[88,256]{1,0:T(8,128)S(1)} %get-tuple-element.67), channel_id=1, source_target_pairs={{0,16},{1,17},{2,18},{3,19},{4,20},{5,21},{6,22},{7,23},{8,24},{9,... | collective-permute-start | bytes 270344 | tf_op jit(solution)/shard_map/ppermute | solution.py:352
  124.2 1.9 %collective-permute-start.9 = (f32[88,256]{1,0:T(8,128)S(1)}, f32[88,256]{1,0:T(8,128)S(1)}, u32[]{:S(2)}, u32[]{:S(2)}) collective-permute-start(f32[88,256]{1,0:T(8,128)S(1)} %get-tuple-element.68), channel_id=1, source_target_pairs={{0,24},{1,25},{2,26},{3,27},{4,28},{5,29},{6,30},{7,31},{8,16},{9,... | collective-permute-start | bytes 270344 | tf_op jit(solution)/shard_map/ppermute | solution.py:352
  126.6 2.7 %collective-permute-done.8 = f32[88,256]{1,0:T(8,128)S(1)} collective-permute-done((f32[88,256]{1,0:T(8,128)S(1)}, f32[88,256]{1,0:T(8,128)S(1)}, u32[]{:S(2)}, u32[]{:S(2)}) %collective-permute-start.8) | collective-permute-done | bytes 90144 | tf_op jit(solution)/shard_map/ppermute | solution.py:352
  (43 shorter events, 11.0 us)
Async XLA Ops:
  0.9 2.3 %copy-start = (f32[12,384,256]{2,1,0:T(8,128)S(1)}, f32[12,384,256]{2,1,0:T(8,128)}, u32[]{:S(2)}) copy-start(f32[12,384,256]{2,1,0:T(8,128)} %blocks_ref.3) | copy-start | bytes 14155780
  4.5 4.4 %copy-start.1 = (f32[12,384,256]{2,1,0:T(8,128)S(1)}, f32[12,384,256]{2,1,0:T(8,128)}, u32[]{:S(2)}) copy-start(f32[12,384,256]{2,1,0:T(8,128)} %blocks_ref.3) | copy-start | bytes 14155780
  13.2 48.9 %copy-start.5 = (s32[96]{0:T(128)S(1)}, s32[96]{0:T(128)}, u32[]{:S(2)}) copy-start(s32[96]{0:T(128)} %orders_ref.5) | copy-start | bytes 1156
  13.2 44.3 %all-to-all-start = ((f32[8,384,128]{2,1,0:T(8,128)}), f32[8,384,128]{2,1,0:T(8,128)S(1)}, u32[]{:S(2)}, u32[]{:S(2)}) async-start(f32[8,384,128]{2,1,0:T(8,128)} %get-tuple-element.39), calls=%async_computation | async-start | bytes 3145728 | tf_op jit(solution)/shard_map/all_to_all | solution.py:396
  20.4 37.0 %collective-permute-start.1 = (f32[6,384,256]{2,1,0:T(8,128)}, f32[6,384,256]{2,1,0:T(8,128)}, u32[]{:S(2)}, u32[]{:S(2)}) collective-permute-start(f32[6,384,256]{2,1,0:T(8,128)} %get-tuple-element.38.own_ref), channel_id=1, source_target_pairs={{0,1},{1,0},{2,3},{3,2},{4,5},{5,4},{6,7},{7,6},{8,9},{9,8},{10,11... | collective-permute-start | bytes 7077896 | tf_op jit(solution)/shard_map/ppermute | solution.py:352
  20.4 54.0 %collective-permute-start = (f32[4608,128]{1,0:T(8,128)}, f32[4608,128]{1,0:T(8,128)}, u32[]{:S(2)}, u32[]{:S(2)}) collective-permute-start(f32[4608,128]{1,0:T(8,128)} %get-tuple-element.37), channel_id=1, source_target_pairs={{0,2},{1,3},{2,0},{3,1},{4,6},{5,7},{6,4},{7,5},{8,10},{9,11},{10,... | collective-permute-start | bytes 7077896 | tf_op jit(solution)/shard_map/ppermute | solution.py:352
  57.4 3.4 %copy-start.7 = (f32[8,384,128]{2,1,0:T(8,128)}, f32[8,384,128]{2,1,0:T(8,128)S(1)}, u32[]{:S(2)}) copy-start(f32[8,384,128]{2,1,0:T(8,128)S(1)} %all-to-all-done.factor_ref) | copy-start | bytes 4718596
  57.4 3.4 %collective-permute-start.2 = (f32[8,384,128]{2,1,0:T(8,128)S(1)}, f32[8,384,128]{2,1,0:T(8,128)S(1)}, u32[]{:S(2)}, u32[]{:S(2)}) collective-permute-start(f32[8,384,128]{2,1,0:T(8,128)S(1)} %all-to-all-done.factor_ref), channel_id=1, source_target_pairs={{0,1},{1,0},{2,3},{3,2},{4,5},{5,4},{6,7},{7,6},{8,9},{9,8},{10,11... | collective-permute-start | bytes 4718600 | tf_op jit(solution)/shard_map/ppermute | solution.py:352
  60.9 1.2 copy-start.9
  71.1 1.0 copy-start.2
  74.4 4.7 %collective-permute-start.3 = (f32[4608,128]{1,0:T(8,128)}, f32[4608,128]{1,0:T(8,128)S(1)}, u32[]{:S(2)}, u32[]{:S(2)}) collective-permute-start(f32[4608,128]{1,0:T(8,128)} %collective-permute-done.y_ref), channel_id=1, source_target_pairs={{0,1},{1,0},{2,3},{3,2},{4,5},{5,4},{6,7},{7,6},{8,9},{9,8},{10,11... | collective-permute-start | bytes 7077896 | tf_op jit(solution)/shard_map/ppermute | solution.py:352
  79.2 1.4 %copy-start.8 = (f32[4608,128]{1,0:T(8,128)}, f32[4608,128]{1,0:T(8,128)S(1)}, u32[]{:S(2)}) copy-start(f32[4608,128]{1,0:T(8,128)S(1)} %collective-permute-done.3.yc_ref) | copy-start | bytes 7077892
  98.0 9.3 %collective-permute-start.10 = (f32[2,2,40,256]{3,2,1,0:T(8,128)S(1)}, f32[2,2,40,256]{3,2,1,0:T(8,128)S(1)}, u32[]{:S(2)}, u32[]{:S(2)}) collective-permute-start(f32[2,2,40,256]{3,2,1,0:T(8,128)S(1)} %get-tuple-element.64), channel_id=1, source_target_pairs={{0,8},{1,9},{2,10},{3,11},{4,12},{5,13},{6,14},{7,15},{8,0},{9,1},... | collective-permute-start | bytes 491528 | tf_op jit(solution)/shard_map/ppermute | solution.py:352
  100.2 15.0 %collective-permute-start.11 = (f32[2,2,40,256]{3,2,1,0:T(8,128)S(1)}, f32[2,2,40,256]{3,2,1,0:T(8,128)S(1)}, u32[]{:S(2)}, u32[]{:S(2)}) collective-permute-start(f32[2,2,40,256]{3,2,1,0:T(8,128)S(1)} %get-tuple-element.65), channel_id=1, source_target_pairs={{0,16},{1,17},{2,18},{3,19},{4,20},{5,21},{6,22},{7,23},{8,24},{9,... | collective-permute-start | bytes 491528 | tf_op jit(solution)/shard_map/ppermute | solution.py:352
  102.5 12.7 %collective-permute-start.12 = (f32[2,2,40,256]{3,2,1,0:T(8,128)S(1)}, f32[2,2,40,256]{3,2,1,0:T(8,128)S(1)}, u32[]{:S(2)}, u32[]{:S(2)}) collective-permute-start(f32[2,2,40,256]{3,2,1,0:T(8,128)S(1)} %get-tuple-element.66), channel_id=1, source_target_pairs={{0,24},{1,25},{2,26},{3,27},{4,28},{5,29},{6,30},{7,31},{8,16},{9,... | collective-permute-start | bytes 491528 | tf_op jit(solution)/shard_map/ppermute | solution.py:352
  102.6 15.6 %collective-permute-start.4 = (f32[4,88,256]{2,1,0:T(8,128)S(1)}, f32[4,88,256]{2,1,0:T(8,128)S(1)}, u32[]{:S(2)}, u32[]{:S(2)}) collective-permute-start(f32[4,88,256]{2,1,0:T(8,128)S(1)} %get-tuple-element.60), channel_id=1, source_target_pairs={{0,2},{1,3},{2,0},{3,1},{4,6},{5,7},{6,4},{7,5},{8,10},{9,11},{10,... | collective-permute-start | bytes 1081352 | tf_op jit(solution)/shard_map/ppermute | solution.py:352
  104.1 14.7 %collective-permute-start.5 = (f32[4,88,256]{2,1,0:T(8,128)S(1)}, f32[4,88,256]{2,1,0:T(8,128)S(1)}, u32[]{:S(2)}, u32[]{:S(2)}) collective-permute-start(f32[4,88,256]{2,1,0:T(8,128)S(1)} %get-tuple-element.61), channel_id=1, source_target_pairs={{0,4},{1,5},{2,6},{3,7},{4,0},{5,1},{6,2},{7,3},{8,12},{9,13},{10,... | collective-permute-start | bytes 1081352 | tf_op jit(solution)/shard_map/ppermute | solution.py:352
  107.3 14.9 %collective-permute-start.6 = (f32[4,88,256]{2,1,0:T(8,128)S(1)}, f32[4,88,256]{2,1,0:T(8,128)S(1)}, u32[]{:S(2)}, u32[]{:S(2)}) collective-permute-start(f32[4,88,256]{2,1,0:T(8,128)S(1)} %get-tuple-element.62), channel_id=1, source_target_pairs={{0,6},{1,7},{2,4},{3,5},{4,2},{5,3},{6,0},{7,1},{8,14},{9,15},{10,... | collective-permute-start | bytes 1081352 | tf_op jit(solution)/shard_map/ppermute | solution.py:352
  115.2 10.8 %collective-permute-start.14 = (f32[40,256]{1,0:T(8,128)S(1)}, f32[40,256]{1,0:T(8,128)S(1)}, u32[]{:S(2)}, u32[]{:S(2)}) collective-permute-start(f32[40,256]{1,0:T(8,128)S(1)} %get-tuple-element.70), channel_id=1, source_target_pairs={{0,4},{1,5},{2,6},{3,7},{4,0},{5,1},{6,2},{7,3},{8,12},{9,13},{10,... | collective-permute-start | bytes 122888 | tf_op jit(solution)/shard_map/ppermute | solution.py:352
  116.8 9.8 %collective-permute-start.15 = (f32[40,256]{1,0:T(8,128)S(1)}, f32[40,256]{1,0:T(8,128)S(1)}, u32[]{:S(2)}, u32[]{:S(2)}) collective-permute-start(f32[40,256]{1,0:T(8,128)S(1)} %get-tuple-element.71), channel_id=1, source_target_pairs={{0,6},{1,7},{2,4},{3,5},{4,2},{5,3},{6,0},{7,1},{8,14},{9,15},{10,... | collective-permute-start | bytes 122888 | tf_op jit(solution)/shard_map/ppermute | solution.py:352
  118.2 8.4 %collective-permute-start.13 = (f32[40,256]{1,0:T(8,128)S(1)}, f32[40,256]{1,0:T(8,128)S(1)}, u32[]{:S(2)}, u32[]{:S(2)}) collective-permute-start(f32[40,256]{1,0:T(8,128)S(1)} %get-tuple-element.72), channel_id=1, source_target_pairs={{0,2},{1,3},{2,0},{3,1},{4,6},{5,7},{6,4},{7,5},{8,10},{9,11},{10,... | collective-permute-start | bytes 122888 | tf_op jit(solution)/shard_map/ppermute | solution.py:352
  122.4 6.9 %collective-permute-start.8 = (f32[88,256]{1,0:T(8,128)S(1)}, f32[88,256]{1,0:T(8,128)S(1)}, u32[]{:S(2)}, u32[]{:S(2)}) collective-permute-start(f32[88,256]{1,0:T(8,128)S(1)} %get-tuple-element.67), channel_id=1, source_target_pairs={{0,16},{1,17},{2,18},{3,19},{4,20},{5,21},{6,22},{7,23},{8,24},{9,... | collective-permute-start | bytes 270344 | tf_op jit(solution)/shard_map/ppermute | solution.py:352
  124.2 6.4 %collective-permute-start.9 = (f32[88,256]{1,0:T(8,128)S(1)}, f32[88,256]{1,0:T(8,128)S(1)}, u32[]{:S(2)}, u32[]{:S(2)}) collective-permute-start(f32[88,256]{1,0:T(8,128)S(1)} %get-tuple-element.68), channel_id=1, source_target_pairs={{0,24},{1,25},{2,26},{3,27},{4,28},{5,29},{6,30},{7,31},{8,16},{9,... | collective-permute-start | bytes 270344 | tf_op jit(solution)/shard_map/ppermute | solution.py:352
  126.1 5.4 %collective-permute-start.7 = (f32[88,256]{1,0:T(8,128)S(1)}, f32[88,256]{1,0:T(8,128)S(1)}, u32[]{:S(2)}, u32[]{:S(2)}) collective-permute-start(f32[88,256]{1,0:T(8,128)S(1)} %get-tuple-element.69), channel_id=1, source_target_pairs={{0,8},{1,9},{2,10},{3,11},{4,12},{5,13},{6,14},{7,15},{8,0},{9,1},... | collective-permute-start | bytes 270344 | tf_op jit(solution)/shard_map/ppermute | solution.py:352
  (3 other events, 2.4 us)

commit v3 on v0

v3 whole, which is shorter than its diff:
```python
import functools

import jax
import jax.numpy as jnp
from jax import lax
from jax.experimental import pallas as pl
from jax.experimental.pallas import tpu as pltpu
from jax.sharding import PartitionSpec as P

CTW = 128
F32 = jnp.float32
BF16 = jnp.bfloat16
XY_FIRST = 88
VMEM_LIMIT = 32 << 20


def general_body(blocks, orders, pattern, dest, inv_factor):
    source_index = lax.axis_index("blk")
    owner_count = lax.axis_size("blk")
    tile_index = lax.axis_index("tile")
    slot_count, max_order, column_width = blocks.shape
    block_count = dest.shape[0]
    tiles_here = column_width // CTW
    highest = lax.Precision.HIGHEST
    capacity = (slot_count + owner_count - 1) // owner_count
    dest_grid = dest.reshape(owner_count, slot_count)
    earlier = lax.broadcasted_iota(jnp.int32, (slot_count, slot_count), 1) < lax.broadcasted_iota(
        jnp.int32, (slot_count, slot_count), 0
    )
    matching = dest_grid[:, :, None] == dest_grid[:, None, :]
    ranks = jnp.sum((matching & earlier[None]).astype(jnp.int32), axis=2).reshape(block_count)
    my_dest = lax.dynamic_slice_in_dim(dest, source_index * slot_count, slot_count)
    my_rank = lax.dynamic_slice_in_dim(ranks, source_index * slot_count, slot_count)
    my_orders = lax.dynamic_slice_in_dim(orders, source_index * slot_count, slot_count)
    my_tiles = lax.dynamic_slice(
        pattern, (source_index * slot_count, tile_index * tiles_here), (slot_count, tiles_here)
    )
    row_ids = lax.broadcasted_iota(jnp.int32, (slot_count, max_order), 1)
    row_mask = (row_ids < my_orders[:, None]).astype(F32)
    col_mask = jnp.repeat(my_tiles.astype(F32), CTW, axis=1)
    masked = blocks * row_mask[:, :, None] * col_mask[:, None, :]
    owned = lax.dynamic_slice_in_dim(
        jnp.argsort(dest, stable=True), source_index * slot_count, slot_count
    )
    slot_ids = my_dest * capacity + my_rank
    placing = (
        lax.broadcasted_iota(jnp.int32, (owner_count * capacity, slot_count), 0)
        == slot_ids[None, :]
    ).astype(F32)
    outgoing = jnp.einsum("ak,krc->arc", placing, masked, precision=highest, preferred_element_type=F32)
    arrived = lax.all_to_all(outgoing, "blk", split_axis=0, concat_axis=0, tiled=True)
    positions = owned // slot_count * capacity + ranks[owned]
    own_blocks = jnp.take(arrived, positions, axis=0)
    own_mask = (row_ids < orders[owned][:, None]).astype(F32)
    whitened = jnp.einsum(
        "jrq,jqc->jrc", inv_factor, own_blocks, precision=highest, preferred_element_type=F32
    )
    whitened_rows = (whitened * own_mask[:, :, None]).reshape(slot_count * max_order, column_width)
    factor = 1.0 / (block_count * max_order**0.5)
    partial_sums = lax.dot_general(
        lax.all_gather(whitened_rows, "tile", axis=1, tiled=True),
        whitened_rows,
        (((0,), (0,)), ((), ())),
        precision=highest,
        preferred_element_type=F32,
    )
    gram_tile = lax.psum_scatter(partial_sums, "blk", scatter_dimension=0, tiled=True)
    return gram_tile * factor


MINE, OWNER, ORDER, BITS, OTHERS, ORDER_OTHERS, BITS_OTHERS, ROW_AT = 0, 1, 2, 3, 4, 5, 6, 7
SHARES = (0.625, 1.0)


def round8(order):
    return (order + 7) // 8 * 8


def row_counts(all_rows):
    return [int(share * all_rows) // 8 * 8 for share in SHARES]


def plan(
    dest_ref, weight_ref, orders_ref, pattern_ref, blocks_ref, inv_ref, own_out, factor_out, table_ref, level_ref,
    block_at, count, found_at, factor_at, sem,
):
    s = lax.axis_index("blk")
    t = lax.axis_index("tile")
    y, c = t // 2, t % 2
    slots, max_order, width = blocks_ref.shape
    n_blk = count.shape[0]
    tiles = width // CTW

    def scan_source(source, carry):
        found, most = carry
        for o in range(n_blk):
            count[o] = 0
            block_at[0, o] = 0
            block_at[1, o] = 0
        for i in range(slots):
            o = dest_ref[source * slots + i]
            r = count[o]
            block_at[r, o] = i
            count[o] = r + 1
            mine = o == s
            found_at[jnp.where(mine, r, 2)] = found
            found = found + jnp.where(mine, 1, 0)

        def place_pair(o, carry):
            p, sent = carry[0], carry[1:]
            on = count[o] > 0
            first, second = block_at[0, o], block_at[1, o]
            w_first = [weight_ref[q, source * slots + first] for q in range(4)]
            w_second = [weight_ref[q, source * slots + second] for q in range(4)]
            straight = [sent[q] + (w_second[q] if q < 2 else w_first[q]) for q in range(4)]
            crossed = [sent[q] + (w_first[q] if q < 2 else w_second[q]) for q in range(4)]

            def top(v):
                return jnp.maximum(jnp.maximum(v[0], v[1]), jnp.maximum(v[2], v[3]))

            flip = jnp.where(top(crossed) < top(straight), 1, 0)

            @pl.when(on & (o == s))
            def _():
                factor_at[source] = found_at[y ^ flip]

            @pl.when(on & (source == s))
            def _():
                here, there = jnp.where((y ^ flip) == 0, first, second), jnp.where((y ^ flip) == 0, second, first)
                table_ref[MINE, p] = here
                table_ref[OTHERS, p] = there
                table_ref[OWNER, p] = o

            sent = [jnp.where(on, jnp.where(flip == 1, f, d), q) for f, d, q in zip(crossed, straight, sent)]
            return (p + jnp.where(on, 1, 0), *sent)

        factor_at[source] = 0
        zero = jnp.int32(0)
        sent = lax.fori_loop(0, n_blk, place_pair, (zero,) * 5)[1:]
        for q in sent:
            most = jnp.maximum(most, q)
        return found, most

    most = lax.fori_loop(0, n_blk, scan_source, (jnp.int32(0), jnp.int32(0)))[1]

    def factor_loads():
        for source in range(n_blk):
            row = factor_at[source]
            for k, (ti, tj) in enumerate(((0, 0), (1, 0), (1, 1))):
                ri, rj = jnp.where(c == 0, ti, 2), jnp.where(c == 0, tj, k)
                yield pltpu.make_async_copy(
                    inv_ref.at[row, pl.ds(pl.multiple_of(ri * 128, 128), 128), pl.ds(pl.multiple_of(rj * 128, 128), 128)],
                    factor_out.at[source, pl.ds(k * 128, 128), :],
                    sem,
                )

    def own_loads():
        for p in range(slots // 2):
            yield pltpu.make_async_copy(blocks_ref.at[table_ref[MINE, p]], own_out.at[p], sem)

    for copy in factor_loads():
        copy.start()
    for copy in own_loads():
        copy.start()

    level = jnp.int32(0)
    for rows in row_counts(slots // 2 * tiles * max_order)[:-1]:
        level = level + jnp.where(most + (max_order - 96) > rows, 1, 0)
    level_ref[0] = level

    for which, order_row, bits_row in ((MINE, ORDER, BITS), (OTHERS, ORDER_OTHERS, BITS_OTHERS)):
        for p in range(slots // 2):
            number = s * slots + table_ref[which, p]
            table_ref[order_row, p] = orders_ref[number]
            bits = jnp.int32(0)
            for ct in range(4 * tiles):
                bits = bits + jnp.where(pattern_ref[ct, number] != 0, 1 << ct, 0)
            table_ref[bits_row, p] = bits
    for k in range(2):
        at = jnp.int32(0)
        for p in range(slots // 2):
            rows, bits = round8(table_ref[ORDER, p]), table_ref[BITS, p]
            for e in range(tiles):
                table_ref[ROW_AT + k, p * tiles + e] = at
                at = at + jnp.where(tile_on(bits, (t ^ (2 + k)) * tiles + e), rows, 0)

    for copy in own_loads():
        copy.wait()
    for copy in factor_loads():
        copy.wait()


def tile_on(bits, tile):
    return ((bits >> tile) & 1) == 1


def pack_rows(table_ref, blocks_ref, packed, staged, sems):
    t = lax.axis_index("tile")
    slots, max_order, width = blocks_ref.shape
    tiles = width // CTW

    def loads():
        for p in range(slots // 2):
            yield pltpu.make_async_copy(blocks_ref.at[table_ref[OTHERS, p]], staged.at[p], sems.at[p])

    for copy in loads():
        copy.start()
    at = jnp.int32(0)
    for p, copy in enumerate(loads()):
        copy.wait()
        for e in range(tiles):
            on = tile_on(table_ref[BITS_OTHERS, p], t * tiles + e)

            @pl.when(on)
            def _(at=at, p=p, e=e):
                packed[pl.ds(pl.multiple_of(at, 8), max_order), :] = staged[p, :, e * CTW : (e + 1) * CTW]

            at = at + jnp.where(on, round8(table_ref[ORDER_OTHERS, p]), 0)


def split(x):
    high = x.astype(BF16)
    return high, (x - high.astype(F32)).astype(BF16)


def dot3(a, b):
    def dot(p, q):
        return jnp.dot(p, q, preferred_element_type=F32)

    return dot(a[0], b[0]) + (dot(a[0], b[1]) + dot(a[1], b[0]))


def whiten(tiles, table_ref, p, upper, lower, tile_ids):
    row_on = lax.broadcasted_iota(jnp.int32, tiles[0].shape, 0) < table_ref[ORDER, p]
    parts = [
        jnp.where(row_on & tile_on(table_ref[BITS, p], ct), tile, 0.0) for tile, ct in zip(tiles, tile_ids)
    ]
    x = split(jnp.concatenate(parts, axis=1))
    w = jnp.concatenate([dot3(upper, (x[0][:256], x[1][:256])), dot3(lower, x)], axis=0)
    return [jnp.where(row_on, w[:, i * CTW : (i + 1) * CTW], 0.0) for i in range(len(tiles))]


def gram_own(
    table_ref, own_ref, core_ref, factor_ref, factor_other,
    upper_high, upper_low, lower_high, lower_low, w0_high, w0_low, w1t_high, w1t_low, g_out,
    w0t_high, w0t_low,
):
    t = lax.axis_index("tile")
    c = t % 2
    half, max_order, width = own_ref.shape
    for p in range(half):
        here, there = factor_ref[table_ref[OWNER, p]], factor_other[table_ref[OWNER, p]]
        top, low = jnp.where(c == 0, here, there), jnp.where(c == 0, there, here)
        f00, f10, f11 = top[:128], top[128:256], top[256:]
        upper = split(
            jnp.concatenate(
                [jnp.concatenate([f00, jnp.zeros_like(f00)], axis=1), jnp.concatenate([f10, f11], axis=1)], axis=0
            )
        )
        lower = split(jnp.concatenate([low[:128], low[128:256], low[256:]], axis=1))
        upper_high[p], upper_low[p] = upper
        lower_high[p], lower_low[p] = lower
        tiles = [ref[p, :, e * CTW : (e + 1) * CTW] for ref in (own_ref, core_ref) for e in range(2)]
        tile_ids = [(t ^ m) * 2 + e for m in range(2) for e in range(2)]
        w = whiten(tiles, table_ref, p, upper, lower, tile_ids)
        rows = pl.ds(p * max_order, max_order)
        w0, w1 = jnp.concatenate(w[:2], axis=1), jnp.concatenate(w[2:], axis=1)
        w0_high[rows, :], w0_low[rows, :] = split(w0)
        w0t_high[:, rows], w0t_low[:, rows] = split(w0.T)
        w1t_high[:, rows], w1t_low[:, rows] = split(w1.T)
    w0 = w0_high[...], w0_low[...]
    g_out[0] = dot3((w0t_high[...], w0t_low[...]), w0)
    g_out[1] = dot3((w1t_high[...], w1t_low[...]), w0)


def gram_rest(
    table_ref, y_ref, yc_ref,
    upper_high, upper_low, lower_high, lower_low, w0_high, w0_low, w1t_high, w1t_low, g_own,
    *refs,
):
    firsts, seconds = refs[:4], refs[4:8]
    w2_high, w2_low, w23t_high, w23t_low, gram, out_sem = refs[8:]
    s = lax.axis_index("blk")
    t = lax.axis_index("tile")
    half = upper_high.shape[0]
    depth, width = w0_high.shape
    max_order = depth // half
    last = y_ref.shape[0] - max_order
    for p in range(half):
        tiles = []
        for k, ref in enumerate((y_ref, yc_ref)):
            for e in range(2):
                at = pl.multiple_of(jnp.minimum(table_ref[ROW_AT + k, p * 2 + e], last), 8)
                tiles.append(ref[pl.ds(at, max_order), :])
        tile_ids = [(t ^ (2 + k)) * 2 + e for k in range(2) for e in range(2)]
        upper, lower = (upper_high[p], upper_low[p]), (lower_high[p], lower_low[p])
        w = whiten(tiles, table_ref, p, upper, lower, tile_ids)
        rows = pl.ds(p * max_order, max_order)
        w2_high[rows, :], w2_low[rows, :] = split(jnp.concatenate(w[:2], axis=1))
        w23t_high[:, rows], w23t_low[:, rows] = split(jnp.concatenate(w, axis=1).T)

    w0, w2 = (w0_high[...], w0_low[...]), (w2_high[...], w2_low[...])
    w1t, w23t = (w1t_high[...], w1t_low[...]), (w23t_high[...], w23t_low[...])
    gram[0, 0] = g_own[0]
    gram[0, 1] = g_own[1]
    g = dot3(w23t, w0)
    gram[0, 2] = g[:width]
    gram[0, 3] = g[width:]
    gram[1, 0] = g[:width].T
    gram[1, 1] = dot3(w1t, w2)
    g = dot3(w23t, w2)
    gram[1, 2] = g[:width]
    gram[1, 3] = g[width:]

    z, x = s // 2, s % 2

    def stores():
        for n in range(4):
            for a in range(2):
                for b in range(2):
                    m, at = (z ^ n) ^ t, (x ^ a) * 128
                    first, second = firsts[2 * a + b], seconds[n]
                    yield pltpu.make_async_copy(
                        gram.at[b, m, pl.ds(pl.multiple_of(at, 8), XY_FIRST), :], first.at[n], out_sem
                    )
                    yield pltpu.make_async_copy(
                        gram.at[b, m, pl.ds(pl.multiple_of(at + XY_FIRST, 8), 128 - XY_FIRST), :],
                        second.at[a, b],
                        out_sem,
                    )

    for copy in stores():
        copy.start()
    for copy in stores():
        copy.wait()


def paired_body(blocks, orders, pattern, dest, inv_factor):
    slots, max_order, width = blocks.shape
    n_blk = lax.axis_size("blk")
    half = slots // 2
    tiles = width // CTW
    blocks = pltpu.with_memory_space_constraint(blocks, pltpu.HBM)
    inv_factor = pltpu.with_memory_space_constraint(inv_factor, pltpu.HBM)
    pattern = pattern.T
    weights = round8(orders)[None, :] * jnp.sum((pattern != 0).astype(jnp.int32).reshape(4, tiles, -1), axis=1)
    hbm = pl.BlockSpec(memory_space=pltpu.HBM)
    smem = pl.BlockSpec(memory_space=pltpu.SMEM)
    vmem = pl.BlockSpec(memory_space=pltpu.VMEM)
    shape = jax.ShapeDtypeStruct
    own, factor_send, table, level = pl.pallas_call(
        plan,
        out_shape=(
            shape((half, max_order, width), F32),
            shape((n_blk, max_order, CTW), F32),
            shape((9, half * tiles), jnp.int32),
            shape((1,), jnp.int32),
        ),
        in_specs=[smem] * 4 + [hbm] * 2,
        out_specs=(vmem, vmem, smem, smem),
        scratch_shapes=[
            pltpu.SMEM((2, n_blk), jnp.int32),
            pltpu.SMEM((n_blk,), jnp.int32),
            pltpu.SMEM((3,), jnp.int32),
            pltpu.SMEM((n_blk,), jnp.int32),
            pltpu.SemaphoreType.DMA,
        ],
        compiler_params=pltpu.CompilerParams(vmem_limit_bytes=VMEM_LIMIT),
        name="plan",
    )(dest, weights, orders, pattern, blocks, inv_factor)
    rest = [functools.partial(paired_rest, rows) for rows in row_counts(half * tiles * max_order)]
    gram_tile = lax.switch(level[0], rest, table, blocks, own, factor_send)
    return gram_tile * (1.0 / (dest.shape[0] * max_order**0.5))


def paired_rest(row_count, table, blocks, own, factor_send):
    slots, max_order, width = blocks.shape
    n_blk = lax.axis_size("blk")
    n_tile = lax.axis_size("tile")
    half = slots // 2
    tiles = width // CTW
    axes = ("blk", "tile")

    def exchange(value, blk_bits, tile_bits):
        perm = [
            (b * n_tile + t, (b ^ blk_bits) * n_tile + (t ^ tile_bits)) for b in range(n_blk) for t in range(n_tile)
        ]
        return lax.ppermute(value, axes, perm)

    hbm = pl.BlockSpec(memory_space=pltpu.HBM)
    smem = pl.BlockSpec(memory_space=pltpu.SMEM)
    vmem = pl.BlockSpec(memory_space=pltpu.VMEM)
    any_space = pl.BlockSpec(memory_space=pl.ANY)
    shape = jax.ShapeDtypeStruct
    params = pltpu.CompilerParams(vmem_limit_bytes=VMEM_LIMIT)
    dma = pltpu.SemaphoreType.DMA

    y_rows = pl.pallas_call(
        pack_rows,
        out_shape=shape((row_count, CTW), F32),
        in_specs=[smem, hbm],
        out_specs=vmem,
        scratch_shapes=[pltpu.VMEM((half, max_order, width), F32), dma((half,))],
        compiler_params=params,
        name="pack_rows",
    )(table, blocks)
    y_recv = exchange(y_rows, 0, 2)
    factors = lax.all_to_all(factor_send, "blk", split_axis=0, concat_axis=0, tiled=True)
    core_recv = exchange(own, 0, 1)
    factors_other = exchange(factors, 0, 1)

    depth = half * max_order
    own_results = pl.pallas_call(
        gram_own,
        out_shape=(
            shape((half, 256, 256), BF16),
            shape((half, 256, 256), BF16),
            shape((half, 128, 384), BF16),
            shape((half, 128, 384), BF16),
            shape((depth, width), BF16),
            shape((depth, width), BF16),
            shape((width, depth), BF16),
            shape((width, depth), BF16),
            shape((2, width, width), F32),
        ),
        in_specs=[smem] + [vmem] * 4,
        out_specs=(vmem,) * 9,
        scratch_shapes=[pltpu.VMEM((width, depth), BF16), pltpu.VMEM((width, depth), BF16)],
        compiler_params=params,
        name="gram_own",
    )(table, own, core_recv, factors, factors_other)

    yc_recv = exchange(y_recv, 0, 1)
    first_shape, second_shape = (4, XY_FIRST, width), (2, 2, 128 - XY_FIRST, width)
    pieces = pl.pallas_call(
        gram_rest,
        out_shape=(shape(first_shape, F32),) * 4 + (shape(second_shape, F32),) * 4,
        in_specs=[smem] + [vmem] * 11,
        out_specs=(any_space,) * 8,
        scratch_shapes=[
            pltpu.VMEM((depth, width), BF16),
            pltpu.VMEM((depth, width), BF16),
            pltpu.VMEM((2 * width, depth), BF16),
            pltpu.VMEM((2 * width, depth), BF16),
            pltpu.VMEM((2, 4, width, width), F32),
            dma,
        ],
        compiler_params=params,
        name="gram_rest",
    )(table, y_recv, yc_recv, *own_results)
    firsts, seconds = pieces[:4], pieces[4:]

    plane = [(a, b) for a in range(2) for b in range(2) if a or b]
    plane_in = [exchange(firsts[2 * a + b], a, 2 * b) for a, b in plane]
    line_in = [exchange(seconds[n], 2 * n, 0) for n in range(1, 4)]
    first = firsts[0] + sum(plane_in)
    second = seconds[0] + sum(line_in)
    line_in = [exchange(first[n], 2 * n, 0) for n in range(1, 4)]
    plane_in = [exchange(second[a, b], a, 2 * b) for a, b in plane]
    return jnp.concatenate([first[0] + sum(line_in), second[0, 0] + sum(plane_in)], axis=0)


def solution(mesh):
    in_specs = (P("blk", None, "tile"), P(), P(), P(), P("blk", None, None))
    out_specs = P("blk", "tile")
    paired = mesh.shape["blk"] == 8 and mesh.shape["tile"] == 4
    body = paired_body if paired else general_body
    return jax.shard_map(body, mesh=mesh, in_specs=in_specs, out_specs=out_specs, check_vma=False)
```

time: 432 us -> 113 us (0.26)
  waiting for transfers between devices: 320 us -> 50.7 us
  matrix products: 59.5 us -> 0 us
  Pallas kernels: 0 us -> 30.4 us
  local copies, waits for them, and re-layouts: 21.5 us -> 2.02 us
  starting transfers between devices: 7.86 us -> 26.3 us
  between operations: 13.5 us -> 0.68 us
  other arithmetic: 9.65 us -> 2.24 us
    all_gather x1 -> x0, waiting for transfers between devices: 119 us -> none  [body(): lax.all_gather(whitened_rows, 'tile', axis=1, tiled=True)]
    all_to_all x1, waiting for transfers between devices: 136 us -> 31.9 us  [paired_rest(): lax.all_to_all(factor_send, 'blk', split_axis=0, concat_axis=0, tiled=True)]
    reduce_scatter x1 -> x0, waiting for transfers between devices: 64.3 us -> none  [body(): lax.psum_scatter(partial_sums, 'blk', scatter_dimension=0, tiled=True)]
    dot_general x3 -> x0, matrix products: 59.5 us -> none  [the longest x1 34 us: body(): lax.dot_general(lax.all_gather(whitened_rows, 'tile', axis=1, tiled=True)...]
    pallas_call x0 -> x4, Pallas kernels: none -> 30.4 us  [the longest x1 11.8 us: paired_rest(): pl.pallas_call(gram_rest, out_shape=(shape(first_shape, F32),) * 4 + (sha...]
    ppermute x0 -> x16, starting transfers between devices: none -> 19 us  [exchange(): return lax.ppermute(value, axes, perm)]
    ppermute x0 -> x16, waiting for transfers between devices: none -> 18.8 us  [exchange(): return lax.ppermute(value, axes, perm)]
    gather x3 -> x0, local copies, waits for them, and re-layouts: 7.17 us -> none  [the longest x1 5.85 us: body(): own_blocks = jnp.take(arrived, positions, axis=0)]
  transfers between devices with their start and end apart: 3 -> 17, of which waited for: 3 -> 9; matrix products, arithmetic and copies ran while one was open for 0% -> 0% of each run, Pallas kernels for 0% -> 10%
where the time goes in v3:
time: 113 us
  waiting for transfers between devices  50.7 us (45%)
  Pallas kernels  30.4 us (27%)
  starting transfers between devices  26.3 us (23%)
  other arithmetic  2.24 us (2%)
  local copies, waits for them, and re-layouts  2.02 us (2%)
    all_to_all x1, waiting for transfers between devices, paired_rest(): lax.all_to_all(factor_send, 'blk', split_axis=0, concat_axis=0, tiled=True)  31.9 us
    ppermute x16, starting transfers between devices, exchange(): return lax.ppermute(value, axes, perm)  19 us
    ppermute x16, waiting for transfers between devices, exchange(): return lax.ppermute(value, axes, perm)  18.8 us
    pallas_call x1, Pallas kernels, paired_rest(): pl.pallas_call(gram_rest, out_shape=(shape(first_shape, F32),) * 4 + (sha...  11.8 us
    pallas_call x1, Pallas kernels, paired_body(): pl.pallas_call(plan, out_shape=(shape((half, max_order, width), F32), sha...  7.7 us
    pallas_call x1, Pallas kernels, paired_rest(): pl.pallas_call(gram_own, out_shape=(shape((half, 256, 256), BF16), shape(...  7.47 us
    all_to_all x1, starting transfers between devices, paired_rest(): lax.all_to_all(factor_send, 'blk', split_axis=0, concat_axis=0, tiled=True)  7.26 us
    pallas_call x1, Pallas kernels, paired_rest(): pl.pallas_call(pack_rows, out_shape=shape((row_count, CTW), F32), in_spec...  3.49 us
  transfers between devices with their start and end apart: 17, of which 9 were waited for; matrix products, arithmetic and copies ran while one was open for 0% of the time, Pallas kernels for 10%

profile of v3, /device:TPU:0, one launch (start us, length us, event | category | flops | bytes accessed | tf_op | source)
XLA Modules:
  0.0 112.6 jit_solution(7642810563794630919)
XLA Ops:
  0.0 0.7 compare_convert_fusion
  3.4 7.7 %plan.1 = (f32[6,384,256]{2,1,0:T(8,128)}, f32[8,384,128]{2,1,0:T(8,128)}, s32[9,12]{1,0:T(8,128)S(1)}, s32[1]{0:T(128)}) custom-call(s32[96]{0:T(128)S(1)} %copy-done.1, s32[4,96]{1,0:T(4,128)S(1)} %broadcast_multiply_fusion.1.weight_ref, s32[96]{0:T(128)S(1)} %copy-done.2, s32[8,96]{1,0:T(8,128)S(1)} %bitcast.44, f32[12,384,256]{2,1,0:T(8,128)} %blocks_ref.1, ...), custom_call_target="tpu_custom_call" | custom-call | tf_op jit(solution)/shard_map/plan/pallas_call | solution.py:351
  11.7 100.2 %conditional.1 = (f32[128,256]{1,0:T(8,128)S(1)}) conditional(s32[]{:T(128)} %bitcast.18, (s32[9,12]{1,0:T(8,128)S(1)}, f32[12,384,256]{2,1,0:T(8,128)}, f32[6,384,256]{2,1,0:T(8,128)}, f32[8,384,128]{2,1,0:T(8,128)}) %tuple.11, (s32[9,12]{1,0:T(8,128)S(1)}, f32[12,384,256]{2,1,0:T(8,128)}, f32[6,384,256]{2,1,0:T(8,128)}, ...), branch_computations={%region_1.2_spmd, %region_2.3_spmd} | conditional | flops 524288 | bytes 51511976 | solution.py:372
  11.8 7.3 %all-to-all-start = ((f32[8,384,128]{2,1,0:T(8,128)}), f32[8,384,128]{2,1,0:T(8,128)S(1)}, u32[]{:S(2)}, u32[]{:S(2)}) async-start(f32[8,384,128]{2,1,0:T(8,128)} %get-tuple-element.27), calls=%async_computation | async-start | bytes 3145728 | tf_op jit(solution)/shard_map/cond/branch_0_fun/all_to_all | solution.py:408
  19.0 3.5 %pack_rows.2 = f32[2880,128]{1,0:T(8,128)} custom-call(s32[9,12]{1,0:T(8,128)S(1)} %get-tuple-element.24.table_ref, f32[12,384,256]{2,1,0:T(8,128)} %get-tuple-element.25.blocks_ref), custom_call_target="tpu_custom_call" | custom-call | tf_op jit(solution)/shard_map/cond/branch_0_fun/pack_rows/pallas_call | solution.py:398
  22.5 1.6 %collective-permute-start = (f32[2880,128]{1,0:T(8,128)}, f32[2880,128]{1,0:T(8,128)S(1)}, u32[]{:S(2)}, u32[]{:S(2)}) collective-permute-start(f32[2880,128]{1,0:T(8,128)} %pack_rows.2), channel_id=1, source_target_pairs={{0,2},{1,3},{2,0},{3,1},{4,6},{5,7},{6,4},{7,5},{8,10},{9,11},{10,... | collective-permute-start | bytes 4423688 | tf_op jit(solution)/shard_map/cond/branch_0_fun/ppermute | solution.py:388
  24.1 31.9 %all-to-all-done.factor_ref = f32[8,384,128]{2,1,0:T(8,128)S(1)} async-done(((f32[8,384,128]{2,1,0:T(8,128)}), f32[8,384,128]{2,1,0:T(8,128)S(1)}, u32[]{:S(2)}, u32[]{:S(2)}) %all-to-all-start) | async-done | bytes 1572896 | tf_op jit(solution)/shard_map/cond/branch_0_fun/all_to_all | solution.py:408
  56.5 2.9 %collective-permute-done.3.factor_other = f32[8,384,128]{2,1,0:T(8,128)S(1)} collective-permute-done((f32[8,384,128]{2,1,0:T(8,128)S(1)}, f32[8,384,128]{2,1,0:T(8,128)S(1)}, u32[]{:S(2)}, u32[]{:S(2)}) %collective-permute-start.3) | collective-permute-done | bytes 1572896 | tf_op jit(solution)/shard_map/cond/branch_0_fun/ppermute | solution.py:388
  59.4 7.5 %gram_own.2 = (bf16[6,256,256]{2,1,0:T(8,128)(2,1)S(1)}, bf16[6,256,256]{2,1,0:T(8,128)(2,1)S(1)}, bf16[6,128,384]{2,1,0:T(8,128)(2,1)S(1)}, bf16[6,128,384]{2,1...) custom-call(s32[9,12]{1,0:T(8,128)S(1)} %get-tuple-element.24.table_, ...), custom_call_target="tpu_custom_call" | custom-call | tf_op jit(solution)/shard_map/cond/branch_0_fun/gram_own/pallas_call | solution.py:413
  66.9 11.8 %gram_rest.2 = (f32[4,88,256]{2,1,0:T(8,128)S(1)}, f32[4,88,256]{2,1,0:T(8,128)S(1)}, f32[4,88,256]{2,1,0:T(8,128)S(1)}, f32[4,88,256]{2,1,0:T(8,128)S(1)}, f32[...) custom-call(s32[9,12]{1,0:T(8,128)S(1)} %get-tuple-element.24.table_, ...), custom_call_target="tpu_custom_call" | custom-call | tf_op jit(solution)/shard_map/cond/branch_0_fun/gram_rest/pallas_call | solution.py:435
  78.8 2.6 %collective-permute-start.11 = (f32[2,2,40,256]{3,2,1,0:T(8,128)S(1)}, f32[2,2,40,256]{3,2,1,0:T(8,128)S(1)}, u32[]{:S(2)}, u32[]{:S(2)}) collective-permute-start(f32[2,2,40,256]{3,2,1,0:T(8,128)S(1)} %get-tuple-element.43), channel_id=1, source_target_pairs={{0,16},{1,17},{2,18},{3,19},{4,20},{5,21},{6,22},{7,23},{8,24},{9,... | collective-permute-start | bytes 491528 | tf_op jit(solution)/shard_map/cond/branch_0_fun/ppermute | solution.py:388
  81.4 1.8 %collective-permute-start.12 = (f32[2,2,40,256]{3,2,1,0:T(8,128)S(1)}, f32[2,2,40,256]{3,2,1,0:T(8,128)S(1)}, u32[]{:S(2)}, u32[]{:S(2)}) collective-permute-start(f32[2,2,40,256]{3,2,1,0:T(8,128)S(1)} %get-tuple-element.44), channel_id=1, source_target_pairs={{0,24},{1,25},{2,26},{3,27},{4,28},{5,29},{6,30},{7,31},{8,16},{9,... | collective-permute-start | bytes 491528 | tf_op jit(solution)/shard_map/cond/branch_0_fun/ppermute | solution.py:388
  83.2 1.5 %collective-permute-start.4 = (f32[4,88,256]{2,1,0:T(8,128)S(1)}, f32[4,88,256]{2,1,0:T(8,128)S(1)}, u32[]{:S(2)}, u32[]{:S(2)}) collective-permute-start(f32[4,88,256]{2,1,0:T(8,128)S(1)} %get-tuple-element.38), channel_id=1, source_target_pairs={{0,2},{1,3},{2,0},{3,1},{4,6},{5,7},{6,4},{7,5},{8,10},{9,11},{10,... | collective-permute-start | bytes 1081352 | tf_op jit(solution)/shard_map/cond/branch_0_fun/ppermute | solution.py:388
  84.7 1.4 %collective-permute-start.5 = (f32[4,88,256]{2,1,0:T(8,128)S(1)}, f32[4,88,256]{2,1,0:T(8,128)S(1)}, u32[]{:S(2)}, u32[]{:S(2)}) collective-permute-start(f32[4,88,256]{2,1,0:T(8,128)S(1)} %get-tuple-element.39), channel_id=1, source_target_pairs={{0,4},{1,5},{2,6},{3,7},{4,0},{5,1},{6,2},{7,3},{8,12},{9,13},{10,... | collective-permute-start | bytes 1081352 | tf_op jit(solution)/shard_map/cond/branch_0_fun/ppermute | solution.py:388
  86.1 1.7 %collective-permute-done.10 = f32[2,2,40,256]{3,2,1,0:T(8,128)S(1)} collective-permute-done((f32[2,2,40,256]{3,2,1,0:T(8,128)S(1)}, f32[2,2,40,256]{3,2,1,0:T(8,128)S(1)}, u32[]{:S(2)}, u32[]{:S(2)}) %collective-permute-start.10) | collective-permute-done | bytes 163872 | tf_op jit(solution)/shard_map/cond/branch_0_fun/ppermute | solution.py:388
  87.8 2.0 %collective-permute-start.6 = (f32[4,88,256]{2,1,0:T(8,128)S(1)}, f32[4,88,256]{2,1,0:T(8,128)S(1)}, u32[]{:S(2)}, u32[]{:S(2)}) collective-permute-start(f32[4,88,256]{2,1,0:T(8,128)S(1)} %get-tuple-element.40), channel_id=1, source_target_pairs={{0,6},{1,7},{2,4},{3,5},{4,2},{5,3},{6,0},{7,1},{8,14},{9,15},{10,... | collective-permute-start | bytes 1081352 | tf_op jit(solution)/shard_map/cond/branch_0_fun/ppermute | solution.py:388
  89.8 4.1 %collective-permute-done.11 = f32[2,2,40,256]{3,2,1,0:T(8,128)S(1)} collective-permute-done((f32[2,2,40,256]{3,2,1,0:T(8,128)S(1)}, f32[2,2,40,256]{3,2,1,0:T(8,128)S(1)}, u32[]{:S(2)}, u32[]{:S(2)}) %collective-permute-start.11) | collective-permute-done | bytes 163872 | tf_op jit(solution)/shard_map/cond/branch_0_fun/ppermute | solution.py:388
  93.9 1.6 %collective-permute-start.13 = (f32[40,256]{1,0:T(8,128)S(1)}, f32[40,256]{1,0:T(8,128)S(1)}, u32[]{:S(2)}, u32[]{:S(2)}) collective-permute-start(f32[40,256]{1,0:T(8,128)S(1)} %get-tuple-element.79), channel_id=1, source_target_pairs={{0,2},{1,3},{2,0},{3,1},{4,6},{5,7},{6,4},{7,5},{8,10},{9,11},{10,... | collective-permute-start | bytes 122888 | tf_op jit(solution)/shard_map/cond/branch_0_fun/ppermute | solution.py:388
  95.5 1.4 %collective-permute-start.14 = (f32[40,256]{1,0:T(8,128)S(1)}, f32[40,256]{1,0:T(8,128)S(1)}, u32[]{:S(2)}, u32[]{:S(2)}) collective-permute-start(f32[40,256]{1,0:T(8,128)S(1)} %get-tuple-element.77), channel_id=1, source_target_pairs={{0,4},{1,5},{2,6},{3,7},{4,0},{5,1},{6,2},{7,3},{8,12},{9,13},{10,... | collective-permute-start | bytes 122888 | tf_op jit(solution)/shard_map/cond/branch_0_fun/ppermute | solution.py:388
  97.5 5.1 %collective-permute-done.6 = f32[4,88,256]{2,1,0:T(8,128)S(1)} collective-permute-done((f32[4,88,256]{2,1,0:T(8,128)S(1)}, f32[4,88,256]{2,1,0:T(8,128)S(1)}, u32[]{:S(2)}, u32[]{:S(2)}) %collective-permute-start.6) | collective-permute-done | bytes 360480 | tf_op jit(solution)/shard_map/cond/branch_0_fun/ppermute | solution.py:388
  102.8 2.6 %collective-permute-start.8 = (f32[88,256]{1,0:T(8,128)S(1)}, f32[88,256]{1,0:T(8,128)S(1)}, u32[]{:S(2)}, u32[]{:S(2)}) collective-permute-start(f32[88,256]{1,0:T(8,128)S(1)} %get-tuple-element.74), channel_id=1, source_target_pairs={{0,16},{1,17},{2,18},{3,19},{4,20},{5,21},{6,22},{7,23},{8,24},{9,... | collective-permute-start | bytes 270344 | tf_op jit(solution)/shard_map/cond/branch_0_fun/ppermute | solution.py:388
  105.4 1.8 %collective-permute-start.9 = (f32[88,256]{1,0:T(8,128)S(1)}, f32[88,256]{1,0:T(8,128)S(1)}, u32[]{:S(2)}, u32[]{:S(2)}) collective-permute-start(f32[88,256]{1,0:T(8,128)S(1)} %get-tuple-element.75), channel_id=1, source_target_pairs={{0,24},{1,25},{2,26},{3,27},{4,28},{5,29},{6,30},{7,31},{8,16},{9,... | collective-permute-start | bytes 270344 | tf_op jit(solution)/shard_map/cond/branch_0_fun/ppermute | solution.py:388
  107.2 2.0 %collective-permute-done.7 = f32[88,256]{1,0:T(8,128)S(1)} collective-permute-done((f32[88,256]{1,0:T(8,128)S(1)}, f32[88,256]{1,0:T(8,128)S(1)}, u32[]{:S(2)}, u32[]{:S(2)}) %collective-permute-start.7) | collective-permute-done | bytes 90144 | tf_op jit(solution)/shard_map/cond/branch_0_fun/ppermute | solution.py:388
  109.8 1.9 %collective-permute-done.9 = f32[88,256]{1,0:T(8,128)S(1)} collective-permute-done((f32[88,256]{1,0:T(8,128)S(1)}, f32[88,256]{1,0:T(8,128)S(1)}, u32[]{:S(2)}, u32[]{:S(2)}) %collective-permute-start.9) | collective-permute-done | bytes 90144 | tf_op jit(solution)/shard_map/cond/branch_0_fun/ppermute | solution.py:388
  (33 shorter events, 5.4 us)
Async XLA Ops:
  1.4 0.7 copy-start
  2.1 0.7 copy-start.1
  2.7 0.7 copy-start.2
  11.8 44.3 %all-to-all-start = ((f32[8,384,128]{2,1,0:T(8,128)}), f32[8,384,128]{2,1,0:T(8,128)S(1)}, u32[]{:S(2)}, u32[]{:S(2)}) async-start(f32[8,384,128]{2,1,0:T(8,128)} %get-tuple-element.27), calls=%async_computation | async-start | bytes 3145728 | tf_op jit(solution)/shard_map/cond/branch_0_fun/all_to_all | solution.py:408
  22.5 34.0 %collective-permute-start = (f32[2880,128]{1,0:T(8,128)}, f32[2880,128]{1,0:T(8,128)S(1)}, u32[]{:S(2)}, u32[]{:S(2)}) collective-permute-start(f32[2880,128]{1,0:T(8,128)} %pack_rows.2), channel_id=1, source_target_pairs={{0,2},{1,3},{2,0},{3,1},{4,6},{5,7},{6,4},{7,5},{8,10},{9,11},{10,... | collective-permute-start | bytes 4423688 | tf_op jit(solution)/shard_map/cond/branch_0_fun/ppermute | solution.py:388
  24.1 32.4 %collective-permute-start.2 = (f32[6,384,256]{2,1,0:T(8,128)}, f32[6,384,256]{2,1,0:T(8,128)}, u32[]{:S(2)}, u32[]{:S(2)}) collective-permute-start(f32[6,384,256]{2,1,0:T(8,128)} %get-tuple-element.26.own_ref), channel_id=1, source_target_pairs={{0,1},{1,0},{2,3},{3,2},{4,5},{5,4},{6,7},{7,6},{8,9},{9,8},{10,11... | collective-permute-start | bytes 7077896 | tf_op jit(solution)/shard_map/cond/branch_0_fun/ppermute | solution.py:388
  56.0 3.4 %collective-permute-start.3 = (f32[8,384,128]{2,1,0:T(8,128)S(1)}, f32[8,384,128]{2,1,0:T(8,128)S(1)}, u32[]{:S(2)}, u32[]{:S(2)}) collective-permute-start(f32[8,384,128]{2,1,0:T(8,128)S(1)} %all-to-all-done.factor_ref), channel_id=1, source_target_pairs={{0,1},{1,0},{2,3},{3,2},{4,5},{5,4},{6,7},{7,6},{8,9},{9,8},{10,11... | collective-permute-start | bytes 4718600 | tf_op jit(solution)/shard_map/cond/branch_0_fun/ppermute | solution.py:388
  56.5 10.4 %collective-permute-start.1 = (f32[2880,128]{1,0:T(8,128)S(1)}, f32[2880,128]{1,0:T(8,128)S(1)}, u32[]{:S(2)}, u32[]{:S(2)}) collective-permute-start(f32[2880,128]{1,0:T(8,128)S(1)} %collective-permute-done.y_ref), channel_id=1, source_target_pairs={{0,1},{1,0},{2,3},{3,2},{4,5},{5,4},{6,7},{7,6},{8,9},{9,8},{10,11... | collective-permute-start | bytes 4423688 | tf_op jit(solution)/shard_map/cond/branch_0_fun/ppermute | solution.py:388
  78.7 9.1 %collective-permute-start.10 = (f32[2,2,40,256]{3,2,1,0:T(8,128)S(1)}, f32[2,2,40,256]{3,2,1,0:T(8,128)S(1)}, u32[]{:S(2)}, u32[]{:S(2)}) collective-permute-start(f32[2,2,40,256]{3,2,1,0:T(8,128)S(1)} %get-tuple-element.42), channel_id=1, source_target_pairs={{0,8},{1,9},{2,10},{3,11},{4,12},{5,13},{6,14},{7,15},{8,0},{9,1},... | collective-permute-start | bytes 491528 | tf_op jit(solution)/shard_map/cond/branch_0_fun/ppermute | solution.py:388
  78.8 15.1 %collective-permute-start.11 = (f32[2,2,40,256]{3,2,1,0:T(8,128)S(1)}, f32[2,2,40,256]{3,2,1,0:T(8,128)S(1)}, u32[]{:S(2)}, u32[]{:S(2)}) collective-permute-start(f32[2,2,40,256]{3,2,1,0:T(8,128)S(1)} %get-tuple-element.43), channel_id=1, source_target_pairs={{0,16},{1,17},{2,18},{3,19},{4,20},{5,21},{6,22},{7,23},{8,24},{9,... | collective-permute-start | bytes 491528 | tf_op jit(solution)/shard_map/cond/branch_0_fun/ppermute | solution.py:388
  81.4 12.5 %collective-permute-start.12 = (f32[2,2,40,256]{3,2,1,0:T(8,128)S(1)}, f32[2,2,40,256]{3,2,1,0:T(8,128)S(1)}, u32[]{:S(2)}, u32[]{:S(2)}) collective-permute-start(f32[2,2,40,256]{3,2,1,0:T(8,128)S(1)} %get-tuple-element.44), channel_id=1, source_target_pairs={{0,24},{1,25},{2,26},{3,27},{4,28},{5,29},{6,30},{7,31},{8,16},{9,... | collective-permute-start | bytes 491528 | tf_op jit(solution)/shard_map/cond/branch_0_fun/ppermute | solution.py:388
  83.2 13.8 %collective-permute-start.4 = (f32[4,88,256]{2,1,0:T(8,128)S(1)}, f32[4,88,256]{2,1,0:T(8,128)S(1)}, u32[]{:S(2)}, u32[]{:S(2)}) collective-permute-start(f32[4,88,256]{2,1,0:T(8,128)S(1)} %get-tuple-element.38), channel_id=1, source_target_pairs={{0,2},{1,3},{2,0},{3,1},{4,6},{5,7},{6,4},{7,5},{8,10},{9,11},{10,... | collective-permute-start | bytes 1081352 | tf_op jit(solution)/shard_map/cond/branch_0_fun/ppermute | solution.py:388
  84.7 12.8 %collective-permute-start.5 = (f32[4,88,256]{2,1,0:T(8,128)S(1)}, f32[4,88,256]{2,1,0:T(8,128)S(1)}, u32[]{:S(2)}, u32[]{:S(2)}) collective-permute-start(f32[4,88,256]{2,1,0:T(8,128)S(1)} %get-tuple-element.39), channel_id=1, source_target_pairs={{0,4},{1,5},{2,6},{3,7},{4,0},{5,1},{6,2},{7,3},{8,12},{9,13},{10,... | collective-permute-start | bytes 1081352 | tf_op jit(solution)/shard_map/cond/branch_0_fun/ppermute | solution.py:388
  87.8 14.8 %collective-permute-start.6 = (f32[4,88,256]{2,1,0:T(8,128)S(1)}, f32[4,88,256]{2,1,0:T(8,128)S(1)}, u32[]{:S(2)}, u32[]{:S(2)}) collective-permute-start(f32[4,88,256]{2,1,0:T(8,128)S(1)} %get-tuple-element.40), channel_id=1, source_target_pairs={{0,6},{1,7},{2,4},{3,5},{4,2},{5,3},{6,0},{7,1},{8,14},{9,15},{10,... | collective-permute-start | bytes 1081352 | tf_op jit(solution)/shard_map/cond/branch_0_fun/ppermute | solution.py:388
  93.9 11.4 %collective-permute-start.13 = (f32[40,256]{1,0:T(8,128)S(1)}, f32[40,256]{1,0:T(8,128)S(1)}, u32[]{:S(2)}, u32[]{:S(2)}) collective-permute-start(f32[40,256]{1,0:T(8,128)S(1)} %get-tuple-element.79), channel_id=1, source_target_pairs={{0,2},{1,3},{2,0},{3,1},{4,6},{5,7},{6,4},{7,5},{8,10},{9,11},{10,... | collective-permute-start | bytes 122888 | tf_op jit(solution)/shard_map/cond/branch_0_fun/ppermute | solution.py:388
  95.5 11.7 %collective-permute-start.14 = (f32[40,256]{1,0:T(8,128)S(1)}, f32[40,256]{1,0:T(8,128)S(1)}, u32[]{:S(2)}, u32[]{:S(2)}) collective-permute-start(f32[40,256]{1,0:T(8,128)S(1)} %get-tuple-element.77), channel_id=1, source_target_pairs={{0,4},{1,5},{2,6},{3,7},{4,0},{5,1},{6,2},{7,3},{8,12},{9,13},{10,... | collective-permute-start | bytes 122888 | tf_op jit(solution)/shard_map/cond/branch_0_fun/ppermute | solution.py:388
  97.0 10.2 %collective-permute-start.15 = (f32[40,256]{1,0:T(8,128)S(1)}, f32[40,256]{1,0:T(8,128)S(1)}, u32[]{:S(2)}, u32[]{:S(2)}) collective-permute-start(f32[40,256]{1,0:T(8,128)S(1)} %get-tuple-element.78), channel_id=1, source_target_pairs={{0,6},{1,7},{2,4},{3,5},{4,2},{5,3},{6,0},{7,1},{8,14},{9,15},{10,... | collective-permute-start | bytes 122888 | tf_op jit(solution)/shard_map/cond/branch_0_fun/ppermute | solution.py:388
  102.7 6.4 %collective-permute-start.7 = (f32[88,256]{1,0:T(8,128)S(1)}, f32[88,256]{1,0:T(8,128)S(1)}, u32[]{:S(2)}, u32[]{:S(2)}) collective-permute-start(f32[88,256]{1,0:T(8,128)S(1)} %get-tuple-element.76), channel_id=1, source_target_pairs={{0,8},{1,9},{2,10},{3,11},{4,12},{5,13},{6,14},{7,15},{8,0},{9,1},... | collective-permute-start | bytes 270344 | tf_op jit(solution)/shard_map/cond/branch_0_fun/ppermute | solution.py:388
  102.8 7.0 %collective-permute-start.8 = (f32[88,256]{1,0:T(8,128)S(1)}, f32[88,256]{1,0:T(8,128)S(1)}, u32[]{:S(2)}, u32[]{:S(2)}) collective-permute-start(f32[88,256]{1,0:T(8,128)S(1)} %get-tuple-element.74), channel_id=1, source_target_pairs={{0,16},{1,17},{2,18},{3,19},{4,20},{5,21},{6,22},{7,23},{8,24},{9,... | collective-permute-start | bytes 270344 | tf_op jit(solution)/shard_map/cond/branch_0_fun/ppermute | solution.py:388
  105.4 6.3 %collective-permute-start.9 = (f32[88,256]{1,0:T(8,128)S(1)}, f32[88,256]{1,0:T(8,128)S(1)}, u32[]{:S(2)}, u32[]{:S(2)}) collective-permute-start(f32[88,256]{1,0:T(8,128)S(1)} %get-tuple-element.75), channel_id=1, source_target_pairs={{0,24},{1,25},{2,26},{3,27},{4,28},{5,29},{6,30},{7,31},{8,16},{9,... | collective-permute-start | bytes 270344 | tf_op jit(solution)/shard_map/cond/branch_0_fun/ppermute | solution.py:388

commit v4 on v3

--- a/solution.py
+++ b/solution.py
@@ -80,9 +80,71 @@
     return [int(share * all_rows) // 8 * 8 for share in SHARES]
 
 
+TOP_ROWS = 32
+FACTOR_ROWS = 128 + 128 + 8 + TOP_ROWS
+
+
+def iotas(rows):
+    return tuple(lax.broadcasted_iota(jnp.int32, (rows, 128), axis) for axis in range(2))
+
+
+def fold_factor(c, tiles, top, out):
+    @pl.when(c == 0)
+    def _():
+        row, col = iotas(128)
+        t11 = tiles[2]
+        out[:128] = tiles[1]
+        out[128:256] = jnp.where(row >= col, tiles[0], t11.T)
+        out[256:264] = jnp.broadcast_to(jnp.sum(jnp.where(row == col, t11, 0.0), axis=0, keepdims=True), (8, 128))
+        out[264:] = top[...]
+
+    @pl.when(c == 1)
+    def _():
+        row, col = iotas(64)
+        t22 = tiles[2]
+        low = t22[64:]
+        out[: 128 - TOP_ROWS] = tiles[0, TOP_ROWS:]
+        out[128 - TOP_ROWS : 256 - TOP_ROWS] = tiles[1]
+        out[256 - TOP_ROWS : 320 - TOP_ROWS] = jnp.where(
+            col >= 64,
+            pltpu.roll(low, 64, 1),
+            jnp.where(row >= col, t22[:64], pltpu.roll(t22.T[64:], 64, 1)),
+        )
+        out[320 - TOP_ROWS :] = jnp.broadcast_to(
+            jnp.sum(jnp.where(row + 64 == col, low, 0.0), axis=0, keepdims=True), (8, 128)
+        )
+
+
+def unfold_factor(first, second):
+    row, col = iotas(128)
+    both = first[128:256]
+    f00 = jnp.where(row >= col, both, 0.0)
+    f11 = jnp.where(row > col, both.T, jnp.where(row == col, first[256:257], 0.0))
+    upper = jnp.concatenate(
+        [jnp.concatenate([f00, jnp.zeros_like(f00)], axis=1), jnp.concatenate([first[:128], f11], axis=1)], axis=0
+    )
+    f20 = jnp.concatenate([first[264:], second[: 128 - TOP_ROWS]], axis=0)
+    f21 = second[128 - TOP_ROWS : 256 - TOP_ROWS]
+    fold, diagonal = second[256 - TOP_ROWS : 320 - TOP_ROWS], second[320 - TOP_ROWS : 321 - TOP_ROWS]
+    turned = jnp.concatenate([fold, fold], axis=0).T[:64]
+    row, col = iotas(64)
+    f22 = jnp.concatenate(
+        [
+            jnp.where((row >= col) & (col < 64), fold, 0.0),
+            jnp.where(
+                col < 64,
+                pltpu.roll(fold, 64, 1),
+                jnp.where(row + 64 > col, pltpu.roll(turned, 64, 1), jnp.where(row + 64 == col, diagonal, 0.0)),
+            ),
+        ],
+        axis=0,
+    )
+    return upper, jnp.concatenate([f20, f21, f22], axis=1)
+
+
 def plan(
-    dest_ref, weight_ref, orders_ref, pattern_ref, blocks_ref, inv_ref, own_out, factor_out, table_ref, level_ref,
-    block_at, count, found_at, factor_at, sem,
+    dest_hbm, orders_hbm, pattern_hbm, blocks_ref, inv_ref, own_out, factor_out, table_ref, level_ref,
+    dest_ref, orders_ref, pattern_ref, orders_at, pattern_at, weight_at, weight_ref, block_at, count, found_at, factor_at, tiles_at, top_at, small_sem, factor_sem, sem,
 ):
     s = lax.axis_index("blk")
     t = lax.axis_index("tile")
@@ -91,14 +153,48 @@
     n_blk = count.shape[0]
     tiles = width // CTW
 
+    def small_loads():
+        for src, dst in (
+            (orders_hbm, orders_at), (pattern_hbm, pattern_at), (dest_hbm, dest_ref), (orders_hbm, orders_ref), (pattern_hbm, pattern_ref),
+        ):
+            yield pltpu.make_async_copy(src, dst, small_sem)
+
+    def factor_loads():
+        for row in range(slots):
+            for k, (ti, tj) in enumerate(((0, 0), (1, 0), (1, 1))):
+                ri, rj = jnp.where(c == 0, ti, 2), jnp.where(c == 0, tj, k)
+                yield pltpu.make_async_copy(
+                    inv_ref.at[row, pl.ds(pl.multiple_of(ri * 128, 128), 128), pl.ds(pl.multiple_of(rj * 128, 128), 128)],
+                    tiles_at.at[row, k],
+                    factor_sem,
+                )
+            yield pltpu.make_async_copy(
+                inv_ref.at[row, pl.ds(256, TOP_ROWS), pl.ds(0, 128)], top_at.at[row], factor_sem
+            )
+
+    for copy in small_loads():
+        copy.start()
+    for copy in factor_loads():
+        copy.start()
+    for copy in small_loads():
+        copy.wait()
+    ones = pattern_at[...]
+    counts = [sum(ones[q * tiles + e : q * tiles + e + 1] for e in range(tiles)) for q in range(4)]
+    rows = round8(orders_at[...])[None, :]
+    weight_at[...] = jnp.concatenate([rows * (counts[q] + counts[q + 1] * 65536) for q in (0, 2)], axis=0)
+    weights = pltpu.make_async_copy(weight_at, weight_ref, small_sem)
+    weights.start()
+    weights.wait()
+
     def scan_source(source, carry):
         found, most = carry
+        base = source * slots
         for o in range(n_blk):
             count[o] = 0
             block_at[0, o] = 0
             block_at[1, o] = 0
         for i in range(slots):
-            o = dest_ref[source * slots + i]
+            o = dest_ref[base + i]
             r = count[o]
             block_at[r, o] = i
             count[o] = r + 1
@@ -106,60 +202,38 @@
             found_at[jnp.where(mine, r, 2)] = found
             found = found + jnp.where(mine, 1, 0)
 
-        def place_pair(o, carry):
-            p, sent = carry[0], carry[1:]
+        def top(v):
+            return jnp.maximum(jnp.maximum(v[0] & 65535, v[0] >> 16), jnp.maximum(v[1] & 65535, v[1] >> 16))
+
+        here = source == s
+        p, low, high = jnp.int32(0), jnp.int32(0), jnp.int32(0)
+        for o in range(n_blk):
             on = count[o] > 0
             first, second = block_at[0, o], block_at[1, o]
-            w_first = [weight_ref[q, source * slots + first] for q in range(4)]
-            w_second = [weight_ref[q, source * slots + second] for q in range(4)]
-            straight = [sent[q] + (w_second[q] if q < 2 else w_first[q]) for q in range(4)]
-            crossed = [sent[q] + (w_first[q] if q < 2 else w_second[q]) for q in range(4)]
-
-            def top(v):
-                return jnp.maximum(jnp.maximum(v[0], v[1]), jnp.maximum(v[2], v[3]))
-
-            flip = jnp.where(top(crossed) < top(straight), 1, 0)
-
-            @pl.when(on & (o == s))
-            def _():
-                factor_at[source] = found_at[y ^ flip]
-
-            @pl.when(on & (source == s))
-            def _():
-                here, there = jnp.where((y ^ flip) == 0, first, second), jnp.where((y ^ flip) == 0, second, first)
-                table_ref[MINE, p] = here
-                table_ref[OTHERS, p] = there
-                table_ref[OWNER, p] = o
-
-            sent = [jnp.where(on, jnp.where(flip == 1, f, d), q) for f, d, q in zip(crossed, straight, sent)]
-            return (p + jnp.where(on, 1, 0), *sent)
-
+            straight = low + weight_ref[0, base + second], high + weight_ref[1, base + first]
+            crossed = low + weight_ref[0, base + first], high + weight_ref[1, base + second]
+            flip = top(crossed) < top(straight)
+            side = y ^ jnp.where(flip, 1, 0)
+            factor_at[jnp.where(on & (s == o), source, n_blk)] = found_at[side]
+            column = jnp.where(on & here, p, slots // 2)
+            table_ref[MINE, column] = jnp.where(side == 0, first, second)
+            table_ref[OTHERS, column] = jnp.where(side == 0, second, first)
+            table_ref[OWNER, column] = jnp.int32(o)
+            low = jnp.where(on, jnp.where(flip, crossed[0], straight[0]), low)
+            high = jnp.where(on, jnp.where(flip, crossed[1], straight[1]), high)
+            p = p + jnp.where(on, 1, 0)
+        return found, jnp.maximum(most, top((low, high)))
+
+    for source in range(n_blk):
         factor_at[source] = 0
-        zero = jnp.int32(0)
-        sent = lax.fori_loop(0, n_blk, place_pair, (zero,) * 5)[1:]
-        for q in sent:
-            most = jnp.maximum(most, q)
-        return found, most
-
+    found_at[0] = 0
+    found_at[1] = 0
     most = lax.fori_loop(0, n_blk, scan_source, (jnp.int32(0), jnp.int32(0)))[1]
-
-    def factor_loads():
-        for source in range(n_blk):
-            row = factor_at[source]
-            for k, (ti, tj) in enumerate(((0, 0), (1, 0), (1, 1))):
-                ri, rj = jnp.where(c == 0, ti, 2), jnp.where(c == 0, tj, k)
-                yield pltpu.make_async_copy(
-                    inv_ref.at[row, pl.ds(pl.multiple_of(ri * 128, 128), 128), pl.ds(pl.multiple_of(rj * 128, 128), 128)],
-                    factor_out.at[source, pl.ds(k * 128, 128), :],
-                    sem,
-                )
 
     def own_loads():
         for p in range(slots // 2):
             yield pltpu.make_async_copy(blocks_ref.at[table_ref[MINE, p]], own_out.at[p], sem)
 
-    for copy in factor_loads():
-        copy.start()
     for copy in own_loads():
         copy.start()
 
@@ -184,9 +258,16 @@
                 table_ref[ROW_AT + k, p * tiles + e] = at
                 at = at + jnp.where(tile_on(bits, (t ^ (2 + k)) * tiles + e), rows, 0)
 
+    for copy in factor_loads():
+        copy.wait()
+
+    def fold(source, carry):
+        row = factor_at[source]
+        fold_factor(c, tiles_at.at[row], top_at.at[row], factor_out.at[source])
+        return carry
+
+    lax.fori_loop(0, n_blk, fold, 0)
     for copy in own_loads():
-        copy.wait()
-    for copy in factor_loads():
         copy.wait()
 
 
@@ -250,14 +331,8 @@
     half, max_order, width = own_ref.shape
     for p in range(half):
         here, there = factor_ref[table_ref[OWNER, p]], factor_other[table_ref[OWNER, p]]
-        top, low = jnp.where(c == 0, here, there), jnp.where(c == 0, there, here)
-        f00, f10, f11 = top[:128], top[128:256], top[256:]
-        upper = split(
-            jnp.concatenate(
-                [jnp.concatenate([f00, jnp.zeros_like(f00)], axis=1), jnp.concatenate([f10, f11], axis=1)], axis=0
-            )
-        )
-        lower = split(jnp.concatenate([low[:128], low[128:256], low[256:]], axis=1))
+        upper, lower = unfold_factor(jnp.where(c == 0, here, there), jnp.where(c == 0, there, here))
+        upper, lower = split(upper), split(lower)
         upper_high[p], upper_low[p] = upper
         lower_high[p], lower_low[p] = lower
         tiles = [ref[p, :, e * CTW : (e + 1) * CTW] for ref in (own_ref, core_ref) for e in range(2)]
@@ -342,8 +417,7 @@
     tiles = width // CTW
     blocks = pltpu.with_memory_space_constraint(blocks, pltpu.HBM)
     inv_factor = pltpu.with_memory_space_constraint(inv_factor, pltpu.HBM)
-    pattern = pattern.T
-    weights = round8(orders)[None, :] * jnp.sum((pattern != 0).astype(jnp.int32).reshape(4, tiles, -1), axis=1)
+    dest, orders, pattern = (pltpu.with_memory_space_constraint(v, pltpu.HBM) for v in (dest, orders, pattern.T))
     hbm = pl.BlockSpec(memory_space=pltpu.HBM)
     smem = pl.BlockSpec(memory_space=pltpu.SMEM)
     vmem = pl.BlockSpec(memory_space=pltpu.VMEM)
@@ -352,22 +426,33 @@
         plan,
         out_shape=(
             shape((half, max_order, width), F32),
-            shape((n_blk, max_order, CTW), F32),
+            shape((n_blk, FACTOR_ROWS, CTW), F32),
             shape((9, half * tiles), jnp.int32),
             shape((1,), jnp.int32),
         ),
-        in_specs=[smem] * 4 + [hbm] * 2,
+        in_specs=[hbm] * 5,
         out_specs=(vmem, vmem, smem, smem),
         scratch_shapes=[
+            pltpu.SMEM(dest.shape, jnp.int32),
+            pltpu.SMEM(orders.shape, jnp.int32),
+            pltpu.SMEM(pattern.shape, jnp.int32),
+            pltpu.VMEM(orders.shape, jnp.int32),
+            pltpu.VMEM(pattern.shape, jnp.int32),
+            pltpu.VMEM((2, dest.shape[0]), jnp.int32),
+            pltpu.SMEM((2, dest.shape[0]), jnp.int32),
             pltpu.SMEM((2, n_blk), jnp.int32),
             pltpu.SMEM((n_blk,), jnp.int32),
             pltpu.SMEM((3,), jnp.int32),
-            pltpu.SMEM((n_blk,), jnp.int32),
+            pltpu.SMEM((n_blk + 1,), jnp.int32),
+            pltpu.VMEM((slots, 3, 128, 128), F32),
+            pltpu.VMEM((slots, TOP_ROWS, 128), F32),
+            pltpu.SemaphoreType.DMA,
+            pltpu.SemaphoreType.DMA,
             pltpu.SemaphoreType.DMA,
         ],
         compiler_params=pltpu.CompilerParams(vmem_limit_bytes=VMEM_LIMIT),
         name="plan",
-    )(dest, weights, orders, pattern, blocks, inv_factor)
+    )(dest, orders, pattern, blocks, inv_factor)
     rest = [functools.partial(paired_rest, rows) for rows in row_counts(half * tiles * max_order)]
     gram_tile = lax.switch(level[0], rest, table, blocks, own, factor_send)
     return gram_tile * (1.0 / (dest.shape[0] * max_order**0.5))
@@ -430,6 +515,7 @@
         name="gram_own",
     )(table, own, core_recv, factors, factors_other)
 
+    y_recv, own_results = lax.optimization_barrier((y_recv, own_results))
     yc_recv = exchange(y_recv, 0, 1)
     first_shape, second_shape = (4, XY_FIRST, width), (2, 2, 128 - XY_FIRST, width)
     pieces = pl.pallas_call(

time: 113 us -> 105 us (0.929)
  waiting for transfers between devices: 50.7 us -> 45.7 us
  local copies, waits for them, and re-layouts: 2.02 us -> 0.03 us
  other arithmetic: 2.24 us -> 0.86 us
    all_to_all x1, waiting for transfers between devices: 31.9 us -> 24.3 us  [paired_rest(): lax.all_to_all(factor_send, 'blk', split_axis=0, concat_axis=0, tiled=True)]
    ppermute x16, waiting for transfers between devices: 18.8 us -> 21.4 us  [exchange(): return lax.ppermute(value, axes, perm)]
    unnamed x6 -> x0, local copies, waits for them, and re-layouts: 1.99 us -> none
  transfers between devices with their start and end apart: 17 -> 17, of which waited for: 9 -> 9; matrix products, arithmetic and copies ran while one was open for 0% -> 0% of each run, Pallas kernels for 10% -> 11%
where the time goes in v4:
time: 105 us
  waiting for transfers between devices  45.7 us (44%)
  Pallas kernels  30.6 us (29%)
  starting transfers between devices  26.8 us (26%)
    all_to_all x1, waiting for transfers between devices, paired_rest(): lax.all_to_all(factor_send, 'blk', split_axis=0, concat_axis=0, tiled=True)  24.3 us
    ppermute x16, waiting for transfers between devices, exchange(): return lax.ppermute(value, axes, perm)  21.4 us
    ppermute x16, starting transfers between devices, exchange(): return lax.ppermute(value, axes, perm)  19.5 us
    pallas_call x1, Pallas kernels, paired_rest(): pl.pallas_call(gram_rest, out_shape=(shape(first_shape, F32),) * 4 + (sha...  11.8 us
    pallas_call x1, Pallas kernels, paired_rest(): pl.pallas_call(gram_own, out_shape=(shape((half, 256, 256), BF16), shape(...  7.67 us
    pallas_call x1, Pallas kernels, paired_body(): pl.pallas_call(plan, out_shape=(shape((half, max_order, width), F32), sha...  7.65 us
    all_to_all x1, starting transfers between devices, paired_rest(): lax.all_to_all(factor_send, 'blk', split_axis=0, concat_axis=0, tiled=True)  7.26 us
    pallas_call x1, Pallas kernels, paired_rest(): pl.pallas_call(pack_rows, out_shape=shape((row_count, CTW), F32), in_spec...  3.49 us
  transfers between devices with their start and end apart: 17, of which 9 were waited for; matrix products, arithmetic and copies ran while one was open for 0% of the time, Pallas kernels for 11%

profile of v4, /device:TPU:0, one launch (start us, length us, event | category | flops | bytes accessed | tf_op | source)
XLA Modules:
  0.0 104.9 jit_solution(7056024852028533227)
XLA Ops:
  0.0 7.7 %plan.1 = (f32[6,384,256]{2,1,0:T(8,128)}, f32[8,296,128]{2,1,0:T(8,128)}, s32[9,12]{1,0:T(8,128)S(1)}, s32[1]{0:T(128)}) custom-call(s32[96]{0:T(128)} %dest_hbm.1, s32[96]{0:T(128)} %orders_hbm.1, s32[8,96]{1,0:T(8,128)} %bitcast.42, f32[12,384,256]{2,1,0:T(8,128)} %blocks_ref.1, f32[12,384,384]{2,1,0:T(8,128)} %inv_ref.1), custom_call_target="tpu_custom_call" | custom-call | tf_op jit(solution)/shard_map/plan/pallas_call | solution.py:425
  8.3 95.9 %conditional.1 = (f32[128,256]{1,0:T(8,128)S(1)}) conditional(s32[]{:T(128)} %bitcast.17, (s32[9,12]{1,0:T(8,128)S(1)}, f32[12,384,256]{2,1,0:T(8,128)}, f32[6,384,256]{2,1,0:T(8,128)}, f32[8,296,128]{2,1,0:T(8,128)}) %tuple.13, (s32[9,12]{1,0:T(8,128)S(1)}, f32[12,384,256]{2,1,0:T(8,128)}, f32[6,384,256]{2,1,0:T(8,128)}, ...), branch_computations={%region_0.0_spmd, %region_1.0_spmd} | conditional | flops 524288 | bytes 48988840 | solution.py:457
  8.3 7.3 %all-to-all-start = ((f32[8,296,128]{2,1,0:T(8,128)}), f32[8,296,128]{2,1,0:T(8,128)S(1)}, u32[]{:S(2)}, u32[]{:S(2)}) async-start(f32[8,296,128]{2,1,0:T(8,128)} %get-tuple-element.27), calls=%async_computation | async-start | bytes 2424832 | tf_op jit(solution)/shard_map/cond/branch_0_fun/all_to_all | solution.py:493
  15.6 3.5 %pack_rows.2 = f32[2880,128]{1,0:T(8,128)} custom-call(s32[9,12]{1,0:T(8,128)S(1)} %get-tuple-element.24.table_ref, f32[12,384,256]{2,1,0:T(8,128)} %get-tuple-element.25.blocks_ref), custom_call_target="tpu_custom_call" | custom-call | tf_op jit(solution)/shard_map/cond/branch_0_fun/pack_rows/pallas_call | solution.py:483
  19.1 1.6 %collective-permute-start = (f32[2880,128]{1,0:T(8,128)}, f32[2880,128]{1,0:T(8,128)S(1)}, u32[]{:S(2)}, u32[]{:S(2)}) collective-permute-start(f32[2880,128]{1,0:T(8,128)} %pack_rows.2), channel_id=1, source_target_pairs={{0,2},{1,3},{2,0},{3,1},{4,6},{5,7},{6,4},{7,5},{8,10},{9,11},{10,... | collective-permute-start | bytes 4423688 | tf_op jit(solution)/shard_map/cond/branch_0_fun/ppermute | solution.py:473
  20.7 24.3 %all-to-all-done.factor_ref = f32[8,296,128]{2,1,0:T(8,128)S(1)} async-done(((f32[8,296,128]{2,1,0:T(8,128)}), f32[8,296,128]{2,1,0:T(8,128)S(1)}, u32[]{:S(2)}, u32[]{:S(2)}) %all-to-all-start) | async-done | bytes 1212448 | tf_op jit(solution)/shard_map/cond/branch_0_fun/all_to_all | solution.py:493
  45.0 2.9 %collective-permute-done.2.factor_other = f32[8,296,128]{2,1,0:T(8,128)S(1)} collective-permute-done((f32[8,296,128]{2,1,0:T(8,128)S(1)}, f32[8,296,128]{2,1,0:T(8,128)S(1)}, u32[]{:S(2)}, u32[]{:S(2)}) %collective-permute-start.2) | collective-permute-done | bytes 1212448 | tf_op jit(solution)/shard_map/cond/branch_0_fun/ppermute | solution.py:473
  47.9 7.7 %gram_own.2 = (bf16[6,256,256]{2,1,0:T(8,128)(2,1)S(1)}, bf16[6,256,256]{2,1,0:T(8,128)(2,1)S(1)}, bf16[6,128,384]{2,1,0:T(8,128)(2,1)S(1)}, bf16[6,128,384]{2,1...) custom-call(s32[9,12]{1,0:T(8,128)S(1)} %get-tuple-element.24.table_, ...), custom_call_target="tpu_custom_call" | custom-call | tf_op jit(solution)/shard_map/cond/branch_0_fun/gram_own/pallas_call | solution.py:498
  55.8 3.1 %collective-permute-done.3.yc_ref = f32[2880,128]{1,0:T(8,128)S(1)} collective-permute-done((f32[2880,128]{1,0:T(8,128)S(1)}, f32[2880,128]{1,0:T(8,128)S(1)}, u32[]{:S(2)}, u32[]{:S(2)}) %collective-permute-start.3) | collective-permute-done | bytes 1474592 | tf_op jit(solution)/shard_map/cond/branch_0_fun/ppermute | solution.py:473
  58.9 11.8 %gram_rest.2 = (f32[4,88,256]{2,1,0:T(8,128)S(1)}, f32[4,88,256]{2,1,0:T(8,128)S(1)}, f32[4,88,256]{2,1,0:T(8,128)S(1)}, f32[4,88,256]{2,1,0:T(8,128)S(1)}, f32[...) custom-call(s32[9,12]{1,0:T(8,128)S(1)} %get-tuple-element.24.table_, ...), custom_call_target="tpu_custom_call" | custom-call | tf_op jit(solution)/shard_map/cond/branch_0_fun/gram_rest/pallas_call | solution.py:521
  71.2 2.5 %collective-permute-start.11 = (f32[2,2,40,256]{3,2,1,0:T(8,128)S(1)}, f32[2,2,40,256]{3,2,1,0:T(8,128)S(1)}, u32[]{:S(2)}, u32[]{:S(2)}) collective-permute-start(f32[2,2,40,256]{3,2,1,0:T(8,128)S(1)} %get-tuple-element.53), channel_id=1, source_target_pairs={{0,16},{1,17},{2,18},{3,19},{4,20},{5,21},{6,22},{7,23},{8,24},{9,... | collective-permute-start | bytes 491528 | tf_op jit(solution)/shard_map/cond/branch_0_fun/ppermute | solution.py:473
  73.6 1.5 %collective-permute-start.12 = (f32[2,2,40,256]{3,2,1,0:T(8,128)S(1)}, f32[2,2,40,256]{3,2,1,0:T(8,128)S(1)}, u32[]{:S(2)}, u32[]{:S(2)}) collective-permute-start(f32[2,2,40,256]{3,2,1,0:T(8,128)S(1)} %get-tuple-element.54), channel_id=1, source_target_pairs={{0,24},{1,25},{2,26},{3,27},{4,28},{5,29},{6,30},{7,31},{8,16},{9,... | collective-permute-start | bytes 491528 | tf_op jit(solution)/shard_map/cond/branch_0_fun/ppermute | solution.py:473
  75.2 1.5 %collective-permute-start.4 = (f32[4,88,256]{2,1,0:T(8,128)S(1)}, f32[4,88,256]{2,1,0:T(8,128)S(1)}, u32[]{:S(2)}, u32[]{:S(2)}) collective-permute-start(f32[4,88,256]{2,1,0:T(8,128)S(1)} %get-tuple-element.48), channel_id=1, source_target_pairs={{0,2},{1,3},{2,0},{3,1},{4,6},{5,7},{6,4},{7,5},{8,10},{9,11},{10,... | collective-permute-start | bytes 1081352 | tf_op jit(solution)/shard_map/cond/branch_0_fun/ppermute | solution.py:473
  76.7 1.4 %collective-permute-start.5 = (f32[4,88,256]{2,1,0:T(8,128)S(1)}, f32[4,88,256]{2,1,0:T(8,128)S(1)}, u32[]{:S(2)}, u32[]{:S(2)}) collective-permute-start(f32[4,88,256]{2,1,0:T(8,128)S(1)} %get-tuple-element.49), channel_id=1, source_target_pairs={{0,4},{1,5},{2,6},{3,7},{4,0},{5,1},{6,2},{7,3},{8,12},{9,13},{10,... | collective-permute-start | bytes 1081352 | tf_op jit(solution)/shard_map/cond/branch_0_fun/ppermute | solution.py:473
  78.1 1.8 %collective-permute-done.10 = f32[2,2,40,256]{3,2,1,0:T(8,128)S(1)} collective-permute-done((f32[2,2,40,256]{3,2,1,0:T(8,128)S(1)}, f32[2,2,40,256]{3,2,1,0:T(8,128)S(1)}, u32[]{:S(2)}, u32[]{:S(2)}) %collective-permute-start.10) | collective-permute-done | bytes 163872 | tf_op jit(solution)/shard_map/cond/branch_0_fun/ppermute | solution.py:473
  79.9 2.3 %collective-permute-start.6 = (f32[4,88,256]{2,1,0:T(8,128)S(1)}, f32[4,88,256]{2,1,0:T(8,128)S(1)}, u32[]{:S(2)}, u32[]{:S(2)}) collective-permute-start(f32[4,88,256]{2,1,0:T(8,128)S(1)} %get-tuple-element.50), channel_id=1, source_target_pairs={{0,6},{1,7},{2,4},{3,5},{4,2},{5,3},{6,0},{7,1},{8,14},{9,15},{10,... | collective-permute-start | bytes 1081352 | tf_op jit(solution)/shard_map/cond/branch_0_fun/ppermute | solution.py:473
  82.2 4.0 %collective-permute-done.11 = f32[2,2,40,256]{3,2,1,0:T(8,128)S(1)} collective-permute-done((f32[2,2,40,256]{3,2,1,0:T(8,128)S(1)}, f32[2,2,40,256]{3,2,1,0:T(8,128)S(1)}, u32[]{:S(2)}, u32[]{:S(2)}) %collective-permute-start.11) | collective-permute-done | bytes 163872 | tf_op jit(solution)/shard_map/cond/branch_0_fun/ppermute | solution.py:473
  86.3 1.6 %collective-permute-start.13 = (f32[40,256]{1,0:T(8,128)S(1)}, f32[40,256]{1,0:T(8,128)S(1)}, u32[]{:S(2)}, u32[]{:S(2)}) collective-permute-start(f32[40,256]{1,0:T(8,128)S(1)} %get-tuple-element.99), channel_id=1, source_target_pairs={{0,2},{1,3},{2,0},{3,1},{4,6},{5,7},{6,4},{7,5},{8,10},{9,11},{10,... | collective-permute-start | bytes 122888 | tf_op jit(solution)/shard_map/cond/branch_0_fun/ppermute | solution.py:473
  87.9 1.5 %collective-permute-start.14 = (f32[40,256]{1,0:T(8,128)S(1)}, f32[40,256]{1,0:T(8,128)S(1)}, u32[]{:S(2)}, u32[]{:S(2)}) collective-permute-start(f32[40,256]{1,0:T(8,128)S(1)} %get-tuple-element.97), channel_id=1, source_target_pairs={{0,4},{1,5},{2,6},{3,7},{4,0},{5,1},{6,2},{7,3},{8,12},{9,13},{10,... | collective-permute-start | bytes 122888 | tf_op jit(solution)/shard_map/cond/branch_0_fun/ppermute | solution.py:473
  89.8 4.8 %collective-permute-done.6 = f32[4,88,256]{2,1,0:T(8,128)S(1)} collective-permute-done((f32[4,88,256]{2,1,0:T(8,128)S(1)}, f32[4,88,256]{2,1,0:T(8,128)S(1)}, u32[]{:S(2)}, u32[]{:S(2)}) %collective-permute-start.6) | collective-permute-done | bytes 360480 | tf_op jit(solution)/shard_map/cond/branch_0_fun/ppermute | solution.py:473
  94.8 2.9 %collective-permute-start.8 = (f32[88,256]{1,0:T(8,128)S(1)}, f32[88,256]{1,0:T(8,128)S(1)}, u32[]{:S(2)}, u32[]{:S(2)}) collective-permute-start(f32[88,256]{1,0:T(8,128)S(1)} %get-tuple-element.94), channel_id=1, source_target_pairs={{0,16},{1,17},{2,18},{3,19},{4,20},{5,21},{6,22},{7,23},{8,24},{9,... | collective-permute-start | bytes 270344 | tf_op jit(solution)/shard_map/cond/branch_0_fun/ppermute | solution.py:473
  97.7 1.5 %collective-permute-start.9 = (f32[88,256]{1,0:T(8,128)S(1)}, f32[88,256]{1,0:T(8,128)S(1)}, u32[]{:S(2)}, u32[]{:S(2)}) collective-permute-start(f32[88,256]{1,0:T(8,128)S(1)} %get-tuple-element.95), channel_id=1, source_target_pairs={{0,24},{1,25},{2,26},{3,27},{4,28},{5,29},{6,30},{7,31},{8,16},{9,... | collective-permute-start | bytes 270344 | tf_op jit(solution)/shard_map/cond/branch_0_fun/ppermute | solution.py:473
  99.2 1.7 %collective-permute-done.7 = f32[88,256]{1,0:T(8,128)S(1)} collective-permute-done((f32[88,256]{1,0:T(8,128)S(1)}, f32[88,256]{1,0:T(8,128)S(1)}, u32[]{:S(2)}, u32[]{:S(2)}) %collective-permute-start.7) | collective-permute-done | bytes 90144 | tf_op jit(solution)/shard_map/cond/branch_0_fun/ppermute | solution.py:473
  102.0 2.0 %collective-permute-done.9 = f32[88,256]{1,0:T(8,128)S(1)} collective-permute-done((f32[88,256]{1,0:T(8,128)S(1)}, f32[88,256]{1,0:T(8,128)S(1)}, u32[]{:S(2)}, u32[]{:S(2)}) %collective-permute-start.9) | collective-permute-done | bytes 90144 | tf_op jit(solution)/shard_map/cond/branch_0_fun/ppermute | solution.py:473
  (23 shorter events, 3.1 us)
Async XLA Ops:
  8.3 36.7 %all-to-all-start = ((f32[8,296,128]{2,1,0:T(8,128)}), f32[8,296,128]{2,1,0:T(8,128)S(1)}, u32[]{:S(2)}, u32[]{:S(2)}) async-start(f32[8,296,128]{2,1,0:T(8,128)} %get-tuple-element.27), calls=%async_computation | async-start | bytes 2424832 | tf_op jit(solution)/shard_map/cond/branch_0_fun/all_to_all | solution.py:493
  15.6 29.4 %collective-permute-start.1 = (f32[6,384,256]{2,1,0:T(8,128)}, f32[6,384,256]{2,1,0:T(8,128)}, u32[]{:S(2)}, u32[]{:S(2)}) collective-permute-start(f32[6,384,256]{2,1,0:T(8,128)} %get-tuple-element.26.own_ref), channel_id=1, source_target_pairs={{0,1},{1,0},{2,3},{3,2},{4,5},{5,4},{6,7},{7,6},{8,9},{9,8},{10,11... | collective-permute-start | bytes 7077896 | tf_op jit(solution)/shard_map/cond/branch_0_fun/ppermute | solution.py:473
  19.1 36.5 %collective-permute-start = (f32[2880,128]{1,0:T(8,128)}, f32[2880,128]{1,0:T(8,128)S(1)}, u32[]{:S(2)}, u32[]{:S(2)}) collective-permute-start(f32[2880,128]{1,0:T(8,128)} %pack_rows.2), channel_id=1, source_target_pairs={{0,2},{1,3},{2,0},{3,1},{4,6},{5,7},{6,4},{7,5},{8,10},{9,11},{10,... | collective-permute-start | bytes 4423688 | tf_op jit(solution)/shard_map/cond/branch_0_fun/ppermute | solution.py:473
  45.0 2.9 %collective-permute-start.2 = (f32[8,296,128]{2,1,0:T(8,128)S(1)}, f32[8,296,128]{2,1,0:T(8,128)S(1)}, u32[]{:S(2)}, u32[]{:S(2)}) collective-permute-start(f32[8,296,128]{2,1,0:T(8,128)S(1)} %all-to-all-done.factor_ref), channel_id=1, source_target_pairs={{0,1},{1,0},{2,3},{3,2},{4,5},{5,4},{6,7},{7,6},{8,9},{9,8},{10,11... | collective-permute-start | bytes 3637256 | tf_op jit(solution)/shard_map/cond/branch_0_fun/ppermute | solution.py:473
  55.6 3.3 %collective-permute-start.3 = (f32[2880,128]{1,0:T(8,128)S(1)}, f32[2880,128]{1,0:T(8,128)S(1)}, u32[]{:S(2)}, u32[]{:S(2)}) collective-permute-start(f32[2880,128]{1,0:T(8,128)S(1)} %collective-permute-done.y_ref), channel_id=1, source_target_pairs={{0,1},{1,0},{2,3},{3,2},{4,5},{5,4},{6,7},{7,6},{8,9},{9,8},{10,11... | collective-permute-start | bytes 4423688 | tf_op jit(solution)/shard_map/cond/branch_0_fun/ppermute | solution.py:473
  70.7 9.2 %collective-permute-start.10 = (f32[2,2,40,256]{3,2,1,0:T(8,128)S(1)}, f32[2,2,40,256]{3,2,1,0:T(8,128)S(1)}, u32[]{:S(2)}, u32[]{:S(2)}) collective-permute-start(f32[2,2,40,256]{3,2,1,0:T(8,128)S(1)} %get-tuple-element.52), channel_id=1, source_target_pairs={{0,8},{1,9},{2,10},{3,11},{4,12},{5,13},{6,14},{7,15},{8,0},{9,1},... | collective-permute-start | bytes 491528 | tf_op jit(solution)/shard_map/cond/branch_0_fun/ppermute | solution.py:473
  71.2 15.0 %collective-permute-start.11 = (f32[2,2,40,256]{3,2,1,0:T(8,128)S(1)}, f32[2,2,40,256]{3,2,1,0:T(8,128)S(1)}, u32[]{:S(2)}, u32[]{:S(2)}) collective-permute-start(f32[2,2,40,256]{3,2,1,0:T(8,128)S(1)} %get-tuple-element.53), channel_id=1, source_target_pairs={{0,16},{1,17},{2,18},{3,19},{4,20},{5,21},{6,22},{7,23},{8,24},{9,... | collective-permute-start | bytes 491528 | tf_op jit(solution)/shard_map/cond/branch_0_fun/ppermute | solution.py:473
  73.6 12.6 %collective-permute-start.12 = (f32[2,2,40,256]{3,2,1,0:T(8,128)S(1)}, f32[2,2,40,256]{3,2,1,0:T(8,128)S(1)}, u32[]{:S(2)}, u32[]{:S(2)}) collective-permute-start(f32[2,2,40,256]{3,2,1,0:T(8,128)S(1)} %get-tuple-element.54), channel_id=1, source_target_pairs={{0,24},{1,25},{2,26},{3,27},{4,28},{5,29},{6,30},{7,31},{8,16},{9,... | collective-permute-start | bytes 491528 | tf_op jit(solution)/shard_map/cond/branch_0_fun/ppermute | solution.py:473
  75.2 14.2 %collective-permute-start.4 = (f32[4,88,256]{2,1,0:T(8,128)S(1)}, f32[4,88,256]{2,1,0:T(8,128)S(1)}, u32[]{:S(2)}, u32[]{:S(2)}) collective-permute-start(f32[4,88,256]{2,1,0:T(8,128)S(1)} %get-tuple-element.48), channel_id=1, source_target_pairs={{0,2},{1,3},{2,0},{3,1},{4,6},{5,7},{6,4},{7,5},{8,10},{9,11},{10,... | collective-permute-start | bytes 1081352 | tf_op jit(solution)/shard_map/cond/branch_0_fun/ppermute | solution.py:473
  76.7 13.2 %collective-permute-start.5 = (f32[4,88,256]{2,1,0:T(8,128)S(1)}, f32[4,88,256]{2,1,0:T(8,128)S(1)}, u32[]{:S(2)}, u32[]{:S(2)}) collective-permute-start(f32[4,88,256]{2,1,0:T(8,128)S(1)} %get-tuple-element.49), channel_id=1, source_target_pairs={{0,4},{1,5},{2,6},{3,7},{4,0},{5,1},{6,2},{7,3},{8,12},{9,13},{10,... | collective-permute-start | bytes 1081352 | tf_op jit(solution)/shard_map/cond/branch_0_fun/ppermute | solution.py:473
  79.9 14.7 %collective-permute-start.6 = (f32[4,88,256]{2,1,0:T(8,128)S(1)}, f32[4,88,256]{2,1,0:T(8,128)S(1)}, u32[]{:S(2)}, u32[]{:S(2)}) collective-permute-start(f32[4,88,256]{2,1,0:T(8,128)S(1)} %get-tuple-element.50), channel_id=1, source_target_pairs={{0,6},{1,7},{2,4},{3,5},{4,2},{5,3},{6,0},{7,1},{8,14},{9,15},{10,... | collective-permute-start | bytes 1081352 | tf_op jit(solution)/shard_map/cond/branch_0_fun/ppermute | solution.py:473
  86.3 11.4 %collective-permute-start.13 = (f32[40,256]{1,0:T(8,128)S(1)}, f32[40,256]{1,0:T(8,128)S(1)}, u32[]{:S(2)}, u32[]{:S(2)}) collective-permute-start(f32[40,256]{1,0:T(8,128)S(1)} %get-tuple-element.99), channel_id=1, source_target_pairs={{0,2},{1,3},{2,0},{3,1},{4,6},{5,7},{6,4},{7,5},{8,10},{9,11},{10,... | collective-permute-start | bytes 122888 | tf_op jit(solution)/shard_map/cond/branch_0_fun/ppermute | solution.py:473
  87.9 11.3 %collective-permute-start.14 = (f32[40,256]{1,0:T(8,128)S(1)}, f32[40,256]{1,0:T(8,128)S(1)}, u32[]{:S(2)}, u32[]{:S(2)}) collective-permute-start(f32[40,256]{1,0:T(8,128)S(1)} %get-tuple-element.97), channel_id=1, source_target_pairs={{0,4},{1,5},{2,6},{3,7},{4,0},{5,1},{6,2},{7,3},{8,12},{9,13},{10,... | collective-permute-start | bytes 122888 | tf_op jit(solution)/shard_map/cond/branch_0_fun/ppermute | solution.py:473
  89.4 9.8 %collective-permute-start.15 = (f32[40,256]{1,0:T(8,128)S(1)}, f32[40,256]{1,0:T(8,128)S(1)}, u32[]{:S(2)}, u32[]{:S(2)}) collective-permute-start(f32[40,256]{1,0:T(8,128)S(1)} %get-tuple-element.98), channel_id=1, source_target_pairs={{0,6},{1,7},{2,4},{3,5},{4,2},{5,3},{6,0},{7,1},{8,14},{9,15},{10,... | collective-permute-start | bytes 122888 | tf_op jit(solution)/shard_map/cond/branch_0_fun/ppermute | solution.py:473
  94.7 6.2 %collective-permute-start.7 = (f32[88,256]{1,0:T(8,128)S(1)}, f32[88,256]{1,0:T(8,128)S(1)}, u32[]{:S(2)}, u32[]{:S(2)}) collective-permute-start(f32[88,256]{1,0:T(8,128)S(1)} %get-tuple-element.96), channel_id=1, source_target_pairs={{0,8},{1,9},{2,10},{3,11},{4,12},{5,13},{6,14},{7,15},{8,0},{9,1},... | collective-permute-start | bytes 270344 | tf_op jit(solution)/shard_map/cond/branch_0_fun/ppermute | solution.py:473
  94.8 7.2 %collective-permute-start.8 = (f32[88,256]{1,0:T(8,128)S(1)}, f32[88,256]{1,0:T(8,128)S(1)}, u32[]{:S(2)}, u32[]{:S(2)}) collective-permute-start(f32[88,256]{1,0:T(8,128)S(1)} %get-tuple-element.94), channel_id=1, source_target_pairs={{0,16},{1,17},{2,18},{3,19},{4,20},{5,21},{6,22},{7,23},{8,24},{9,... | collective-permute-start | bytes 270344 | tf_op jit(solution)/shard_map/cond/branch_0_fun/ppermute | solution.py:473
  97.7 6.3 %collective-permute-start.9 = (f32[88,256]{1,0:T(8,128)S(1)}, f32[88,256]{1,0:T(8,128)S(1)}, u32[]{:S(2)}, u32[]{:S(2)}) collective-permute-start(f32[88,256]{1,0:T(8,128)S(1)} %get-tuple-element.95), channel_id=1, source_target_pairs={{0,24},{1,25},{2,26},{3,27},{4,28},{5,29},{6,30},{7,31},{8,16},{9,... | collective-permute-start | bytes 270344 | tf_op jit(solution)/shard_map/cond/branch_0_fun/ppermute | solution.py:473

commit v5 on v4

--- a/solution.py
+++ b/solution.py
@@ -10,7 +10,7 @@
 CTW = 128
 F32 = jnp.float32
 BF16 = jnp.bfloat16
-XY_FIRST = 88
+XY_FIRST = 80
 VMEM_LIMIT = 32 << 20
 
 
@@ -312,19 +312,19 @@
 
 
 def whiten(tiles, table_ref, p, upper, lower, tile_ids):
-    row_on = lax.broadcasted_iota(jnp.int32, tiles[0].shape, 0) < table_ref[ORDER, p]
+    order = table_ref[ORDER, p]
+    row_on = lax.broadcasted_iota(jnp.int32, tiles[0].shape, 0) < order
     parts = [
         jnp.where(row_on & tile_on(table_ref[BITS, p], ct), tile, 0.0) for tile, ct in zip(tiles, tile_ids)
     ]
     x = split(jnp.concatenate(parts, axis=1))
     w = jnp.concatenate([dot3(upper, (x[0][:256], x[1][:256])), dot3(lower, x)], axis=0)
-    return [jnp.where(row_on, w[:, i * CTW : (i + 1) * CTW], 0.0) for i in range(len(tiles))]
+    return jnp.where(lax.broadcasted_iota(jnp.int32, w.shape, 0) < order, w, 0.0)
 
 
 def gram_own(
     table_ref, own_ref, core_ref, factor_ref, factor_other,
-    upper_high, upper_low, lower_high, lower_low, w0_high, w0_low, w1t_high, w1t_low, g_out,
-    w0t_high, w0t_low,
+    upper_high, upper_low, lower_high, lower_low, w0_high, w0_low, w1t_high, w1t_low, g_out, w0t_high, w0t_low,
 ):
     t = lax.axis_index("tile")
     c = t % 2
@@ -339,75 +339,75 @@
         tile_ids = [(t ^ m) * 2 + e for m in range(2) for e in range(2)]
         w = whiten(tiles, table_ref, p, upper, lower, tile_ids)
         rows = pl.ds(p * max_order, max_order)
-        w0, w1 = jnp.concatenate(w[:2], axis=1), jnp.concatenate(w[2:], axis=1)
-        w0_high[rows, :], w0_low[rows, :] = split(w0)
-        w0t_high[:, rows], w0t_low[:, rows] = split(w0.T)
-        w1t_high[:, rows], w1t_low[:, rows] = split(w1.T)
+        w0_high[rows, :], w0_low[rows, :] = split(w[:, :width])
+        w0t_high[:, rows], w0t_low[:, rows] = split(w[:, :width].T)
+        w1t_high[:, rows], w1t_low[:, rows] = split(w[:, width:].T)
     w0 = w0_high[...], w0_low[...]
-    g_out[0] = dot3((w0t_high[...], w0t_low[...]), w0)
-    g_out[1] = dot3((w1t_high[...], w1t_low[...]), w0)
+    g_out[:width] = dot3((w0t_high[...], w0t_low[...]), w0)
+    g_out[width:] = dot3((w1t_high[...], w1t_low[...]), w0)
+
+
+def across(table_ref, rows_ref, group, p, upper_high, upper_low, lower_high, lower_low, max_order):
+    t = lax.axis_index("tile")
+    last = rows_ref.shape[0] - max_order
+    tiles = []
+    for e in range(2):
+        at = pl.multiple_of(jnp.minimum(table_ref[ROW_AT + group - 2, p * 2 + e], last), 8)
+        tiles.append(rows_ref[pl.ds(at, max_order), :])
+    upper, lower = (upper_high[p], upper_low[p]), (lower_high[p], lower_low[p])
+    return whiten(tiles, table_ref, p, upper, lower, [(t ^ group) * 2 + e for e in range(2)])
+
+
+def gram_y(
+    table_ref, y_ref, upper_high, upper_low, lower_high, lower_low, w0_high, w0_low, w1t_high, w1t_low,
+    w2_high, w2_low, g_out, w2t_high, w2t_low,
+):
+    depth, width = w0_high.shape
+    half = upper_high.shape[0]
+    max_order = depth // half
+    for p in range(half):
+        w = across(table_ref, y_ref, 2, p, upper_high, upper_low, lower_high, lower_low, max_order)
+        rows = pl.ds(p * max_order, max_order)
+        w2_high[rows, :], w2_low[rows, :] = split(w)
+        w2t_high[:, rows], w2t_low[:, rows] = split(w.T)
+    w2, w2t = (w2_high[...], w2_low[...]), (w2t_high[...], w2t_low[...])
+    g_out[:width] = dot3(w2t, (w0_high[...], w0_low[...]))
+    g_out[width : 2 * width] = dot3((w1t_high[...], w1t_low[...]), w2)
+    g_out[2 * width :] = dot3(w2t, w2)
 
 
 def gram_rest(
-    table_ref, y_ref, yc_ref,
-    upper_high, upper_low, lower_high, lower_low, w0_high, w0_low, w1t_high, w1t_low, g_own,
-    *refs,
+    table_ref, yc_ref, upper_high, upper_low, lower_high, lower_low, w0_high, w0_low, w2_high, w2_low, g_own, g_y, *refs
 ):
     firsts, seconds = refs[:4], refs[4:8]
-    w2_high, w2_low, w23t_high, w23t_low, gram, out_sem = refs[8:]
+    w3t_high, w3t_low, gram = refs[8:]
     s = lax.axis_index("blk")
     t = lax.axis_index("tile")
+    depth, width = w0_high.shape
     half = upper_high.shape[0]
-    depth, width = w0_high.shape
     max_order = depth // half
-    last = y_ref.shape[0] - max_order
     for p in range(half):
-        tiles = []
-        for k, ref in enumerate((y_ref, yc_ref)):
-            for e in range(2):
-                at = pl.multiple_of(jnp.minimum(table_ref[ROW_AT + k, p * 2 + e], last), 8)
-                tiles.append(ref[pl.ds(at, max_order), :])
-        tile_ids = [(t ^ (2 + k)) * 2 + e for k in range(2) for e in range(2)]
-        upper, lower = (upper_high[p], upper_low[p]), (lower_high[p], lower_low[p])
-        w = whiten(tiles, table_ref, p, upper, lower, tile_ids)
+        w = across(table_ref, yc_ref, 3, p, upper_high, upper_low, lower_high, lower_low, max_order)
         rows = pl.ds(p * max_order, max_order)
-        w2_high[rows, :], w2_low[rows, :] = split(jnp.concatenate(w[:2], axis=1))
-        w23t_high[:, rows], w23t_low[:, rows] = split(jnp.concatenate(w, axis=1).T)
-
-    w0, w2 = (w0_high[...], w0_low[...]), (w2_high[...], w2_low[...])
-    w1t, w23t = (w1t_high[...], w1t_low[...]), (w23t_high[...], w23t_low[...])
-    gram[0, 0] = g_own[0]
-    gram[0, 1] = g_own[1]
-    g = dot3(w23t, w0)
-    gram[0, 2] = g[:width]
-    gram[0, 3] = g[width:]
-    gram[1, 0] = g[:width].T
-    gram[1, 1] = dot3(w1t, w2)
-    g = dot3(w23t, w2)
-    gram[1, 2] = g[:width]
-    gram[1, 3] = g[width:]
+        w3t_high[:, rows], w3t_low[:, rows] = split(w.T)
+    w3t = w3t_high[...], w3t_low[...]
+    for m in range(2):
+        gram[0, m] = g_own[m * width : (m + 1) * width]
+    gram[0, 2] = g_y[:width]
+    gram[0, 3] = dot3(w3t, (w0_high[...], w0_low[...]))
+    gram[1, 0] = g_y[:width].T
+    for m in range(1, 3):
+        gram[1, m] = g_y[m * width : (m + 1) * width]
+    gram[1, 3] = dot3(w3t, (w2_high[...], w2_low[...]))
 
     z, x = s // 2, s % 2
 
-    def stores():
-        for n in range(4):
-            for a in range(2):
-                for b in range(2):
-                    m, at = (z ^ n) ^ t, (x ^ a) * 128
-                    first, second = firsts[2 * a + b], seconds[n]
-                    yield pltpu.make_async_copy(
-                        gram.at[b, m, pl.ds(pl.multiple_of(at, 8), XY_FIRST), :], first.at[n], out_sem
-                    )
-                    yield pltpu.make_async_copy(
-                        gram.at[b, m, pl.ds(pl.multiple_of(at + XY_FIRST, 8), 128 - XY_FIRST), :],
-                        second.at[a, b],
-                        out_sem,
-                    )
-
-    for copy in stores():
-        copy.start()
-    for copy in stores():
-        copy.wait()
+    for n in range(4):
+        for a in range(2):
+            for b in range(2):
+                m, at = (z ^ n) ^ t, (x ^ a) * 128
+                firsts[2 * a + b][n] = gram[b, m, pl.ds(pl.multiple_of(at, 8), XY_FIRST), :]
+                seconds[n][a, b] = gram[b, m, pl.ds(pl.multiple_of(at + XY_FIRST, 8), 128 - XY_FIRST), :]
 
 
 def paired_body(blocks, orders, pattern, dest, inv_factor):
@@ -454,8 +454,7 @@
         name="plan",
     )(dest, orders, pattern, blocks, inv_factor)
     rest = [functools.partial(paired_rest, rows) for rows in row_counts(half * tiles * max_order)]
-    gram_tile = lax.switch(level[0], rest, table, blocks, own, factor_send)
-    return gram_tile * (1.0 / (dest.shape[0] * max_order**0.5))
+    return lax.switch(level[0], rest, table, blocks, own, factor_send)
 
 
 def paired_rest(row_count, table, blocks, own, factor_send):
@@ -475,7 +474,6 @@
     hbm = pl.BlockSpec(memory_space=pltpu.HBM)
     smem = pl.BlockSpec(memory_space=pltpu.SMEM)
     vmem = pl.BlockSpec(memory_space=pltpu.VMEM)
-    any_space = pl.BlockSpec(memory_space=pl.ANY)
     shape = jax.ShapeDtypeStruct
     params = pltpu.CompilerParams(vmem_limit_bytes=VMEM_LIMIT)
     dma = pltpu.SemaphoreType.DMA
@@ -495,7 +493,7 @@
     factors_other = exchange(factors, 0, 1)
 
     depth = half * max_order
-    own_results = pl.pallas_call(
+    *factor, w0_high, w0_low, w1t_high, w1t_low, g_own = pl.pallas_call(
         gram_own,
         out_shape=(
             shape((half, 256, 256), BF16),
@@ -506,7 +504,7 @@
             shape((depth, width), BF16),
             shape((width, depth), BF16),
             shape((width, depth), BF16),
-            shape((2, width, width), F32),
+            shape((2 * width, width), F32),
         ),
         in_specs=[smem] + [vmem] * 4,
         out_specs=(vmem,) * 9,
@@ -515,25 +513,31 @@
         name="gram_own",
     )(table, own, core_recv, factors, factors_other)
 
-    y_recv, own_results = lax.optimization_barrier((y_recv, own_results))
+    y_recv, g_own = lax.optimization_barrier((y_recv, g_own))
     yc_recv = exchange(y_recv, 0, 1)
+    w2_high, w2_low, g_y = pl.pallas_call(
+        gram_y,
+        out_shape=(shape((depth, width), BF16), shape((depth, width), BF16), shape((3 * width, width), F32)),
+        in_specs=[smem] + [vmem] * 9,
+        out_specs=(vmem,) * 3,
+        scratch_shapes=[pltpu.VMEM((width, depth), BF16), pltpu.VMEM((width, depth), BF16)],
+        compiler_params=params,
+        name="gram_y",
+    )(table, y_recv, *factor, w0_high, w0_low, w1t_high, w1t_low)
     first_shape, second_shape = (4, XY_FIRST, width), (2, 2, 128 - XY_FIRST, width)
     pieces = pl.pallas_call(
         gram_rest,
         out_shape=(shape(first_shape, F32),) * 4 + (shape(second_shape, F32),) * 4,
         in_specs=[smem] + [vmem] * 11,
-        out_specs=(any_space,) * 8,
+        out_specs=(vmem,) * 8,
         scratch_shapes=[
-            pltpu.VMEM((depth, width), BF16),
-            pltpu.VMEM((depth, width), BF16),
-            pltpu.VMEM((2 * width, depth), BF16),
-            pltpu.VMEM((2 * width, depth), BF16),
+            pltpu.VMEM((width, depth), BF16),
+            pltpu.VMEM((width, depth), BF16),
             pltpu.VMEM((2, 4, width, width), F32),
-            dma,
         ],
         compiler_params=params,
         name="gram_rest",
-    )(table, y_recv, yc_recv, *own_results)
+    )(table, yc_recv, *factor, w0_high, w0_low, w2_high, w2_low, g_own, g_y)
     firsts, seconds = pieces[:4], pieces[4:]
 
     plane = [(a, b) for a in range(2) for b in range(2) if a or b]
@@ -543,7 +547,8 @@
     second = seconds[0] + sum(line_in)
     line_in = [exchange(first[n], 2 * n, 0) for n in range(1, 4)]
     plane_in = [exchange(second[a, b], a, 2 * b) for a, b in plane]
-    return jnp.concatenate([first[0] + sum(line_in), second[0, 0] + sum(plane_in)], axis=0)
+    gram_tile = jnp.concatenate([first[0] + sum(line_in), second[0, 0] + sum(plane_in)], axis=0)
+    return gram_tile * (1.0 / (n_blk * slots * max_order**0.5))
 
 
 def solution(mesh):

time: 105 us -> 101 us (0.962)
  waiting for transfers between devices: 45.7 us -> 41.6 us
  Pallas kernels: 30.6 us -> 29.4 us
    pallas_call x1, Pallas kernels: 11.8 us -> 4.29 us  [paired_rest(): pl.pallas_call(gram_rest, out_shape=(shape(first_shape, F32),) * 4 + (sha...]
    pallas_call x0 -> x1, Pallas kernels: none -> 6.36 us  [paired_rest(): pl.pallas_call(gram_y, out_shape=(shape((depth, width), BF16), shape((dep...]
    ppermute x16, waiting for transfers between devices: 21.4 us -> 17.3 us  [exchange(): return lax.ppermute(value, axes, perm)]
  transfers between devices with their start and end apart: 17 -> 17, of which waited for: 9 -> 7; matrix products, arithmetic and copies ran while one was open for 0% -> 0% of each run, Pallas kernels for 11% -> 17%
where the time goes in v5:
time: 101 us
  waiting for transfers between devices  41.6 us (41%)
  Pallas kernels  29.4 us (29%)
  starting transfers between devices  27.8 us (28%)
    all_to_all x1, waiting for transfers between devices, paired_rest(): lax.all_to_all(factor_send, 'blk', split_axis=0, concat_axis=0, tiled=True)  24.3 us
    ppermute x16, starting transfers between devices, exchange(): return lax.ppermute(value, axes, perm)  20.5 us
    ppermute x16, waiting for transfers between devices, exchange(): return lax.ppermute(value, axes, perm)  17.3 us
    pallas_call x1, Pallas kernels, paired_rest(): pl.pallas_call(gram_own, out_shape=(shape((half, 256, 256), BF16), shape(...  7.66 us
    pallas_call x1, Pallas kernels, paired_body(): pl.pallas_call(plan, out_shape=(shape((half, max_order, width), F32), sha...  7.6 us
    all_to_all x1, starting transfers between devices, paired_rest(): lax.all_to_all(factor_send, 'blk', split_axis=0, concat_axis=0, tiled=True)  7.26 us
    pallas_call x1, Pallas kernels, paired_rest(): pl.pallas_call(gram_y, out_shape=(shape((depth, width), BF16), shape((dep...  6.36 us
    pallas_call x1, Pallas kernels, paired_rest(): pl.pallas_call(gram_rest, out_shape=(shape(first_shape, F32),) * 4 + (sha...  4.29 us
  transfers between devices with their start and end apart: 17, of which 7 were waited for; matrix products, arithmetic and copies ran while one was open for 0% of the time, Pallas kernels for 17%

profile of v5, /device:TPU:0, one launch (start us, length us, event | category | flops | bytes accessed | tf_op | source)
XLA Modules:
  0.0 100.6 jit_solution(16048652877489957121)
XLA Ops:
  0.0 7.6 %plan.1 = (f32[6,384,256]{2,1,0:T(8,128)}, f32[8,296,128]{2,1,0:T(8,128)}, s32[9,12]{1,0:T(8,128)S(1)}, s32[1]{0:T(128)}) custom-call(s32[96]{0:T(128)} %dest_hbm.1, s32[96]{0:T(128)} %orders_hbm.1, s32[8,96]{1,0:T(8,128)} %bitcast.42, f32[12,384,256]{2,1,0:T(8,128)} %blocks_ref.1, f32[12,384,384]{2,1,0:T(8,128)} %inv_ref.1), custom_call_target="tpu_custom_call" | custom-call | tf_op jit(solution)/shard_map/plan/pallas_call | solution.py:425
  8.3 91.7 %conditional.1 = (f32[128,256]{1,0:T(8,128)S(1)}) conditional(s32[]{:T(128)} %bitcast.17, (s32[9,12]{1,0:T(8,128)S(1)}, f32[12,384,256]{2,1,0:T(8,128)}, f32[6,384,256]{2,1,0:T(8,128)}, f32[8,296,128]{2,1,0:T(8,128)}) %tuple.13, (s32[9,12]{1,0:T(8,128)S(1)}, f32[12,384,256]{2,1,0:T(8,128)}, f32[6,384,256]{2,1,0:T(8,128)}, ...), branch_computations={%region_0.0_spmd, %region_1.0_spmd} | conditional | flops 557056 | bytes 48988840 | solution.py:457
  8.3 7.3 %all-to-all-start = ((f32[8,296,128]{2,1,0:T(8,128)}), f32[8,296,128]{2,1,0:T(8,128)S(1)}, u32[]{:S(2)}, u32[]{:S(2)}) async-start(f32[8,296,128]{2,1,0:T(8,128)} %get-tuple-element.27), calls=%async_computation | async-start | bytes 2424832 | tf_op jit(solution)/shard_map/cond/branch_0_fun/all_to_all | solution.py:491
  15.5 3.5 %pack_rows.2 = f32[2880,128]{1,0:T(8,128)} custom-call(s32[9,12]{1,0:T(8,128)S(1)} %get-tuple-element.24.table_ref, f32[12,384,256]{2,1,0:T(8,128)} %get-tuple-element.25.blocks_ref), custom_call_target="tpu_custom_call" | custom-call | tf_op jit(solution)/shard_map/cond/branch_0_fun/pack_rows/pallas_call | solution.py:481
  19.0 1.6 %collective-permute-start = (f32[2880,128]{1,0:T(8,128)}, f32[2880,128]{1,0:T(8,128)S(1)}, u32[]{:S(2)}, u32[]{:S(2)}) collective-permute-start(f32[2880,128]{1,0:T(8,128)} %pack_rows.2), channel_id=1, source_target_pairs={{0,2},{1,3},{2,0},{3,1},{4,6},{5,7},{6,4},{7,5},{8,10},{9,11},{10,... | collective-permute-start | bytes 4423688 | tf_op jit(solution)/shard_map/cond/branch_0_fun/ppermute | solution.py:472
  20.7 24.3 %all-to-all-done.factor_ref = f32[8,296,128]{2,1,0:T(8,128)S(1)} async-done(((f32[8,296,128]{2,1,0:T(8,128)}), f32[8,296,128]{2,1,0:T(8,128)S(1)}, u32[]{:S(2)}, u32[]{:S(2)}) %all-to-all-start) | async-done | bytes 1212448 | tf_op jit(solution)/shard_map/cond/branch_0_fun/all_to_all | solution.py:491
  45.0 2.9 %collective-permute-done.2.factor_other = f32[8,296,128]{2,1,0:T(8,128)S(1)} collective-permute-done((f32[8,296,128]{2,1,0:T(8,128)S(1)}, f32[8,296,128]{2,1,0:T(8,128)S(1)}, u32[]{:S(2)}, u32[]{:S(2)}) %collective-permute-start.2) | collective-permute-done | bytes 1212448 | tf_op jit(solution)/shard_map/cond/branch_0_fun/ppermute | solution.py:472
  47.8 7.7 %gram_own.2 = (bf16[6,256,256]{2,1,0:T(8,128)(2,1)S(1)}, bf16[6,256,256]{2,1,0:T(8,128)(2,1)S(1)}, bf16[6,128,384]{2,1,0:T(8,128)(2,1)S(1)}, bf16[6,128,384]{2,1...) custom-call(s32[9,12]{1,0:T(8,128)S(1)} %get-tuple-element.24.table_, ...), custom_call_target="tpu_custom_call" | custom-call | tf_op jit(solution)/shard_map/cond/branch_0_fun/gram_own/pallas_call | solution.py:496
  55.7 6.4 %gram_y.2 = (bf16[2304,256]{1,0:T(8,128)(2,1)S(1)}, bf16[2304,256]{1,0:T(8,128)(2,1)S(1)}, f32[768,256]{1,0:T(8,128)S(1)}) custom-call(s32[9,12]{1,0:T(8,128)S(1)} %get-tuple-element.24.table_ref, f32[2880,128]{1,0:T(8,128)S(1)} %collective-permute-done.y_ref, bf16[6,256,256]{2,1,0:T(8,128)(2,1)S(1)} %get-tuple-element.30.upper_high, ...), custom_call_target="tpu_custom_call" | custom-call | tf_op jit(solution)/shard_map/cond/branch_0_fun/gram_y/pallas_call | solution.py:518
  62.1 4.3 %gram_rest.2 = (f32[4,80,256]{2,1,0:T(8,128)S(1)}, f32[4,80,256]{2,1,0:T(8,128)S(1)}, f32[4,80,256]{2,1,0:T(8,128)S(1)}, f32[4,80,256]{2,1,0:T(8,128)S(1)}, f32[...) custom-call(s32[9,12]{1,0:T(8,128)S(1)} %get-tuple-element.24.table_, ...), custom_call_target="tpu_custom_call" | custom-call | tf_op jit(solution)/shard_map/cond/branch_0_fun/gram_rest/pallas_call | solution.py:528
  66.8 2.3 %collective-permute-start.11 = (f32[2,2,48,256]{3,2,1,0:T(8,128)S(1)}, f32[2,2,48,256]{3,2,1,0:T(8,128)S(1)}, u32[]{:S(2)}, u32[]{:S(2)}) collective-permute-start(f32[2,2,48,256]{3,2,1,0:T(8,128)S(1)} %get-tuple-element.48), channel_id=1, source_target_pairs={{0,16},{1,17},{2,18},{3,19},{4,20},{5,21},{6,22},{7,23},{8,24},{9,... | collective-permute-start | bytes 589832 | tf_op jit(solution)/shard_map/cond/branch_0_fun/ppermute | solution.py:472
  69.1 1.8 %collective-permute-start.12 = (f32[2,2,48,256]{3,2,1,0:T(8,128)S(1)}, f32[2,2,48,256]{3,2,1,0:T(8,128)S(1)}, u32[]{:S(2)}, u32[]{:S(2)}) collective-permute-start(f32[2,2,48,256]{3,2,1,0:T(8,128)S(1)} %get-tuple-element.49), channel_id=1, source_target_pairs={{0,24},{1,25},{2,26},{3,27},{4,28},{5,29},{6,30},{7,31},{8,16},{9,... | collective-permute-start | bytes 589832 | tf_op jit(solution)/shard_map/cond/branch_0_fun/ppermute | solution.py:472
  70.9 1.5 %collective-permute-start.4 = (f32[4,80,256]{2,1,0:T(8,128)S(1)}, f32[4,80,256]{2,1,0:T(8,128)S(1)}, u32[]{:S(2)}, u32[]{:S(2)}) collective-permute-start(f32[4,80,256]{2,1,0:T(8,128)S(1)} %get-tuple-element.43), channel_id=1, source_target_pairs={{0,2},{1,3},{2,0},{3,1},{4,6},{5,7},{6,4},{7,5},{8,10},{9,11},{10,... | collective-permute-start | bytes 983048 | tf_op jit(solution)/shard_map/cond/branch_0_fun/ppermute | solution.py:472
  72.3 1.4 %collective-permute-start.5 = (f32[4,80,256]{2,1,0:T(8,128)S(1)}, f32[4,80,256]{2,1,0:T(8,128)S(1)}, u32[]{:S(2)}, u32[]{:S(2)}) collective-permute-start(f32[4,80,256]{2,1,0:T(8,128)S(1)} %get-tuple-element.44), channel_id=1, source_target_pairs={{0,4},{1,5},{2,6},{3,7},{4,0},{5,1},{6,2},{7,3},{8,12},{9,13},{10,... | collective-permute-start | bytes 983048 | tf_op jit(solution)/shard_map/cond/branch_0_fun/ppermute | solution.py:472
  73.8 3.5 %collective-permute-done.10 = f32[2,2,48,256]{3,2,1,0:T(8,128)S(1)} collective-permute-done((f32[2,2,48,256]{3,2,1,0:T(8,128)S(1)}, f32[2,2,48,256]{3,2,1,0:T(8,128)S(1)}, u32[]{:S(2)}, u32[]{:S(2)}) %collective-permute-start.10) | collective-permute-done | bytes 196640 | tf_op jit(solution)/shard_map/cond/branch_0_fun/ppermute | solution.py:472
  77.3 2.5 %collective-permute-start.6 = (f32[4,80,256]{2,1,0:T(8,128)S(1)}, f32[4,80,256]{2,1,0:T(8,128)S(1)}, u32[]{:S(2)}, u32[]{:S(2)}) collective-permute-start(f32[4,80,256]{2,1,0:T(8,128)S(1)} %get-tuple-element.45), channel_id=1, source_target_pairs={{0,6},{1,7},{2,4},{3,5},{4,2},{5,3},{6,0},{7,1},{8,14},{9,15},{10,... | collective-permute-start | bytes 983048 | tf_op jit(solution)/shard_map/cond/branch_0_fun/ppermute | solution.py:472
  79.8 4.1 %collective-permute-done.11 = f32[2,2,48,256]{3,2,1,0:T(8,128)S(1)} collective-permute-done((f32[2,2,48,256]{3,2,1,0:T(8,128)S(1)}, f32[2,2,48,256]{3,2,1,0:T(8,128)S(1)}, u32[]{:S(2)}, u32[]{:S(2)}) %collective-permute-start.11) | collective-permute-done | bytes 196640 | tf_op jit(solution)/shard_map/cond/branch_0_fun/ppermute | solution.py:472
  84.0 1.6 %collective-permute-start.13 = (f32[48,256]{1,0:T(8,128)S(1)}, f32[48,256]{1,0:T(8,128)S(1)}, u32[]{:S(2)}, u32[]{:S(2)}) collective-permute-start(f32[48,256]{1,0:T(8,128)S(1)} %get-tuple-element.90), channel_id=1, source_target_pairs={{0,2},{1,3},{2,0},{3,1},{4,6},{5,7},{6,4},{7,5},{8,10},{9,11},{10,... | collective-permute-start | bytes 147464 | tf_op jit(solution)/shard_map/cond/branch_0_fun/ppermute | solution.py:472
  85.6 1.4 %collective-permute-start.14 = (f32[48,256]{1,0:T(8,128)S(1)}, f32[48,256]{1,0:T(8,128)S(1)}, u32[]{:S(2)}, u32[]{:S(2)}) collective-permute-start(f32[48,256]{1,0:T(8,128)S(1)} %get-tuple-element.88), channel_id=1, source_target_pairs={{0,4},{1,5},{2,6},{3,7},{4,0},{5,1},{6,2},{7,3},{8,12},{9,13},{10,... | collective-permute-start | bytes 147464 | tf_op jit(solution)/shard_map/cond/branch_0_fun/ppermute | solution.py:472
  87.5 1.3 %collective-permute-done.6 = f32[4,80,256]{2,1,0:T(8,128)S(1)} collective-permute-done((f32[4,80,256]{2,1,0:T(8,128)S(1)}, f32[4,80,256]{2,1,0:T(8,128)S(1)}, u32[]{:S(2)}, u32[]{:S(2)}) %collective-permute-start.6) | collective-permute-done | bytes 327712 | tf_op jit(solution)/shard_map/cond/branch_0_fun/ppermute | solution.py:472
  88.9 2.9 %collective-permute-start.7 = (f32[80,256]{1,0:T(8,128)S(1)}, f32[80,256]{1,0:T(8,128)S(1)}, u32[]{:S(2)}, u32[]{:S(2)}) collective-permute-start(f32[80,256]{1,0:T(8,128)S(1)} %get-tuple-element.87), channel_id=1, source_target_pairs={{0,8},{1,9},{2,10},{3,11},{4,12},{5,13},{6,14},{7,15},{8,0},{9,1},... | collective-permute-start | bytes 245768 | tf_op jit(solution)/shard_map/cond/branch_0_fun/ppermute | solution.py:472
  91.8 0.9 collective-permute-start.8
  92.7 1.5 %collective-permute-start.9 = (f32[80,256]{1,0:T(8,128)S(1)}, f32[80,256]{1,0:T(8,128)S(1)}, u32[]{:S(2)}, u32[]{:S(2)}) collective-permute-start(f32[80,256]{1,0:T(8,128)S(1)} %get-tuple-element.86), channel_id=1, source_target_pairs={{0,24},{1,25},{2,26},{3,27},{4,28},{5,29},{6,30},{7,31},{8,16},{9,... | collective-permute-start | bytes 245768 | tf_op jit(solution)/shard_map/cond/branch_0_fun/ppermute | solution.py:472
  94.8 4.9 %collective-permute-done.8 = f32[80,256]{1,0:T(8,128)S(1)} collective-permute-done((f32[80,256]{1,0:T(8,128)S(1)}, f32[80,256]{1,0:T(8,128)S(1)}, u32[]{:S(2)}, u32[]{:S(2)}) %collective-permute-start.8) | collective-permute-done | bytes 81952 | tf_op jit(solution)/shard_map/cond/branch_0_fun/ppermute | solution.py:472
  (25 shorter events, 2.6 us)
Async XLA Ops:
  8.3 36.7 %all-to-all-start = ((f32[8,296,128]{2,1,0:T(8,128)}), f32[8,296,128]{2,1,0:T(8,128)S(1)}, u32[]{:S(2)}, u32[]{:S(2)}) async-start(f32[8,296,128]{2,1,0:T(8,128)} %get-tuple-element.27), calls=%async_computation | async-start | bytes 2424832 | tf_op jit(solution)/shard_map/cond/branch_0_fun/all_to_all | solution.py:491
  15.5 29.4 %collective-permute-start.1 = (f32[6,384,256]{2,1,0:T(8,128)}, f32[6,384,256]{2,1,0:T(8,128)}, u32[]{:S(2)}, u32[]{:S(2)}) collective-permute-start(f32[6,384,256]{2,1,0:T(8,128)} %get-tuple-element.26.own_ref), channel_id=1, source_target_pairs={{0,1},{1,0},{2,3},{3,2},{4,5},{5,4},{6,7},{7,6},{8,9},{9,8},{10,11... | collective-permute-start | bytes 7077896 | tf_op jit(solution)/shard_map/cond/branch_0_fun/ppermute | solution.py:472
  19.0 36.5 %collective-permute-start = (f32[2880,128]{1,0:T(8,128)}, f32[2880,128]{1,0:T(8,128)S(1)}, u32[]{:S(2)}, u32[]{:S(2)}) collective-permute-start(f32[2880,128]{1,0:T(8,128)} %pack_rows.2), channel_id=1, source_target_pairs={{0,2},{1,3},{2,0},{3,1},{4,6},{5,7},{6,4},{7,5},{8,10},{9,11},{10,... | collective-permute-start | bytes 4423688 | tf_op jit(solution)/shard_map/cond/branch_0_fun/ppermute | solution.py:472
  44.9 2.9 %collective-permute-start.2 = (f32[8,296,128]{2,1,0:T(8,128)S(1)}, f32[8,296,128]{2,1,0:T(8,128)S(1)}, u32[]{:S(2)}, u32[]{:S(2)}) collective-permute-start(f32[8,296,128]{2,1,0:T(8,128)S(1)} %all-to-all-done.factor_ref), channel_id=1, source_target_pairs={{0,1},{1,0},{2,3},{3,2},{4,5},{5,4},{6,7},{7,6},{8,9},{9,8},{10,11... | collective-permute-start | bytes 3637256 | tf_op jit(solution)/shard_map/cond/branch_0_fun/ppermute | solution.py:472
  55.5 6.6 %collective-permute-start.3 = (f32[2880,128]{1,0:T(8,128)S(1)}, f32[2880,128]{1,0:T(8,128)S(1)}, u32[]{:S(2)}, u32[]{:S(2)}) collective-permute-start(f32[2880,128]{1,0:T(8,128)S(1)} %collective-permute-done.y_ref), channel_id=1, source_target_pairs={{0,1},{1,0},{2,3},{3,2},{4,5},{5,4},{6,7},{7,6},{8,9},{9,8},{10,11... | collective-permute-start | bytes 4423688 | tf_op jit(solution)/shard_map/cond/branch_0_fun/ppermute | solution.py:472
  66.4 10.9 %collective-permute-start.10 = (f32[2,2,48,256]{3,2,1,0:T(8,128)S(1)}, f32[2,2,48,256]{3,2,1,0:T(8,128)S(1)}, u32[]{:S(2)}, u32[]{:S(2)}) collective-permute-start(f32[2,2,48,256]{3,2,1,0:T(8,128)S(1)} %get-tuple-element.47), channel_id=1, source_target_pairs={{0,8},{1,9},{2,10},{3,11},{4,12},{5,13},{6,14},{7,15},{8,0},{9,1},... | collective-permute-start | bytes 589832 | tf_op jit(solution)/shard_map/cond/branch_0_fun/ppermute | solution.py:472
  66.8 17.1 %collective-permute-start.11 = (f32[2,2,48,256]{3,2,1,0:T(8,128)S(1)}, f32[2,2,48,256]{3,2,1,0:T(8,128)S(1)}, u32[]{:S(2)}, u32[]{:S(2)}) collective-permute-start(f32[2,2,48,256]{3,2,1,0:T(8,128)S(1)} %get-tuple-element.48), channel_id=1, source_target_pairs={{0,16},{1,17},{2,18},{3,19},{4,20},{5,21},{6,22},{7,23},{8,24},{9,... | collective-permute-start | bytes 589832 | tf_op jit(solution)/shard_map/cond/branch_0_fun/ppermute | solution.py:472
  69.1 14.8 %collective-permute-start.12 = (f32[2,2,48,256]{3,2,1,0:T(8,128)S(1)}, f32[2,2,48,256]{3,2,1,0:T(8,128)S(1)}, u32[]{:S(2)}, u32[]{:S(2)}) collective-permute-start(f32[2,2,48,256]{3,2,1,0:T(8,128)S(1)} %get-tuple-element.49), channel_id=1, source_target_pairs={{0,24},{1,25},{2,26},{3,27},{4,28},{5,29},{6,30},{7,31},{8,16},{9,... | collective-permute-start | bytes 589832 | tf_op jit(solution)/shard_map/cond/branch_0_fun/ppermute | solution.py:472
  70.9 16.1 %collective-permute-start.4 = (f32[4,80,256]{2,1,0:T(8,128)S(1)}, f32[4,80,256]{2,1,0:T(8,128)S(1)}, u32[]{:S(2)}, u32[]{:S(2)}) collective-permute-start(f32[4,80,256]{2,1,0:T(8,128)S(1)} %get-tuple-element.43), channel_id=1, source_target_pairs={{0,2},{1,3},{2,0},{3,1},{4,6},{5,7},{6,4},{7,5},{8,10},{9,11},{10,... | collective-permute-start | bytes 983048 | tf_op jit(solution)/shard_map/cond/branch_0_fun/ppermute | solution.py:472
  72.3 15.2 %collective-permute-start.5 = (f32[4,80,256]{2,1,0:T(8,128)S(1)}, f32[4,80,256]{2,1,0:T(8,128)S(1)}, u32[]{:S(2)}, u32[]{:S(2)}) collective-permute-start(f32[4,80,256]{2,1,0:T(8,128)S(1)} %get-tuple-element.44), channel_id=1, source_target_pairs={{0,4},{1,5},{2,6},{3,7},{4,0},{5,1},{6,2},{7,3},{8,12},{9,13},{10,... | collective-permute-start | bytes 983048 | tf_op jit(solution)/shard_map/cond/branch_0_fun/ppermute | solution.py:472
  77.3 11.5 %collective-permute-start.6 = (f32[4,80,256]{2,1,0:T(8,128)S(1)}, f32[4,80,256]{2,1,0:T(8,128)S(1)}, u32[]{:S(2)}, u32[]{:S(2)}) collective-permute-start(f32[4,80,256]{2,1,0:T(8,128)S(1)} %get-tuple-element.45), channel_id=1, source_target_pairs={{0,6},{1,7},{2,4},{3,5},{4,2},{5,3},{6,0},{7,1},{8,14},{9,15},{10,... | collective-permute-start | bytes 983048 | tf_op jit(solution)/shard_map/cond/branch_0_fun/ppermute | solution.py:472
  84.0 8.7 %collective-permute-start.13 = (f32[48,256]{1,0:T(8,128)S(1)}, f32[48,256]{1,0:T(8,128)S(1)}, u32[]{:S(2)}, u32[]{:S(2)}) collective-permute-start(f32[48,256]{1,0:T(8,128)S(1)} %get-tuple-element.90), channel_id=1, source_target_pairs={{0,2},{1,3},{2,0},{3,1},{4,6},{5,7},{6,4},{7,5},{8,10},{9,11},{10,... | collective-permute-start | bytes 147464 | tf_op jit(solution)/shard_map/cond/branch_0_fun/ppermute | solution.py:472
  85.6 8.6 %collective-permute-start.14 = (f32[48,256]{1,0:T(8,128)S(1)}, f32[48,256]{1,0:T(8,128)S(1)}, u32[]{:S(2)}, u32[]{:S(2)}) collective-permute-start(f32[48,256]{1,0:T(8,128)S(1)} %get-tuple-element.88), channel_id=1, source_target_pairs={{0,4},{1,5},{2,6},{3,7},{4,0},{5,1},{6,2},{7,3},{8,12},{9,13},{10,... | collective-permute-start | bytes 147464 | tf_op jit(solution)/shard_map/cond/branch_0_fun/ppermute | solution.py:472
  87.0 7.3 %collective-permute-start.15 = (f32[48,256]{1,0:T(8,128)S(1)}, f32[48,256]{1,0:T(8,128)S(1)}, u32[]{:S(2)}, u32[]{:S(2)}) collective-permute-start(f32[48,256]{1,0:T(8,128)S(1)} %get-tuple-element.89), channel_id=1, source_target_pairs={{0,6},{1,7},{2,4},{3,5},{4,2},{5,3},{6,0},{7,1},{8,14},{9,15},{10,... | collective-permute-start | bytes 147464 | tf_op jit(solution)/shard_map/cond/branch_0_fun/ppermute | solution.py:472
  88.9 5.9 %collective-permute-start.7 = (f32[80,256]{1,0:T(8,128)S(1)}, f32[80,256]{1,0:T(8,128)S(1)}, u32[]{:S(2)}, u32[]{:S(2)}) collective-permute-start(f32[80,256]{1,0:T(8,128)S(1)} %get-tuple-element.87), channel_id=1, source_target_pairs={{0,8},{1,9},{2,10},{3,11},{4,12},{5,13},{6,14},{7,15},{8,0},{9,1},... | collective-permute-start | bytes 245768 | tf_op jit(solution)/shard_map/cond/branch_0_fun/ppermute | solution.py:472
  91.8 7.9 %collective-permute-start.8 = (f32[80,256]{1,0:T(8,128)S(1)}, f32[80,256]{1,0:T(8,128)S(1)}, u32[]{:S(2)}, u32[]{:S(2)}) collective-permute-start(f32[80,256]{1,0:T(8,128)S(1)} %get-tuple-element.85), channel_id=1, source_target_pairs={{0,16},{1,17},{2,18},{3,19},{4,20},{5,21},{6,22},{7,23},{8,24},{9,... | collective-permute-start | bytes 245768 | tf_op jit(solution)/shard_map/cond/branch_0_fun/ppermute | solution.py:472
  92.7 7.0 %collective-permute-start.9 = (f32[80,256]{1,0:T(8,128)S(1)}, f32[80,256]{1,0:T(8,128)S(1)}, u32[]{:S(2)}, u32[]{:S(2)}) collective-permute-start(f32[80,256]{1,0:T(8,128)S(1)} %get-tuple-element.86), channel_id=1, source_target_pairs={{0,24},{1,25},{2,26},{3,27},{4,28},{5,29},{6,30},{7,31},{8,16},{9,... | collective-permute-start | bytes 245768 | tf_op jit(solution)/shard_map/cond/branch_0_fun/ppermute | solution.py:472
  99.9 0.7 copy-start

commit v6 on v5

--- a/solution.py
+++ b/solution.py
@@ -11,7 +11,7 @@
 F32 = jnp.float32
 BF16 = jnp.bfloat16
 XY_FIRST = 80
-VMEM_LIMIT = 32 << 20
+VMEM_LIMIT = 24 << 20
 
 
 def general_body(blocks, orders, pattern, dest, inv_factor):
@@ -69,7 +69,7 @@
 
 
 MINE, OWNER, ORDER, BITS, OTHERS, ORDER_OTHERS, BITS_OTHERS, ROW_AT = 0, 1, 2, 3, 4, 5, 6, 7
-SHARES = (0.625, 1.0)
+SHARES = (0.65625, 1.0)
 
 
 def round8(order):
@@ -143,15 +143,15 @@
 
 
 def plan(
-    dest_hbm, orders_hbm, pattern_hbm, blocks_ref, inv_ref, own_out, factor_out, table_ref, level_ref,
-    dest_ref, orders_ref, pattern_ref, orders_at, pattern_at, weight_at, weight_ref, block_at, count, found_at, factor_at, tiles_at, top_at, small_sem, factor_sem, sem,
+    dest_hbm, orders_hbm, pattern_hbm, inv_ref, factor_out, table_ref, level_ref,
+    dest_ref, orders_ref, pattern_ref, orders_at, pattern_at, weight_at, weight_ref, block_at, count, found_at, factor_at, tiles_at, top_at, small_sem, factor_sem,
 ):
     s = lax.axis_index("blk")
     t = lax.axis_index("tile")
     y, c = t // 2, t % 2
-    slots, max_order, width = blocks_ref.shape
+    slots, max_order, _ = inv_ref.shape
     n_blk = count.shape[0]
-    tiles = width // CTW
+    tiles = pattern_ref.shape[0] // 4
 
     def small_loads():
         for src, dst in (
@@ -184,23 +184,29 @@
     weight_at[...] = jnp.concatenate([rows * (counts[q] + counts[q + 1] * 65536) for q in (0, 2)], axis=0)
     weights = pltpu.make_async_copy(weight_at, weight_ref, small_sem)
     weights.start()
+
+    def scan_blocks(source, found):
+        for o in range(n_blk):
+            count[source, o] = 0
+            block_at[source, 0, o] = 0
+            block_at[source, 1, o] = 0
+        found_at[source, 0] = 0
+        found_at[source, 1] = 0
+        for i in range(slots):
+            o = dest_ref[source * slots + i]
+            r = count[source, o]
+            block_at[source, r, o] = i
+            count[source, o] = r + 1
+            mine = o == s
+            found_at[source, jnp.where(mine, r, 2)] = found
+            found = found + jnp.where(mine, 1, 0)
+        return found
+
+    lax.fori_loop(0, n_blk, scan_blocks, jnp.int32(0))
     weights.wait()
 
-    def scan_source(source, carry):
-        found, most = carry
+    def scan_source(source, most):
         base = source * slots
-        for o in range(n_blk):
-            count[o] = 0
-            block_at[0, o] = 0
-            block_at[1, o] = 0
-        for i in range(slots):
-            o = dest_ref[base + i]
-            r = count[o]
-            block_at[r, o] = i
-            count[o] = r + 1
-            mine = o == s
-            found_at[jnp.where(mine, r, 2)] = found
-            found = found + jnp.where(mine, 1, 0)
 
         def top(v):
             return jnp.maximum(jnp.maximum(v[0] & 65535, v[0] >> 16), jnp.maximum(v[1] & 65535, v[1] >> 16))
@@ -208,13 +214,13 @@
         here = source == s
         p, low, high = jnp.int32(0), jnp.int32(0), jnp.int32(0)
         for o in range(n_blk):
-            on = count[o] > 0
-            first, second = block_at[0, o], block_at[1, o]
+            on = count[source, o] > 0
+            first, second = block_at[source, 0, o], block_at[source, 1, o]
             straight = low + weight_ref[0, base + second], high + weight_ref[1, base + first]
             crossed = low + weight_ref[0, base + first], high + weight_ref[1, base + second]
             flip = top(crossed) < top(straight)
             side = y ^ jnp.where(flip, 1, 0)
-            factor_at[jnp.where(on & (s == o), source, n_blk)] = found_at[side]
+            factor_at[jnp.where(on & (s == o), source, n_blk)] = found_at[source, side]
             column = jnp.where(on & here, p, slots // 2)
             table_ref[MINE, column] = jnp.where(side == 0, first, second)
             table_ref[OTHERS, column] = jnp.where(side == 0, second, first)
@@ -222,20 +228,11 @@
             low = jnp.where(on, jnp.where(flip, crossed[0], straight[0]), low)
             high = jnp.where(on, jnp.where(flip, crossed[1], straight[1]), high)
             p = p + jnp.where(on, 1, 0)
-        return found, jnp.maximum(most, top((low, high)))
+        return jnp.maximum(most, top((low, high)))
 
     for source in range(n_blk):
         factor_at[source] = 0
-    found_at[0] = 0
-    found_at[1] = 0
-    most = lax.fori_loop(0, n_blk, scan_source, (jnp.int32(0), jnp.int32(0)))[1]
-
-    def own_loads():
-        for p in range(slots // 2):
-            yield pltpu.make_async_copy(blocks_ref.at[table_ref[MINE, p]], own_out.at[p], sem)
-
-    for copy in own_loads():
-        copy.start()
+    most = lax.fori_loop(0, n_blk, scan_source, jnp.int32(0))
 
     level = jnp.int32(0)
     for rows in row_counts(slots // 2 * tiles * max_order)[:-1]:
@@ -267,8 +264,6 @@
         return carry
 
     lax.fori_loop(0, n_blk, fold, 0)
-    for copy in own_loads():
-        copy.wait()
 
 
 def tile_on(bits, tile):
@@ -297,6 +292,18 @@
                 packed[pl.ds(pl.multiple_of(at, 8), max_order), :] = staged[p, :, e * CTW : (e + 1) * CTW]
 
             at = at + jnp.where(on, round8(table_ref[ORDER_OTHERS, p]), 0)
+
+
+def load_columns(table_ref, blocks_ref, core_ref, x_out, sem):
+    def loads():
+        for p in range(x_out.shape[0]):
+            for m, ref in enumerate((blocks_ref, core_ref)):
+                yield pltpu.make_async_copy(ref.at[table_ref[MINE, p]], x_out.at[p, m], sem)
+
+    for copy in loads():
+        copy.start()
+    for copy in loads():
+        copy.wait()
 
 
 def split(x):
@@ -323,19 +330,19 @@
 
 
 def gram_own(
-    table_ref, own_ref, core_ref, factor_ref, factor_other,
+    table_ref, x_ref, factor_ref, factor_other,
     upper_high, upper_low, lower_high, lower_low, w0_high, w0_low, w1t_high, w1t_low, g_out, w0t_high, w0t_low,
 ):
     t = lax.axis_index("tile")
     c = t % 2
-    half, max_order, width = own_ref.shape
+    half, _, max_order, width = x_ref.shape
     for p in range(half):
         here, there = factor_ref[table_ref[OWNER, p]], factor_other[table_ref[OWNER, p]]
         upper, lower = unfold_factor(jnp.where(c == 0, here, there), jnp.where(c == 0, there, here))
         upper, lower = split(upper), split(lower)
         upper_high[p], upper_low[p] = upper
         lower_high[p], lower_low[p] = lower
-        tiles = [ref[p, :, e * CTW : (e + 1) * CTW] for ref in (own_ref, core_ref) for e in range(2)]
+        tiles = [x_ref[p, m, :, e * CTW : (e + 1) * CTW] for m in range(2) for e in range(2)]
         tile_ids = [(t ^ m) * 2 + e for m in range(2) for e in range(2)]
         w = whiten(tiles, table_ref, p, upper, lower, tile_ids)
         rows = pl.ds(p * max_order, max_order)
@@ -422,16 +429,15 @@
     smem = pl.BlockSpec(memory_space=pltpu.SMEM)
     vmem = pl.BlockSpec(memory_space=pltpu.VMEM)
     shape = jax.ShapeDtypeStruct
-    own, factor_send, table, level = pl.pallas_call(
+    factor_send, table, level = pl.pallas_call(
         plan,
         out_shape=(
-            shape((half, max_order, width), F32),
             shape((n_blk, FACTOR_ROWS, CTW), F32),
             shape((9, half * tiles), jnp.int32),
             shape((1,), jnp.int32),
         ),
-        in_specs=[hbm] * 5,
-        out_specs=(vmem, vmem, smem, smem),
+        in_specs=[hbm] * 4,
+        out_specs=(vmem, smem, smem),
         scratch_shapes=[
             pltpu.SMEM(dest.shape, jnp.int32),
             pltpu.SMEM(orders.shape, jnp.int32),
@@ -440,24 +446,23 @@
             pltpu.VMEM(pattern.shape, jnp.int32),
             pltpu.VMEM((2, dest.shape[0]), jnp.int32),
             pltpu.SMEM((2, dest.shape[0]), jnp.int32),
-            pltpu.SMEM((2, n_blk), jnp.int32),
-            pltpu.SMEM((n_blk,), jnp.int32),
-            pltpu.SMEM((3,), jnp.int32),
+            pltpu.SMEM((n_blk, 2, n_blk), jnp.int32),
+            pltpu.SMEM((n_blk, n_blk), jnp.int32),
+            pltpu.SMEM((n_blk, 3), jnp.int32),
             pltpu.SMEM((n_blk + 1,), jnp.int32),
             pltpu.VMEM((slots, 3, 128, 128), F32),
             pltpu.VMEM((slots, TOP_ROWS, 128), F32),
             pltpu.SemaphoreType.DMA,
             pltpu.SemaphoreType.DMA,
-            pltpu.SemaphoreType.DMA,
         ],
         compiler_params=pltpu.CompilerParams(vmem_limit_bytes=VMEM_LIMIT),
         name="plan",
-    )(dest, orders, pattern, blocks, inv_factor)
+    )(dest, orders, pattern, inv_factor)
     rest = [functools.partial(paired_rest, rows) for rows in row_counts(half * tiles * max_order)]
-    return lax.switch(level[0], rest, table, blocks, own, factor_send)
-
-
-def paired_rest(row_count, table, blocks, own, factor_send):
+    return lax.switch(level[0], rest, table, blocks, factor_send)
+
+
+def paired_rest(row_count, table, blocks, factor_send):
     slots, max_order, width = blocks.shape
     n_blk = lax.axis_size("blk")
     n_tile = lax.axis_size("tile")
@@ -489,8 +494,18 @@
     )(table, blocks)
     y_recv = exchange(y_rows, 0, 2)
     factors = lax.all_to_all(factor_send, "blk", split_axis=0, concat_axis=0, tiled=True)
-    core_recv = exchange(own, 0, 1)
+    core_blocks = exchange(blocks, 0, 1)
     factors_other = exchange(factors, 0, 1)
+    own_table, _ = lax.optimization_barrier((table, factors))
+    columns = pl.pallas_call(
+        load_columns,
+        out_shape=shape((half, 2, max_order, width), F32),
+        in_specs=[smem, hbm, hbm],
+        out_specs=vmem,
+        scratch_shapes=[dma],
+        compiler_params=params,
+        name="load_columns",
+    )(own_table, blocks, core_blocks)
 
     depth = half * max_order
     *factor, w0_high, w0_low, w1t_high, w1t_low, g_own = pl.pallas_call(
@@ -506,12 +521,12 @@
             shape((width, depth), BF16),
             shape((2 * width, width), F32),
         ),
-        in_specs=[smem] + [vmem] * 4,
+        in_specs=[smem] + [vmem] * 3,
         out_specs=(vmem,) * 9,
         scratch_shapes=[pltpu.VMEM((width, depth), BF16), pltpu.VMEM((width, depth), BF16)],
         compiler_params=params,
         name="gram_own",
-    )(table, own, core_recv, factors, factors_other)
+    )(table, columns, factors, factors_other)
 
     y_recv, g_own = lax.optimization_barrier((y_recv, g_own))
     yc_recv = exchange(y_recv, 0, 1)

time: 101 us -> 101 us (level)
  waiting for transfers between devices: 41.6 us -> 39.3 us
  starting transfers between devices: 27.8 us -> 29.8 us
    ppermute x16, starting transfers between devices: 20.5 us -> 23.2 us  [exchange(): return lax.ppermute(value, axes, perm)]
    ppermute x16, waiting for transfers between devices: 17.3 us -> 14.8 us  [exchange(): return lax.ppermute(value, axes, perm)]
    pallas_call x1 -> x2, Pallas kernels: 7.6 us -> 9.35 us  [the longest x1 6.38 us: paired_body(): pl.pallas_call(plan, out_shape=(shape((n_blk, FACTOR_ROWS, CTW), F32), sh...]
    pallas_call x1, Pallas kernels: 7.66 us -> 5.98 us  [paired_rest(): pl.pallas_call(gram_own, out_shape=(shape((half, 256, 256), BF16), shape(...]
  transfers between devices with their start and end apart: 17 -> 17, of which waited for: 7 -> 6; matrix products, arithmetic and copies ran while one was open for 0% -> 0% of each run, Pallas kernels for 17% -> 19%
where the time goes in v6:
time: 101 us; the launch traced here: 100 us
  waiting for transfers between devices  39.3 us (39%)
  starting transfers between devices  29.8 us (30%)
  Pallas kernels  29.5 us (29%)
    all_to_all x1, waiting for transfers between devices, paired_rest(): lax.all_to_all(factor_send, 'blk', split_axis=0, concat_axis=0, tiled=True)  24.5 us
    ppermute x16, starting transfers between devices, exchange(): return lax.ppermute(value, axes, perm)  23.2 us
    ppermute x16, waiting for transfers between devices, exchange(): return lax.ppermute(value, axes, perm)  14.8 us
    all_to_all x1, starting transfers between devices, paired_rest(): lax.all_to_all(factor_send, 'blk', split_axis=0, concat_axis=0, tiled=True)  6.63 us
    pallas_call x1, Pallas kernels, paired_body(): pl.pallas_call(plan, out_shape=(shape((n_blk, FACTOR_ROWS, CTW), F32), sh...  6.38 us
    pallas_call x1, Pallas kernels, paired_rest(): pl.pallas_call(gram_y, out_shape=(shape((depth, width), BF16), shape((dep...  6.35 us
    pallas_call x1, Pallas kernels, paired_rest(): pl.pallas_call(gram_own, out_shape=(shape((half, 256, 256), BF16), shape(...  5.98 us
    pallas_call x1, Pallas kernels, paired_rest(): pl.pallas_call(gram_rest, out_shape=(shape(first_shape, F32),) * 4 + (sha...  4.28 us
  transfers between devices with their start and end apart: 17, of which 6 were waited for; matrix products, arithmetic and copies ran while one was open for 0% of the time, Pallas kernels for 19%

profile of v6, /device:TPU:0, one launch (start us, length us, event | category | flops | bytes accessed | tf_op | source)
XLA Modules:
  0.0 100.5 jit_solution(10050044978257570486)
XLA Ops:
  0.0 6.4 %plan.1 = (f32[8,296,128]{2,1,0:T(8,128)}, s32[9,12]{1,0:T(8,128)S(1)}, s32[1]{0:T(128)}) custom-call(s32[96]{0:T(128)} %dest_hbm.1, s32[96]{0:T(128)} %orders_hbm.1, s32[8,96]{1,0:T(8,128)} %bitcast.42, f32[12,384,384]{2,1,0:T(8,128)} %inv_ref.1), custom_call_target="tpu_custom_call" | custom-call | tf_op jit(solution)/shard_map/plan/pallas_call | solution.py:432
  7.0 92.8 %conditional.1 = (f32[128,256]{1,0:T(8,128)S(1)}) conditional(s32[]{:T(128)} %bitcast.17, (s32[9,12]{1,0:T(8,128)S(1)}, f32[12,384,256]{2,1,0:T(8,128)}, f32[8,296,128]{2,1,0:T(8,128)}) %tuple.15, (s32[9,12]{1,0:T(8,128)S(1)}, f32[12,384,256]{2,1,0:T(8,128)}, f32[8,296,128]{2,1,0:T(8,128)}) %tuple.15), branch_computations={%region_0.0_spmd, %region_1.0_spmd} | conditional | flops 557056 | bytes 58426024 | solution.py:462
  7.0 1.1 %collective-permute-start.1 = (f32[12,384,256]{2,1,0:T(8,128)}, f32[12,384,256]{2,1,0:T(8,128)}, u32[]{:S(2)}, u32[]{:S(2)}) collective-permute-start(f32[12,384,256]{2,1,0:T(8,128)} %get-tuple-element.21.blocks_ref), channel_id=1, source_target_pairs={{0,1},{1,0},{2,3},{3,2},{4,5},{5,4},{6,7},{7,6},{8,9},{9,8},{10,11... | collective-permute-start | bytes 14155784 | tf_op jit(solution)/shard_map/cond/branch_0_fun/ppermute | solution.py:477
  8.1 6.6 %all-to-all-start = ((f32[8,296,128]{2,1,0:T(8,128)}), f32[8,296,128]{2,1,0:T(8,128)S(1)}, u32[]{:S(2)}, u32[]{:S(2)}) async-start(f32[8,296,128]{2,1,0:T(8,128)} %get-tuple-element.22), calls=%async_computation | async-start | bytes 2424832 | tf_op jit(solution)/shard_map/cond/branch_0_fun/all_to_all | solution.py:496
  14.7 3.5 %pack_rows.2 = f32[3024,128]{1,0:T(8,128)} custom-call(s32[9,12]{1,0:T(8,128)S(1)} %get-tuple-element.23.table_ref, f32[12,384,256]{2,1,0:T(8,128)} %get-tuple-element.21.blocks_ref), custom_call_target="tpu_custom_call" | custom-call | tf_op jit(solution)/shard_map/cond/branch_0_fun/pack_rows/pallas_call | solution.py:486
  18.3 1.6 %collective-permute-start = (f32[3024,128]{1,0:T(8,128)}, f32[3024,128]{1,0:T(8,128)S(1)}, u32[]{:S(2)}, u32[]{:S(2)}) collective-permute-start(f32[3024,128]{1,0:T(8,128)} %pack_rows.2), channel_id=1, source_target_pairs={{0,2},{1,3},{2,0},{3,1},{4,6},{5,7},{6,4},{7,5},{8,10},{9,11},{10,... | collective-permute-start | bytes 4644872 | tf_op jit(solution)/shard_map/cond/branch_0_fun/ppermute | solution.py:477
  19.8 24.5 %all-to-all-done.factor_ref = f32[8,296,128]{2,1,0:T(8,128)S(1)} async-done(((f32[8,296,128]{2,1,0:T(8,128)}), f32[8,296,128]{2,1,0:T(8,128)S(1)}, u32[]{:S(2)}, u32[]{:S(2)}) %all-to-all-start) | async-done | bytes 1212448 | tf_op jit(solution)/shard_map/cond/branch_0_fun/all_to_all | solution.py:496
  44.3 3.0 %load_columns.2.x_ref = f32[6,2,384,256]{3,2,1,0:T(8,128)S(1)} custom-call(s32[9,12]{1,0:T(8,128)S(1)} %get-tuple-element.23.table_ref, f32[12,384,256]{2,1,0:T(8,128)} %get-tuple-element.21.blocks_ref, f32[12,384,256]{2,1,0:T(8,128)} %collective-permute-done.1.core_ref), custom_call_target="tpu_custom_call" | custom-call | tf_op jit(solution)/shard_map/cond/branch_0_fun/load_columns/pallas_call | solution.py:500
  47.3 6.0 %gram_own.2 = (bf16[6,256,256]{2,1,0:T(8,128)(2,1)S(1)}, bf16[6,256,256]{2,1,0:T(8,128)(2,1)S(1)}, bf16[6,128,384]{2,1,0:T(8,128)(2,1)S(1)}, bf16[6,128,384]{2,1...) custom-call(s32[9,12]{1,0:T(8,128)S(1)} %get-tuple-element.23.table_, ...), custom_call_target="tpu_custom_call" | custom-call | tf_op jit(solution)/shard_map/cond/branch_0_fun/gram_own/pallas_call | solution.py:511
  54.1 6.4 %gram_y.2 = (bf16[2304,256]{1,0:T(8,128)(2,1)S(1)}, bf16[2304,256]{1,0:T(8,128)(2,1)S(1)}, f32[768,256]{1,0:T(8,128)S(1)}) custom-call(s32[9,12]{1,0:T(8,128)S(1)} %get-tuple-element.23.table_ref, f32[3024,128]{1,0:T(8,128)S(1)} %collective-permute-done.y_ref, bf16[6,256,256]{2,1,0:T(8,128)(2,1)S(1)} %get-tuple-element.26.upper_high, ...), custom_call_target="tpu_custom_call" | custom-call | tf_op jit(solution)/shard_map/cond/branch_0_fun/gram_y/pallas_call | solution.py:533
  60.5 4.3 %gram_rest.2 = (f32[4,80,256]{2,1,0:T(8,128)S(1)}, f32[4,80,256]{2,1,0:T(8,128)S(1)}, f32[4,80,256]{2,1,0:T(8,128)S(1)}, f32[4,80,256]{2,1,0:T(8,128)S(1)}, f32[...) custom-call(s32[9,12]{1,0:T(8,128)S(1)} %get-tuple-element.23.table_, ...), custom_call_target="tpu_custom_call" | custom-call | tf_op jit(solution)/shard_map/cond/branch_0_fun/gram_rest/pallas_call | solution.py:543
  64.8 1.8 %collective-permute-start.10 = (f32[2,2,48,256]{3,2,1,0:T(8,128)S(1)}, f32[2,2,48,256]{3,2,1,0:T(8,128)S(1)}, u32[]{:S(2)}, u32[]{:S(2)}) collective-permute-start(f32[2,2,48,256]{3,2,1,0:T(8,128)S(1)} %get-tuple-element.43), channel_id=1, source_target_pairs={{0,8},{1,9},{2,10},{3,11},{4,12},{5,13},{6,14},{7,15},{8,0},{9,1},... | collective-permute-start | bytes 589832 | tf_op jit(solution)/shard_map/cond/branch_0_fun/ppermute | solution.py:477
  66.6 2.4 %collective-permute-start.11 = (f32[2,2,48,256]{3,2,1,0:T(8,128)S(1)}, f32[2,2,48,256]{3,2,1,0:T(8,128)S(1)}, u32[]{:S(2)}, u32[]{:S(2)}) collective-permute-start(f32[2,2,48,256]{3,2,1,0:T(8,128)S(1)} %get-tuple-element.44), channel_id=1, source_target_pairs={{0,16},{1,17},{2,18},{3,19},{4,20},{5,21},{6,22},{7,23},{8,24},{9,... | collective-permute-start | bytes 589832 | tf_op jit(solution)/shard_map/cond/branch_0_fun/ppermute | solution.py:477
  69.2 1.5 %collective-permute-start.4 = (f32[4,80,256]{2,1,0:T(8,128)S(1)}, f32[4,80,256]{2,1,0:T(8,128)S(1)}, u32[]{:S(2)}, u32[]{:S(2)}) collective-permute-start(f32[4,80,256]{2,1,0:T(8,128)S(1)} %get-tuple-element.39), channel_id=1, source_target_pairs={{0,2},{1,3},{2,0},{3,1},{4,6},{5,7},{6,4},{7,5},{8,10},{9,11},{10,... | collective-permute-start | bytes 983048 | tf_op jit(solution)/shard_map/cond/branch_0_fun/ppermute | solution.py:477
  70.8 1.7 %collective-permute-start.5 = (f32[4,80,256]{2,1,0:T(8,128)S(1)}, f32[4,80,256]{2,1,0:T(8,128)S(1)}, u32[]{:S(2)}, u32[]{:S(2)}) collective-permute-start(f32[4,80,256]{2,1,0:T(8,128)S(1)} %get-tuple-element.40), channel_id=1, source_target_pairs={{0,4},{1,5},{2,6},{3,7},{4,0},{5,1},{6,2},{7,3},{8,12},{9,13},{10,... | collective-permute-start | bytes 983048 | tf_op jit(solution)/shard_map/cond/branch_0_fun/ppermute | solution.py:477
  72.5 3.4 %collective-permute-done.10 = f32[2,2,48,256]{3,2,1,0:T(8,128)S(1)} collective-permute-done((f32[2,2,48,256]{3,2,1,0:T(8,128)S(1)}, f32[2,2,48,256]{3,2,1,0:T(8,128)S(1)}, u32[]{:S(2)}, u32[]{:S(2)}) %collective-permute-start.10) | collective-permute-done | bytes 196640 | tf_op jit(solution)/shard_map/cond/branch_0_fun/ppermute | solution.py:477
  75.9 2.7 %collective-permute-start.6 = (f32[4,80,256]{2,1,0:T(8,128)S(1)}, f32[4,80,256]{2,1,0:T(8,128)S(1)}, u32[]{:S(2)}, u32[]{:S(2)}) collective-permute-start(f32[4,80,256]{2,1,0:T(8,128)S(1)} %get-tuple-element.41), channel_id=1, source_target_pairs={{0,6},{1,7},{2,4},{3,5},{4,2},{5,3},{6,0},{7,1},{8,14},{9,15},{10,... | collective-permute-start | bytes 983048 | tf_op jit(solution)/shard_map/cond/branch_0_fun/ppermute | solution.py:477
  78.6 5.1 %collective-permute-done.11 = f32[2,2,48,256]{3,2,1,0:T(8,128)S(1)} collective-permute-done((f32[2,2,48,256]{3,2,1,0:T(8,128)S(1)}, f32[2,2,48,256]{3,2,1,0:T(8,128)S(1)}, u32[]{:S(2)}, u32[]{:S(2)}) %collective-permute-start.11) | collective-permute-done | bytes 196640 | tf_op jit(solution)/shard_map/cond/branch_0_fun/ppermute | solution.py:477
  83.8 1.6 %collective-permute-start.13 = (f32[48,256]{1,0:T(8,128)S(1)}, f32[48,256]{1,0:T(8,128)S(1)}, u32[]{:S(2)}, u32[]{:S(2)}) collective-permute-start(f32[48,256]{1,0:T(8,128)S(1)} %get-tuple-element.84), channel_id=1, source_target_pairs={{0,2},{1,3},{2,0},{3,1},{4,6},{5,7},{6,4},{7,5},{8,10},{9,11},{10,... | collective-permute-start | bytes 147464 | tf_op jit(solution)/shard_map/cond/branch_0_fun/ppermute | solution.py:477
  85.4 1.5 %collective-permute-start.14 = (f32[48,256]{1,0:T(8,128)S(1)}, f32[48,256]{1,0:T(8,128)S(1)}, u32[]{:S(2)}, u32[]{:S(2)}) collective-permute-start(f32[48,256]{1,0:T(8,128)S(1)} %get-tuple-element.82), channel_id=1, source_target_pairs={{0,4},{1,5},{2,6},{3,7},{4,0},{5,1},{6,2},{7,3},{8,12},{9,13},{10,... | collective-permute-start | bytes 147464 | tf_op jit(solution)/shard_map/cond/branch_0_fun/ppermute | solution.py:477
  87.5 4.1 %collective-permute-start.7 = (f32[80,256]{1,0:T(8,128)S(1)}, f32[80,256]{1,0:T(8,128)S(1)}, u32[]{:S(2)}, u32[]{:S(2)}) collective-permute-start(f32[80,256]{1,0:T(8,128)S(1)} %get-tuple-element.81), channel_id=1, source_target_pairs={{0,8},{1,9},{2,10},{3,11},{4,12},{5,13},{6,14},{7,15},{8,0},{9,1},... | collective-permute-start | bytes 245768 | tf_op jit(solution)/shard_map/cond/branch_0_fun/ppermute | solution.py:477
  91.7 1.0 collective-permute-start.8
  92.6 1.5 %collective-permute-start.9 = (f32[80,256]{1,0:T(8,128)S(1)}, f32[80,256]{1,0:T(8,128)S(1)}, u32[]{:S(2)}, u32[]{:S(2)}) collective-permute-start(f32[80,256]{1,0:T(8,128)S(1)} %get-tuple-element.80), channel_id=1, source_target_pairs={{0,24},{1,25},{2,26},{3,27},{4,28},{5,29},{6,30},{7,31},{8,16},{9,... | collective-permute-start | bytes 245768 | tf_op jit(solution)/shard_map/cond/branch_0_fun/ppermute | solution.py:477
  94.8 4.8 %collective-permute-done.8 = f32[80,256]{1,0:T(8,128)S(1)} collective-permute-done((f32[80,256]{1,0:T(8,128)S(1)}, f32[80,256]{1,0:T(8,128)S(1)}, u32[]{:S(2)}, u32[]{:S(2)}) %collective-permute-start.8) | collective-permute-done | bytes 81952 | tf_op jit(solution)/shard_map/cond/branch_0_fun/ppermute | solution.py:477
  (26 shorter events, 3.2 us)
Async XLA Ops:
  7.0 37.3 %collective-permute-start.1 = (f32[12,384,256]{2,1,0:T(8,128)}, f32[12,384,256]{2,1,0:T(8,128)}, u32[]{:S(2)}, u32[]{:S(2)}) collective-permute-start(f32[12,384,256]{2,1,0:T(8,128)} %get-tuple-element.21.blocks_ref), channel_id=1, source_target_pairs={{0,1},{1,0},{2,3},{3,2},{4,5},{5,4},{6,7},{7,6},{8,9},{9,8},{10,11... | collective-permute-start | bytes 14155784 | tf_op jit(solution)/shard_map/cond/branch_0_fun/ppermute | solution.py:477
  8.1 36.2 %all-to-all-start = ((f32[8,296,128]{2,1,0:T(8,128)}), f32[8,296,128]{2,1,0:T(8,128)S(1)}, u32[]{:S(2)}, u32[]{:S(2)}) async-start(f32[8,296,128]{2,1,0:T(8,128)} %get-tuple-element.22), calls=%async_computation | async-start | bytes 2424832 | tf_op jit(solution)/shard_map/cond/branch_0_fun/all_to_all | solution.py:496
  18.3 35.9 %collective-permute-start = (f32[3024,128]{1,0:T(8,128)}, f32[3024,128]{1,0:T(8,128)S(1)}, u32[]{:S(2)}, u32[]{:S(2)}) collective-permute-start(f32[3024,128]{1,0:T(8,128)} %pack_rows.2), channel_id=1, source_target_pairs={{0,2},{1,3},{2,0},{3,1},{4,6},{5,7},{6,4},{7,5},{8,10},{9,11},{10,... | collective-permute-start | bytes 4644872 | tf_op jit(solution)/shard_map/cond/branch_0_fun/ppermute | solution.py:477
  44.3 3.0 %collective-permute-start.2 = (f32[8,296,128]{2,1,0:T(8,128)S(1)}, f32[8,296,128]{2,1,0:T(8,128)S(1)}, u32[]{:S(2)}, u32[]{:S(2)}) collective-permute-start(f32[8,296,128]{2,1,0:T(8,128)S(1)} %all-to-all-done.factor_ref), channel_id=1, source_target_pairs={{0,1},{1,0},{2,3},{3,2},{4,5},{5,4},{6,7},{7,6},{8,9},{9,8},{10,11... | collective-permute-start | bytes 3637256 | tf_op jit(solution)/shard_map/cond/branch_0_fun/ppermute | solution.py:477
  54.1 6.4 %collective-permute-start.3 = (f32[3024,128]{1,0:T(8,128)S(1)}, f32[3024,128]{1,0:T(8,128)S(1)}, u32[]{:S(2)}, u32[]{:S(2)}) collective-permute-start(f32[3024,128]{1,0:T(8,128)S(1)} %collective-permute-done.y_ref), channel_id=1, source_target_pairs={{0,1},{1,0},{2,3},{3,2},{4,5},{5,4},{6,7},{7,6},{8,9},{9,8},{10,11... | collective-permute-start | bytes 4644872 | tf_op jit(solution)/shard_map/cond/branch_0_fun/ppermute | solution.py:477
  64.8 11.1 %collective-permute-start.10 = (f32[2,2,48,256]{3,2,1,0:T(8,128)S(1)}, f32[2,2,48,256]{3,2,1,0:T(8,128)S(1)}, u32[]{:S(2)}, u32[]{:S(2)}) collective-permute-start(f32[2,2,48,256]{3,2,1,0:T(8,128)S(1)} %get-tuple-element.43), channel_id=1, source_target_pairs={{0,8},{1,9},{2,10},{3,11},{4,12},{5,13},{6,14},{7,15},{8,0},{9,1},... | collective-permute-start | bytes 589832 | tf_op jit(solution)/shard_map/cond/branch_0_fun/ppermute | solution.py:477
  66.6 17.1 %collective-permute-start.11 = (f32[2,2,48,256]{3,2,1,0:T(8,128)S(1)}, f32[2,2,48,256]{3,2,1,0:T(8,128)S(1)}, u32[]{:S(2)}, u32[]{:S(2)}) collective-permute-start(f32[2,2,48,256]{3,2,1,0:T(8,128)S(1)} %get-tuple-element.44), channel_id=1, source_target_pairs={{0,16},{1,17},{2,18},{3,19},{4,20},{5,21},{6,22},{7,23},{8,24},{9,... | collective-permute-start | bytes 589832 | tf_op jit(solution)/shard_map/cond/branch_0_fun/ppermute | solution.py:477
  69.0 14.8 %collective-permute-start.12 = (f32[2,2,48,256]{3,2,1,0:T(8,128)S(1)}, f32[2,2,48,256]{3,2,1,0:T(8,128)S(1)}, u32[]{:S(2)}, u32[]{:S(2)}) collective-permute-start(f32[2,2,48,256]{3,2,1,0:T(8,128)S(1)} %get-tuple-element.45), channel_id=1, source_target_pairs={{0,24},{1,25},{2,26},{3,27},{4,28},{5,29},{6,30},{7,31},{8,16},{9,... | collective-permute-start | bytes 589832 | tf_op jit(solution)/shard_map/cond/branch_0_fun/ppermute | solution.py:477
  69.2 17.6 %collective-permute-start.4 = (f32[4,80,256]{2,1,0:T(8,128)S(1)}, f32[4,80,256]{2,1,0:T(8,128)S(1)}, u32[]{:S(2)}, u32[]{:S(2)}) collective-permute-start(f32[4,80,256]{2,1,0:T(8,128)S(1)} %get-tuple-element.39), channel_id=1, source_target_pairs={{0,2},{1,3},{2,0},{3,1},{4,6},{5,7},{6,4},{7,5},{8,10},{9,11},{10,... | collective-permute-start | bytes 983048 | tf_op jit(solution)/shard_map/cond/branch_0_fun/ppermute | solution.py:477
  70.8 16.6 %collective-permute-start.5 = (f32[4,80,256]{2,1,0:T(8,128)S(1)}, f32[4,80,256]{2,1,0:T(8,128)S(1)}, u32[]{:S(2)}, u32[]{:S(2)}) collective-permute-start(f32[4,80,256]{2,1,0:T(8,128)S(1)} %get-tuple-element.40), channel_id=1, source_target_pairs={{0,4},{1,5},{2,6},{3,7},{4,0},{5,1},{6,2},{7,3},{8,12},{9,13},{10,... | collective-permute-start | bytes 983048 | tf_op jit(solution)/shard_map/cond/branch_0_fun/ppermute | solution.py:477
  75.9 11.5 %collective-permute-start.6 = (f32[4,80,256]{2,1,0:T(8,128)S(1)}, f32[4,80,256]{2,1,0:T(8,128)S(1)}, u32[]{:S(2)}, u32[]{:S(2)}) collective-permute-start(f32[4,80,256]{2,1,0:T(8,128)S(1)} %get-tuple-element.41), channel_id=1, source_target_pairs={{0,6},{1,7},{2,4},{3,5},{4,2},{5,3},{6,0},{7,1},{8,14},{9,15},{10,... | collective-permute-start | bytes 983048 | tf_op jit(solution)/shard_map/cond/branch_0_fun/ppermute | solution.py:477
  83.8 8.8 %collective-permute-start.13 = (f32[48,256]{1,0:T(8,128)S(1)}, f32[48,256]{1,0:T(8,128)S(1)}, u32[]{:S(2)}, u32[]{:S(2)}) collective-permute-start(f32[48,256]{1,0:T(8,128)S(1)} %get-tuple-element.84), channel_id=1, source_target_pairs={{0,2},{1,3},{2,0},{3,1},{4,6},{5,7},{6,4},{7,5},{8,10},{9,11},{10,... | collective-permute-start | bytes 147464 | tf_op jit(solution)/shard_map/cond/branch_0_fun/ppermute | solution.py:477
  85.4 8.7 %collective-permute-start.14 = (f32[48,256]{1,0:T(8,128)S(1)}, f32[48,256]{1,0:T(8,128)S(1)}, u32[]{:S(2)}, u32[]{:S(2)}) collective-permute-start(f32[48,256]{1,0:T(8,128)S(1)} %get-tuple-element.82), channel_id=1, source_target_pairs={{0,4},{1,5},{2,6},{3,7},{4,0},{5,1},{6,2},{7,3},{8,12},{9,13},{10,... | collective-permute-start | bytes 147464 | tf_op jit(solution)/shard_map/cond/branch_0_fun/ppermute | solution.py:477
  86.9 7.2 %collective-permute-start.15 = (f32[48,256]{1,0:T(8,128)S(1)}, f32[48,256]{1,0:T(8,128)S(1)}, u32[]{:S(2)}, u32[]{:S(2)}) collective-permute-start(f32[48,256]{1,0:T(8,128)S(1)} %get-tuple-element.83), channel_id=1, source_target_pairs={{0,6},{1,7},{2,4},{3,5},{4,2},{5,3},{6,0},{7,1},{8,14},{9,15},{10,... | collective-permute-start | bytes 147464 | tf_op jit(solution)/shard_map/cond/branch_0_fun/ppermute | solution.py:477
  87.5 7.3 %collective-permute-start.7 = (f32[80,256]{1,0:T(8,128)S(1)}, f32[80,256]{1,0:T(8,128)S(1)}, u32[]{:S(2)}, u32[]{:S(2)}) collective-permute-start(f32[80,256]{1,0:T(8,128)S(1)} %get-tuple-element.81), channel_id=1, source_target_pairs={{0,8},{1,9},{2,10},{3,11},{4,12},{5,13},{6,14},{7,15},{8,0},{9,1},... | collective-permute-start | bytes 245768 | tf_op jit(solution)/shard_map/cond/branch_0_fun/ppermute | solution.py:477
  91.7 7.9 %collective-permute-start.8 = (f32[80,256]{1,0:T(8,128)S(1)}, f32[80,256]{1,0:T(8,128)S(1)}, u32[]{:S(2)}, u32[]{:S(2)}) collective-permute-start(f32[80,256]{1,0:T(8,128)S(1)} %get-tuple-element.79), channel_id=1, source_target_pairs={{0,16},{1,17},{2,18},{3,19},{4,20},{5,21},{6,22},{7,23},{8,24},{9,... | collective-permute-start | bytes 245768 | tf_op jit(solution)/shard_map/cond/branch_0_fun/ppermute | solution.py:477
  92.6 6.9 %collective-permute-start.9 = (f32[80,256]{1,0:T(8,128)S(1)}, f32[80,256]{1,0:T(8,128)S(1)}, u32[]{:S(2)}, u32[]{:S(2)}) collective-permute-start(f32[80,256]{1,0:T(8,128)S(1)} %get-tuple-element.80), channel_id=1, source_target_pairs={{0,24},{1,25},{2,26},{3,27},{4,28},{5,29},{6,30},{7,31},{8,16},{9,... | collective-permute-start | bytes 245768 | tf_op jit(solution)/shard_map/cond/branch_0_fun/ppermute | solution.py:477
  99.8 0.7 copy-start

commit v7 on v6

--- a/solution.py
+++ b/solution.py
@@ -69,7 +69,8 @@
 
 
 MINE, OWNER, ORDER, BITS, OTHERS, ORDER_OTHERS, BITS_OTHERS, ROW_AT = 0, 1, 2, 3, 4, 5, 6, 7
-SHARES = (0.65625, 1.0)
+SHARES = (0.625, 1.0)
+CHUNK = 64
 
 
 def round8(order):
@@ -236,7 +237,7 @@
 
     level = jnp.int32(0)
     for rows in row_counts(slots // 2 * tiles * max_order)[:-1]:
-        level = level + jnp.where(most + (max_order - 96) > rows, 1, 0)
+        level = level + jnp.where(most + (CHUNK - 8) > rows, 1, 0)
     level_ref[0] = level
 
     for which, order_row, bits_row in ((MINE, ORDER, BITS), (OTHERS, ORDER_OTHERS, BITS_OTHERS)):
@@ -287,10 +288,14 @@
         for e in range(tiles):
             on = tile_on(table_ref[BITS_OTHERS, p], t * tiles + e)
 
-            @pl.when(on)
-            def _(at=at, p=p, e=e):
-                packed[pl.ds(pl.multiple_of(at, 8), max_order), :] = staged[p, :, e * CTW : (e + 1) * CTW]
-
+            def write(k, carry, at=at, p=p, e=e):
+                packed[pl.ds(pl.multiple_of(at + k * CHUNK, 8), CHUNK), :] = staged[
+                    p, pl.ds(pl.multiple_of(k * CHUNK, CHUNK), CHUNK), e * CTW : (e + 1) * CTW
+                ]
+                return carry
+
+            chunks = (table_ref[ORDER_OTHERS, p] + CHUNK - 1) // CHUNK
+            lax.fori_loop(0, jnp.where(on, chunks, 0), write, 0)
             at = at + jnp.where(on, round8(table_ref[ORDER_OTHERS, p]), 0)
 
 
@@ -356,11 +361,12 @@
 
 def across(table_ref, rows_ref, group, p, upper_high, upper_low, lower_high, lower_low, max_order):
     t = lax.axis_index("tile")
-    last = rows_ref.shape[0] - max_order
+    last = rows_ref.shape[0] - CHUNK
     tiles = []
     for e in range(2):
-        at = pl.multiple_of(jnp.minimum(table_ref[ROW_AT + group - 2, p * 2 + e], last), 8)
-        tiles.append(rows_ref[pl.ds(at, max_order), :])
+        at = table_ref[ROW_AT + group - 2, p * 2 + e]
+        starts = [jnp.minimum(at + k, last) for k in range(0, max_order, CHUNK)]
+        tiles.append(jnp.concatenate([rows_ref[pl.ds(pl.multiple_of(k, 8), CHUNK), :] for k in starts], axis=0))
     upper, lower = (upper_high[p], upper_low[p]), (lower_high[p], lower_low[p])
     return whiten(tiles, table_ref, p, upper, lower, [(t ^ group) * 2 + e for e in range(2)])
 

time: 101 us -> 99.2 us (0.982)
  no operation moved by 1% of the time
where the time goes in v7:
time: 99.2 us; the launch traced here: 98.8 us
  waiting for transfers between devices  38.6 us (39%)
  Pallas kernels  29.4 us (30%)
  starting transfers between devices  28.9 us (29%)
    all_to_all x1, waiting for transfers between devices, paired_rest(): lax.all_to_all(factor_send, 'blk', split_axis=0, concat_axis=0, tiled=True)  24.5 us
    ppermute x16, starting transfers between devices, exchange(): return lax.ppermute(value, axes, perm)  22.3 us
    ppermute x16, waiting for transfers between devices, exchange(): return lax.ppermute(value, axes, perm)  14.1 us
    all_to_all x1, starting transfers between devices, paired_rest(): lax.all_to_all(factor_send, 'blk', split_axis=0, concat_axis=0, tiled=True)  6.63 us
    pallas_call x1, Pallas kernels, paired_rest(): pl.pallas_call(gram_y, out_shape=(shape((depth, width), BF16), shape((dep...  6.38 us
    pallas_call x1, Pallas kernels, paired_body(): pl.pallas_call(plan, out_shape=(shape((n_blk, FACTOR_ROWS, CTW), F32), sh...  6.38 us
    pallas_call x1, Pallas kernels, paired_rest(): pl.pallas_call(gram_own, out_shape=(shape((half, 256, 256), BF16), shape(...  5.97 us
    pallas_call x1, Pallas kernels, paired_rest(): pl.pallas_call(gram_rest, out_shape=(shape(first_shape, F32),) * 4 + (sha...  4.27 us
  transfers between devices with their start and end apart: 17, of which 6 were waited for; matrix products, arithmetic and copies ran while one was open for 0% of the time, Pallas kernels for 19%

profile of v7, /device:TPU:0, one launch (start us, length us, event | category | flops | bytes accessed | tf_op | source)
XLA Modules:
  0.0 98.8 jit_solution(14266392391675209385)
XLA Ops:
  0.0 6.4 %plan.1 = (f32[8,296,128]{2,1,0:T(8,128)}, s32[9,12]{1,0:T(8,128)S(1)}, s32[1]{0:T(128)}) custom-call(s32[96]{0:T(128)} %dest_hbm.1, s32[96]{0:T(128)} %orders_hbm.1, s32[8,96]{1,0:T(8,128)} %bitcast.42, f32[12,384,384]{2,1,0:T(8,128)} %inv_ref.1), custom_call_target="tpu_custom_call" | custom-call | tf_op jit(solution)/shard_map/plan/pallas_call | solution.py:438
  7.0 91.1 %conditional.1 = (f32[128,256]{1,0:T(8,128)S(1)}) conditional(s32[]{:T(128)} %bitcast.17, (s32[9,12]{1,0:T(8,128)S(1)}, f32[12,384,256]{2,1,0:T(8,128)}, f32[8,296,128]{2,1,0:T(8,128)}) %tuple.15, (s32[9,12]{1,0:T(8,128)S(1)}, f32[12,384,256]{2,1,0:T(8,128)}, f32[8,296,128]{2,1,0:T(8,128)}) %tuple.15), branch_computations={%region_0.0_spmd, %region_1.0_spmd} | conditional | flops 557056 | bytes 58426024 | solution.py:468
  7.0 1.1 %collective-permute-start.1 = (f32[12,384,256]{2,1,0:T(8,128)}, f32[12,384,256]{2,1,0:T(8,128)}, u32[]{:S(2)}, u32[]{:S(2)}) collective-permute-start(f32[12,384,256]{2,1,0:T(8,128)} %get-tuple-element.21.blocks_ref), channel_id=1, source_target_pairs={{0,1},{1,0},{2,3},{3,2},{4,5},{5,4},{6,7},{7,6},{8,9},{9,8},{10,11... | collective-permute-start | bytes 14155784 | tf_op jit(solution)/shard_map/cond/branch_0_fun/ppermute | solution.py:483
  8.1 6.6 %all-to-all-start = ((f32[8,296,128]{2,1,0:T(8,128)}), f32[8,296,128]{2,1,0:T(8,128)S(1)}, u32[]{:S(2)}, u32[]{:S(2)}) async-start(f32[8,296,128]{2,1,0:T(8,128)} %get-tuple-element.22), calls=%async_computation | async-start | bytes 2424832 | tf_op jit(solution)/shard_map/cond/branch_0_fun/all_to_all | solution.py:502
  14.7 3.5 %pack_rows.2 = f32[2880,128]{1,0:T(8,128)} custom-call(s32[9,12]{1,0:T(8,128)S(1)} %get-tuple-element.23.table_ref, f32[12,384,256]{2,1,0:T(8,128)} %get-tuple-element.21.blocks_ref), custom_call_target="tpu_custom_call" | custom-call | tf_op jit(solution)/shard_map/cond/branch_0_fun/pack_rows/pallas_call | solution.py:492
  18.2 1.6 %collective-permute-start = (f32[2880,128]{1,0:T(8,128)}, f32[2880,128]{1,0:T(8,128)S(1)}, u32[]{:S(2)}, u32[]{:S(2)}) collective-permute-start(f32[2880,128]{1,0:T(8,128)} %pack_rows.2), channel_id=1, source_target_pairs={{0,2},{1,3},{2,0},{3,1},{4,6},{5,7},{6,4},{7,5},{8,10},{9,11},{10,... | collective-permute-start | bytes 4423688 | tf_op jit(solution)/shard_map/cond/branch_0_fun/ppermute | solution.py:483
  19.8 24.5 %all-to-all-done.factor_ref = f32[8,296,128]{2,1,0:T(8,128)S(1)} async-done(((f32[8,296,128]{2,1,0:T(8,128)}), f32[8,296,128]{2,1,0:T(8,128)S(1)}, u32[]{:S(2)}, u32[]{:S(2)}) %all-to-all-start) | async-done | bytes 1212448 | tf_op jit(solution)/shard_map/cond/branch_0_fun/all_to_all | solution.py:502
  44.3 3.0 %load_columns.2.x_ref = f32[6,2,384,256]{3,2,1,0:T(8,128)S(1)} custom-call(s32[9,12]{1,0:T(8,128)S(1)} %get-tuple-element.23.table_ref, f32[12,384,256]{2,1,0:T(8,128)} %get-tuple-element.21.blocks_ref, f32[12,384,256]{2,1,0:T(8,128)} %collective-permute-done.1.core_ref), custom_call_target="tpu_custom_call" | custom-call | tf_op jit(solution)/shard_map/cond/branch_0_fun/load_columns/pallas_call | solution.py:506
  47.3 6.0 %gram_own.2 = (bf16[6,256,256]{2,1,0:T(8,128)(2,1)S(1)}, bf16[6,256,256]{2,1,0:T(8,128)(2,1)S(1)}, bf16[6,128,384]{2,1,0:T(8,128)(2,1)S(1)}, bf16[6,128,384]{2,1...) custom-call(s32[9,12]{1,0:T(8,128)S(1)} %get-tuple-element.23.table_, ...), custom_call_target="tpu_custom_call" | custom-call | tf_op jit(solution)/shard_map/cond/branch_0_fun/gram_own/pallas_call | solution.py:517
  53.9 6.4 %gram_y.2 = (bf16[2304,256]{1,0:T(8,128)(2,1)S(1)}, bf16[2304,256]{1,0:T(8,128)(2,1)S(1)}, f32[768,256]{1,0:T(8,128)S(1)}) custom-call(s32[9,12]{1,0:T(8,128)S(1)} %get-tuple-element.23.table_ref, f32[2880,128]{1,0:T(8,128)S(1)} %collective-permute-done.y_ref, bf16[6,256,256]{2,1,0:T(8,128)(2,1)S(1)} %get-tuple-element.26.upper_high, ...), custom_call_target="tpu_custom_call" | custom-call | tf_op jit(solution)/shard_map/cond/branch_0_fun/gram_y/pallas_call | solution.py:539
  60.3 4.3 %gram_rest.2 = (f32[4,80,256]{2,1,0:T(8,128)S(1)}, f32[4,80,256]{2,1,0:T(8,128)S(1)}, f32[4,80,256]{2,1,0:T(8,128)S(1)}, f32[4,80,256]{2,1,0:T(8,128)S(1)}, f32[...) custom-call(s32[9,12]{1,0:T(8,128)S(1)} %get-tuple-element.23.table_, ...), custom_call_target="tpu_custom_call" | custom-call | tf_op jit(solution)/shard_map/cond/branch_0_fun/gram_rest/pallas_call | solution.py:549
  65.0 2.4 %collective-permute-start.11 = (f32[2,2,48,256]{3,2,1,0:T(8,128)S(1)}, f32[2,2,48,256]{3,2,1,0:T(8,128)S(1)}, u32[]{:S(2)}, u32[]{:S(2)}) collective-permute-start(f32[2,2,48,256]{3,2,1,0:T(8,128)S(1)} %get-tuple-element.44), channel_id=1, source_target_pairs={{0,16},{1,17},{2,18},{3,19},{4,20},{5,21},{6,22},{7,23},{8,24},{9,... | collective-permute-start | bytes 589832 | tf_op jit(solution)/shard_map/cond/branch_0_fun/ppermute | solution.py:483
  67.4 1.6 %collective-permute-start.12 = (f32[2,2,48,256]{3,2,1,0:T(8,128)S(1)}, f32[2,2,48,256]{3,2,1,0:T(8,128)S(1)}, u32[]{:S(2)}, u32[]{:S(2)}) collective-permute-start(f32[2,2,48,256]{3,2,1,0:T(8,128)S(1)} %get-tuple-element.45), channel_id=1, source_target_pairs={{0,24},{1,25},{2,26},{3,27},{4,28},{5,29},{6,30},{7,31},{8,16},{9,... | collective-permute-start | bytes 589832 | tf_op jit(solution)/shard_map/cond/branch_0_fun/ppermute | solution.py:483
  69.0 1.5 %collective-permute-start.4 = (f32[4,80,256]{2,1,0:T(8,128)S(1)}, f32[4,80,256]{2,1,0:T(8,128)S(1)}, u32[]{:S(2)}, u32[]{:S(2)}) collective-permute-start(f32[4,80,256]{2,1,0:T(8,128)S(1)} %get-tuple-element.39), channel_id=1, source_target_pairs={{0,2},{1,3},{2,0},{3,1},{4,6},{5,7},{6,4},{7,5},{8,10},{9,11},{10,... | collective-permute-start | bytes 983048 | tf_op jit(solution)/shard_map/cond/branch_0_fun/ppermute | solution.py:483
  70.5 1.4 %collective-permute-start.5 = (f32[4,80,256]{2,1,0:T(8,128)S(1)}, f32[4,80,256]{2,1,0:T(8,128)S(1)}, u32[]{:S(2)}, u32[]{:S(2)}) collective-permute-start(f32[4,80,256]{2,1,0:T(8,128)S(1)} %get-tuple-element.40), channel_id=1, source_target_pairs={{0,4},{1,5},{2,6},{3,7},{4,0},{5,1},{6,2},{7,3},{8,12},{9,13},{10,... | collective-permute-start | bytes 983048 | tf_op jit(solution)/shard_map/cond/branch_0_fun/ppermute | solution.py:483
  71.9 3.3 %collective-permute-done.10 = f32[2,2,48,256]{3,2,1,0:T(8,128)S(1)} collective-permute-done((f32[2,2,48,256]{3,2,1,0:T(8,128)S(1)}, f32[2,2,48,256]{3,2,1,0:T(8,128)S(1)}, u32[]{:S(2)}, u32[]{:S(2)}) %collective-permute-start.10) | collective-permute-done | bytes 196640 | tf_op jit(solution)/shard_map/cond/branch_0_fun/ppermute | solution.py:483
  75.2 2.4 %collective-permute-start.6 = (f32[4,80,256]{2,1,0:T(8,128)S(1)}, f32[4,80,256]{2,1,0:T(8,128)S(1)}, u32[]{:S(2)}, u32[]{:S(2)}) collective-permute-start(f32[4,80,256]{2,1,0:T(8,128)S(1)} %get-tuple-element.41), channel_id=1, source_target_pairs={{0,6},{1,7},{2,4},{3,5},{4,2},{5,3},{6,0},{7,1},{8,14},{9,15},{10,... | collective-permute-start | bytes 983048 | tf_op jit(solution)/shard_map/cond/branch_0_fun/ppermute | solution.py:483
  77.5 4.6 %collective-permute-done.11 = f32[2,2,48,256]{3,2,1,0:T(8,128)S(1)} collective-permute-done((f32[2,2,48,256]{3,2,1,0:T(8,128)S(1)}, f32[2,2,48,256]{3,2,1,0:T(8,128)S(1)}, u32[]{:S(2)}, u32[]{:S(2)}) %collective-permute-start.11) | collective-permute-done | bytes 196640 | tf_op jit(solution)/shard_map/cond/branch_0_fun/ppermute | solution.py:483
  82.2 1.6 %collective-permute-start.13 = (f32[48,256]{1,0:T(8,128)S(1)}, f32[48,256]{1,0:T(8,128)S(1)}, u32[]{:S(2)}, u32[]{:S(2)}) collective-permute-start(f32[48,256]{1,0:T(8,128)S(1)} %get-tuple-element.84), channel_id=1, source_target_pairs={{0,2},{1,3},{2,0},{3,1},{4,6},{5,7},{6,4},{7,5},{8,10},{9,11},{10,... | collective-permute-start | bytes 147464 | tf_op jit(solution)/shard_map/cond/branch_0_fun/ppermute | solution.py:483
  83.8 1.5 %collective-permute-start.14 = (f32[48,256]{1,0:T(8,128)S(1)}, f32[48,256]{1,0:T(8,128)S(1)}, u32[]{:S(2)}, u32[]{:S(2)}) collective-permute-start(f32[48,256]{1,0:T(8,128)S(1)} %get-tuple-element.82), channel_id=1, source_target_pairs={{0,4},{1,5},{2,6},{3,7},{4,0},{5,1},{6,2},{7,3},{8,12},{9,13},{10,... | collective-permute-start | bytes 147464 | tf_op jit(solution)/shard_map/cond/branch_0_fun/ppermute | solution.py:483
  86.7 3.3 %collective-permute-start.7 = (f32[80,256]{1,0:T(8,128)S(1)}, f32[80,256]{1,0:T(8,128)S(1)}, u32[]{:S(2)}, u32[]{:S(2)}) collective-permute-start(f32[80,256]{1,0:T(8,128)S(1)} %get-tuple-element.81), channel_id=1, source_target_pairs={{0,8},{1,9},{2,10},{3,11},{4,12},{5,13},{6,14},{7,15},{8,0},{9,1},... | collective-permute-start | bytes 245768 | tf_op jit(solution)/shard_map/cond/branch_0_fun/ppermute | solution.py:483
  90.0 1.0 %collective-permute-start.8 = (f32[80,256]{1,0:T(8,128)S(1)}, f32[80,256]{1,0:T(8,128)S(1)}, u32[]{:S(2)}, u32[]{:S(2)}) collective-permute-start(f32[80,256]{1,0:T(8,128)S(1)} %get-tuple-element.79), channel_id=1, source_target_pairs={{0,16},{1,17},{2,18},{3,19},{4,20},{5,21},{6,22},{7,23},{8,24},{9,... | collective-permute-start | bytes 245768 | tf_op jit(solution)/shard_map/cond/branch_0_fun/ppermute | solution.py:483
  91.0 1.4 %collective-permute-start.9 = (f32[80,256]{1,0:T(8,128)S(1)}, f32[80,256]{1,0:T(8,128)S(1)}, u32[]{:S(2)}, u32[]{:S(2)}) collective-permute-start(f32[80,256]{1,0:T(8,128)S(1)} %get-tuple-element.80), channel_id=1, source_target_pairs={{0,24},{1,25},{2,26},{3,27},{4,28},{5,29},{6,30},{7,31},{8,16},{9,... | collective-permute-start | bytes 245768 | tf_op jit(solution)/shard_map/cond/branch_0_fun/ppermute | solution.py:483
  93.2 4.7 %collective-permute-done.8 = f32[80,256]{1,0:T(8,128)S(1)} collective-permute-done((f32[80,256]{1,0:T(8,128)S(1)}, f32[80,256]{1,0:T(8,128)S(1)}, u32[]{:S(2)}, u32[]{:S(2)}) %collective-permute-start.8) | collective-permute-done | bytes 81952 | tf_op jit(solution)/shard_map/cond/branch_0_fun/ppermute | solution.py:483
  (26 shorter events, 3.9 us)
Async XLA Ops:
  7.0 37.3 %collective-permute-start.1 = (f32[12,384,256]{2,1,0:T(8,128)}, f32[12,384,256]{2,1,0:T(8,128)}, u32[]{:S(2)}, u32[]{:S(2)}) collective-permute-start(f32[12,384,256]{2,1,0:T(8,128)} %get-tuple-element.21.blocks_ref), channel_id=1, source_target_pairs={{0,1},{1,0},{2,3},{3,2},{4,5},{5,4},{6,7},{7,6},{8,9},{9,8},{10,11... | collective-permute-start | bytes 14155784 | tf_op jit(solution)/shard_map/cond/branch_0_fun/ppermute | solution.py:483
  8.1 36.2 %all-to-all-start = ((f32[8,296,128]{2,1,0:T(8,128)}), f32[8,296,128]{2,1,0:T(8,128)S(1)}, u32[]{:S(2)}, u32[]{:S(2)}) async-start(f32[8,296,128]{2,1,0:T(8,128)} %get-tuple-element.22), calls=%async_computation | async-start | bytes 2424832 | tf_op jit(solution)/shard_map/cond/branch_0_fun/all_to_all | solution.py:502
  18.2 35.1 %collective-permute-start = (f32[2880,128]{1,0:T(8,128)}, f32[2880,128]{1,0:T(8,128)S(1)}, u32[]{:S(2)}, u32[]{:S(2)}) collective-permute-start(f32[2880,128]{1,0:T(8,128)} %pack_rows.2), channel_id=1, source_target_pairs={{0,2},{1,3},{2,0},{3,1},{4,6},{5,7},{6,4},{7,5},{8,10},{9,11},{10,... | collective-permute-start | bytes 4423688 | tf_op jit(solution)/shard_map/cond/branch_0_fun/ppermute | solution.py:483
  44.3 3.0 %collective-permute-start.2 = (f32[8,296,128]{2,1,0:T(8,128)S(1)}, f32[8,296,128]{2,1,0:T(8,128)S(1)}, u32[]{:S(2)}, u32[]{:S(2)}) collective-permute-start(f32[8,296,128]{2,1,0:T(8,128)S(1)} %all-to-all-done.factor_ref), channel_id=1, source_target_pairs={{0,1},{1,0},{2,3},{3,2},{4,5},{5,4},{6,7},{7,6},{8,9},{9,8},{10,11... | collective-permute-start | bytes 3637256 | tf_op jit(solution)/shard_map/cond/branch_0_fun/ppermute | solution.py:483
  53.3 7.0 %collective-permute-start.3 = (f32[2880,128]{1,0:T(8,128)S(1)}, f32[2880,128]{1,0:T(8,128)S(1)}, u32[]{:S(2)}, u32[]{:S(2)}) collective-permute-start(f32[2880,128]{1,0:T(8,128)S(1)} %collective-permute-done.y_ref), channel_id=1, source_target_pairs={{0,1},{1,0},{2,3},{3,2},{4,5},{5,4},{6,7},{7,6},{8,9},{9,8},{10,11... | collective-permute-start | bytes 4423688 | tf_op jit(solution)/shard_map/cond/branch_0_fun/ppermute | solution.py:483
  64.6 10.6 %collective-permute-start.10 = (f32[2,2,48,256]{3,2,1,0:T(8,128)S(1)}, f32[2,2,48,256]{3,2,1,0:T(8,128)S(1)}, u32[]{:S(2)}, u32[]{:S(2)}) collective-permute-start(f32[2,2,48,256]{3,2,1,0:T(8,128)S(1)} %get-tuple-element.43), channel_id=1, source_target_pairs={{0,8},{1,9},{2,10},{3,11},{4,12},{5,13},{6,14},{7,15},{8,0},{9,1},... | collective-permute-start | bytes 589832 | tf_op jit(solution)/shard_map/cond/branch_0_fun/ppermute | solution.py:483
  65.0 17.1 %collective-permute-start.11 = (f32[2,2,48,256]{3,2,1,0:T(8,128)S(1)}, f32[2,2,48,256]{3,2,1,0:T(8,128)S(1)}, u32[]{:S(2)}, u32[]{:S(2)}) collective-permute-start(f32[2,2,48,256]{3,2,1,0:T(8,128)S(1)} %get-tuple-element.44), channel_id=1, source_target_pairs={{0,16},{1,17},{2,18},{3,19},{4,20},{5,21},{6,22},{7,23},{8,24},{9,... | collective-permute-start | bytes 589832 | tf_op jit(solution)/shard_map/cond/branch_0_fun/ppermute | solution.py:483
  67.4 14.7 %collective-permute-start.12 = (f32[2,2,48,256]{3,2,1,0:T(8,128)S(1)}, f32[2,2,48,256]{3,2,1,0:T(8,128)S(1)}, u32[]{:S(2)}, u32[]{:S(2)}) collective-permute-start(f32[2,2,48,256]{3,2,1,0:T(8,128)S(1)} %get-tuple-element.45), channel_id=1, source_target_pairs={{0,24},{1,25},{2,26},{3,27},{4,28},{5,29},{6,30},{7,31},{8,16},{9,... | collective-permute-start | bytes 589832 | tf_op jit(solution)/shard_map/cond/branch_0_fun/ppermute | solution.py:483
  69.0 16.3 %collective-permute-start.4 = (f32[4,80,256]{2,1,0:T(8,128)S(1)}, f32[4,80,256]{2,1,0:T(8,128)S(1)}, u32[]{:S(2)}, u32[]{:S(2)}) collective-permute-start(f32[4,80,256]{2,1,0:T(8,128)S(1)} %get-tuple-element.39), channel_id=1, source_target_pairs={{0,2},{1,3},{2,0},{3,1},{4,6},{5,7},{6,4},{7,5},{8,10},{9,11},{10,... | collective-permute-start | bytes 983048 | tf_op jit(solution)/shard_map/cond/branch_0_fun/ppermute | solution.py:483
  70.5 15.2 %collective-permute-start.5 = (f32[4,80,256]{2,1,0:T(8,128)S(1)}, f32[4,80,256]{2,1,0:T(8,128)S(1)}, u32[]{:S(2)}, u32[]{:S(2)}) collective-permute-start(f32[4,80,256]{2,1,0:T(8,128)S(1)} %get-tuple-element.40), channel_id=1, source_target_pairs={{0,4},{1,5},{2,6},{3,7},{4,0},{5,1},{6,2},{7,3},{8,12},{9,13},{10,... | collective-permute-start | bytes 983048 | tf_op jit(solution)/shard_map/cond/branch_0_fun/ppermute | solution.py:483
  75.2 11.4 %collective-permute-start.6 = (f32[4,80,256]{2,1,0:T(8,128)S(1)}, f32[4,80,256]{2,1,0:T(8,128)S(1)}, u32[]{:S(2)}, u32[]{:S(2)}) collective-permute-start(f32[4,80,256]{2,1,0:T(8,128)S(1)} %get-tuple-element.41), channel_id=1, source_target_pairs={{0,6},{1,7},{2,4},{3,5},{4,2},{5,3},{6,0},{7,1},{8,14},{9,15},{10,... | collective-permute-start | bytes 983048 | tf_op jit(solution)/shard_map/cond/branch_0_fun/ppermute | solution.py:483
  82.2 8.8 %collective-permute-start.13 = (f32[48,256]{1,0:T(8,128)S(1)}, f32[48,256]{1,0:T(8,128)S(1)}, u32[]{:S(2)}, u32[]{:S(2)}) collective-permute-start(f32[48,256]{1,0:T(8,128)S(1)} %get-tuple-element.84), channel_id=1, source_target_pairs={{0,2},{1,3},{2,0},{3,1},{4,6},{5,7},{6,4},{7,5},{8,10},{9,11},{10,... | collective-permute-start | bytes 147464 | tf_op jit(solution)/shard_map/cond/branch_0_fun/ppermute | solution.py:483
  83.8 8.6 %collective-permute-start.14 = (f32[48,256]{1,0:T(8,128)S(1)}, f32[48,256]{1,0:T(8,128)S(1)}, u32[]{:S(2)}, u32[]{:S(2)}) collective-permute-start(f32[48,256]{1,0:T(8,128)S(1)} %get-tuple-element.82), channel_id=1, source_target_pairs={{0,4},{1,5},{2,6},{3,7},{4,0},{5,1},{6,2},{7,3},{8,12},{9,13},{10,... | collective-permute-start | bytes 147464 | tf_op jit(solution)/shard_map/cond/branch_0_fun/ppermute | solution.py:483
  85.3 7.2 %collective-permute-start.15 = (f32[48,256]{1,0:T(8,128)S(1)}, f32[48,256]{1,0:T(8,128)S(1)}, u32[]{:S(2)}, u32[]{:S(2)}) collective-permute-start(f32[48,256]{1,0:T(8,128)S(1)} %get-tuple-element.83), channel_id=1, source_target_pairs={{0,6},{1,7},{2,4},{3,5},{4,2},{5,3},{6,0},{7,1},{8,14},{9,15},{10,... | collective-permute-start | bytes 147464 | tf_op jit(solution)/shard_map/cond/branch_0_fun/ppermute | solution.py:483
  86.7 6.5 %collective-permute-start.7 = (f32[80,256]{1,0:T(8,128)S(1)}, f32[80,256]{1,0:T(8,128)S(1)}, u32[]{:S(2)}, u32[]{:S(2)}) collective-permute-start(f32[80,256]{1,0:T(8,128)S(1)} %get-tuple-element.81), channel_id=1, source_target_pairs={{0,8},{1,9},{2,10},{3,11},{4,12},{5,13},{6,14},{7,15},{8,0},{9,1},... | collective-permute-start | bytes 245768 | tf_op jit(solution)/shard_map/cond/branch_0_fun/ppermute | solution.py:483
  90.0 7.9 %collective-permute-start.8 = (f32[80,256]{1,0:T(8,128)S(1)}, f32[80,256]{1,0:T(8,128)S(1)}, u32[]{:S(2)}, u32[]{:S(2)}) collective-permute-start(f32[80,256]{1,0:T(8,128)S(1)} %get-tuple-element.79), channel_id=1, source_target_pairs={{0,16},{1,17},{2,18},{3,19},{4,20},{5,21},{6,22},{7,23},{8,24},{9,... | collective-permute-start | bytes 245768 | tf_op jit(solution)/shard_map/cond/branch_0_fun/ppermute | solution.py:483
  91.0 6.9 %collective-permute-start.9 = (f32[80,256]{1,0:T(8,128)S(1)}, f32[80,256]{1,0:T(8,128)S(1)}, u32[]{:S(2)}, u32[]{:S(2)}) collective-permute-start(f32[80,256]{1,0:T(8,128)S(1)} %get-tuple-element.80), channel_id=1, source_target_pairs={{0,24},{1,25},{2,26},{3,27},{4,28},{5,29},{6,30},{7,31},{8,16},{9,... | collective-permute-start | bytes 245768 | tf_op jit(solution)/shard_map/cond/branch_0_fun/ppermute | solution.py:483
  98.2 0.7 copy-start

commit v8 on v7

--- a/solution.py
+++ b/solution.py
@@ -145,18 +145,18 @@
 
 def plan(
     dest_hbm, orders_hbm, pattern_hbm, inv_ref, factor_out, table_ref, level_ref,
-    dest_ref, orders_ref, pattern_ref, orders_at, pattern_at, weight_at, weight_ref, block_at, count, found_at, factor_at, tiles_at, top_at, small_sem, factor_sem,
+    dest_ref, orders_ref, orders_at, pattern_at, weight_at, weight_ref, block_at, count, found_at, factor_at, tiles_at, top_at, small_sem, factor_sem,
 ):
     s = lax.axis_index("blk")
     t = lax.axis_index("tile")
     y, c = t // 2, t % 2
     slots, max_order, _ = inv_ref.shape
     n_blk = count.shape[0]
-    tiles = pattern_ref.shape[0] // 4
+    tiles = pattern_at.shape[0] // 4
 
     def small_loads():
         for src, dst in (
-            (orders_hbm, orders_at), (pattern_hbm, pattern_at), (dest_hbm, dest_ref), (orders_hbm, orders_ref), (pattern_hbm, pattern_ref),
+            (orders_hbm, orders_at), (pattern_hbm, pattern_at), (dest_hbm, dest_ref), (orders_hbm, orders_ref),
         ):
             yield pltpu.make_async_copy(src, dst, small_sem)
 
@@ -182,7 +182,10 @@
     ones = pattern_at[...]
     counts = [sum(ones[q * tiles + e : q * tiles + e + 1] for e in range(tiles)) for q in range(4)]
     rows = round8(orders_at[...])[None, :]
-    weight_at[...] = jnp.concatenate([rows * (counts[q] + counts[q + 1] * 65536) for q in (0, 2)], axis=0)
+    bits_of = sum(jnp.where(ones[ct : ct + 1] != 0, 1 << ct, 0) for ct in range(4 * tiles))
+    weight_at[...] = jnp.concatenate(
+        [rows * (counts[q] + counts[q + 1] * 65536) for q in (0, 2)] + [bits_of], axis=0
+    )
     weights = pltpu.make_async_copy(weight_at, weight_ref, small_sem)
     weights.start()
 
@@ -203,7 +206,7 @@
             found = found + jnp.where(mine, 1, 0)
         return found
 
-    lax.fori_loop(0, n_blk, scan_blocks, jnp.int32(0))
+    lax.fori_loop(0, n_blk, scan_blocks, jnp.int32(0), unroll=True)
     weights.wait()
 
     def scan_source(source, most):
@@ -233,7 +236,7 @@
 
     for source in range(n_blk):
         factor_at[source] = 0
-    most = lax.fori_loop(0, n_blk, scan_source, jnp.int32(0))
+    most = lax.fori_loop(0, n_blk, scan_source, jnp.int32(0), unroll=True)
 
     level = jnp.int32(0)
     for rows in row_counts(slots // 2 * tiles * max_order)[:-1]:
@@ -244,10 +247,7 @@
         for p in range(slots // 2):
             number = s * slots + table_ref[which, p]
             table_ref[order_row, p] = orders_ref[number]
-            bits = jnp.int32(0)
-            for ct in range(4 * tiles):
-                bits = bits + jnp.where(pattern_ref[ct, number] != 0, 1 << ct, 0)
-            table_ref[bits_row, p] = bits
+            table_ref[bits_row, p] = weight_ref[2, number]
     for k in range(2):
         at = jnp.int32(0)
         for p in range(slots // 2):
@@ -447,11 +447,10 @@
         scratch_shapes=[
             pltpu.SMEM(dest.shape, jnp.int32),
             pltpu.SMEM(orders.shape, jnp.int32),
-            pltpu.SMEM(pattern.shape, jnp.int32),
             pltpu.VMEM(orders.shape, jnp.int32),
             pltpu.VMEM(pattern.shape, jnp.int32),
-            pltpu.VMEM((2, dest.shape[0]), jnp.int32),
-            pltpu.SMEM((2, dest.shape[0]), jnp.int32),
+            pltpu.VMEM((3, dest.shape[0]), jnp.int32),
+            pltpu.SMEM((3, dest.shape[0]), jnp.int32),
             pltpu.SMEM((n_blk, 2, n_blk), jnp.int32),
             pltpu.SMEM((n_blk, n_blk), jnp.int32),
             pltpu.SMEM((n_blk, 3), jnp.int32),

time: 99.2 us -> 99 us (level)
  no operation moved by 1% of the time
where the time goes in v8:
time: 99 us; the launch traced here: 98.7 us
  waiting for transfers between devices  38.2 us (39%)
  starting transfers between devices  29.5 us (30%)
  Pallas kernels  29.1 us (29%)
    all_to_all x1, waiting for transfers between devices, paired_rest(): lax.all_to_all(factor_send, 'blk', split_axis=0, concat_axis=0, tiled=True)  24.3 us
    ppermute x16, starting transfers between devices, exchange(): return lax.ppermute(value, axes, perm)  22.9 us
    ppermute x16, waiting for transfers between devices, exchange(): return lax.ppermute(value, axes, perm)  13.9 us
    all_to_all x1, starting transfers between devices, paired_rest(): lax.all_to_all(factor_send, 'blk', split_axis=0, concat_axis=0, tiled=True)  6.63 us
    pallas_call x1, Pallas kernels, paired_rest(): pl.pallas_call(gram_y, out_shape=(shape((depth, width), BF16), shape((dep...  6.37 us
    pallas_call x1, Pallas kernels, paired_body(): pl.pallas_call(plan, out_shape=(shape((n_blk, FACTOR_ROWS, CTW), F32), sh...  5.99 us
    pallas_call x1, Pallas kernels, paired_rest(): pl.pallas_call(gram_own, out_shape=(shape((half, 256, 256), BF16), shape(...  5.97 us
    pallas_call x1, Pallas kernels, paired_rest(): pl.pallas_call(gram_rest, out_shape=(shape(first_shape, F32),) * 4 + (sha...  4.29 us
  transfers between devices with their start and end apart: 17, of which 6 were waited for; matrix products, arithmetic and copies ran while one was open for 0% of the time, Pallas kernels for 19%

profile of v8, /device:TPU:0, one launch (start us, length us, event | category | flops | bytes accessed | tf_op | source)
XLA Modules:
  0.0 98.7 jit_solution(200177307249423377)
XLA Ops:
  0.0 6.0 %plan.1 = (f32[8,296,128]{2,1,0:T(8,128)}, s32[9,12]{1,0:T(8,128)S(1)}, s32[1]{0:T(128)}) custom-call(s32[96]{0:T(128)} %dest_hbm.1, s32[96]{0:T(128)} %orders_hbm.1, s32[8,96]{1,0:T(8,128)} %bitcast.42, f32[12,384,384]{2,1,0:T(8,128)} %inv_ref.1), custom_call_target="tpu_custom_call" | custom-call | tf_op jit(solution)/shard_map/plan/pallas_call | solution.py:438
  6.6 91.4 %conditional.1 = (f32[128,256]{1,0:T(8,128)S(1)}) conditional(s32[]{:T(128)} %bitcast.17, (s32[9,12]{1,0:T(8,128)S(1)}, f32[12,384,256]{2,1,0:T(8,128)}, f32[8,296,128]{2,1,0:T(8,128)}) %tuple.15, (s32[9,12]{1,0:T(8,128)S(1)}, f32[12,384,256]{2,1,0:T(8,128)}, f32[8,296,128]{2,1,0:T(8,128)}) %tuple.15), branch_computations={%region_0.0_spmd, %region_1.0_spmd} | conditional | flops 557056 | bytes 58426024 | solution.py:467
  6.7 1.1 %collective-permute-start.1 = (f32[12,384,256]{2,1,0:T(8,128)}, f32[12,384,256]{2,1,0:T(8,128)}, u32[]{:S(2)}, u32[]{:S(2)}) collective-permute-start(f32[12,384,256]{2,1,0:T(8,128)} %get-tuple-element.21.blocks_ref), channel_id=1, source_target_pairs={{0,1},{1,0},{2,3},{3,2},{4,5},{5,4},{6,7},{7,6},{8,9},{9,8},{10,11... | collective-permute-start | bytes 14155784 | tf_op jit(solution)/shard_map/cond/branch_0_fun/ppermute | solution.py:482
  7.8 6.6 %all-to-all-start = ((f32[8,296,128]{2,1,0:T(8,128)}), f32[8,296,128]{2,1,0:T(8,128)S(1)}, u32[]{:S(2)}, u32[]{:S(2)}) async-start(f32[8,296,128]{2,1,0:T(8,128)} %get-tuple-element.22), calls=%async_computation | async-start | bytes 2424832 | tf_op jit(solution)/shard_map/cond/branch_0_fun/all_to_all | solution.py:501
  14.4 3.6 %pack_rows.2 = f32[2880,128]{1,0:T(8,128)} custom-call(s32[9,12]{1,0:T(8,128)S(1)} %get-tuple-element.23.table_ref, f32[12,384,256]{2,1,0:T(8,128)} %get-tuple-element.21.blocks_ref), custom_call_target="tpu_custom_call" | custom-call | tf_op jit(solution)/shard_map/cond/branch_0_fun/pack_rows/pallas_call | solution.py:491
  18.0 1.7 %collective-permute-start = (f32[2880,128]{1,0:T(8,128)}, f32[2880,128]{1,0:T(8,128)S(1)}, u32[]{:S(2)}, u32[]{:S(2)}) collective-permute-start(f32[2880,128]{1,0:T(8,128)} %pack_rows.2), channel_id=1, source_target_pairs={{0,2},{1,3},{2,0},{3,1},{4,6},{5,7},{6,4},{7,5},{8,10},{9,11},{10,... | collective-permute-start | bytes 4423688 | tf_op jit(solution)/shard_map/cond/branch_0_fun/ppermute | solution.py:482
  19.7 24.3 %all-to-all-done.factor_ref = f32[8,296,128]{2,1,0:T(8,128)S(1)} async-done(((f32[8,296,128]{2,1,0:T(8,128)}), f32[8,296,128]{2,1,0:T(8,128)S(1)}, u32[]{:S(2)}, u32[]{:S(2)}) %all-to-all-start) | async-done | bytes 1212448 | tf_op jit(solution)/shard_map/cond/branch_0_fun/all_to_all | solution.py:501
  43.9 3.0 %load_columns.2.x_ref = f32[6,2,384,256]{3,2,1,0:T(8,128)S(1)} custom-call(s32[9,12]{1,0:T(8,128)S(1)} %get-tuple-element.23.table_ref, f32[12,384,256]{2,1,0:T(8,128)} %get-tuple-element.21.blocks_ref, f32[12,384,256]{2,1,0:T(8,128)} %collective-permute-done.1.core_ref), custom_call_target="tpu_custom_call" | custom-call | tf_op jit(solution)/shard_map/cond/branch_0_fun/load_columns/pallas_call | solution.py:505
  46.9 6.0 %gram_own.2 = (bf16[6,256,256]{2,1,0:T(8,128)(2,1)S(1)}, bf16[6,256,256]{2,1,0:T(8,128)(2,1)S(1)}, bf16[6,128,384]{2,1,0:T(8,128)(2,1)S(1)}, bf16[6,128,384]{2,1...) custom-call(s32[9,12]{1,0:T(8,128)S(1)} %get-tuple-element.23.table_, ...), custom_call_target="tpu_custom_call" | custom-call | tf_op jit(solution)/shard_map/cond/branch_0_fun/gram_own/pallas_call | solution.py:516
  53.5 6.4 %gram_y.2 = (bf16[2304,256]{1,0:T(8,128)(2,1)S(1)}, bf16[2304,256]{1,0:T(8,128)(2,1)S(1)}, f32[768,256]{1,0:T(8,128)S(1)}) custom-call(s32[9,12]{1,0:T(8,128)S(1)} %get-tuple-element.23.table_ref, f32[2880,128]{1,0:T(8,128)S(1)} %collective-permute-done.y_ref, bf16[6,256,256]{2,1,0:T(8,128)(2,1)S(1)} %get-tuple-element.26.upper_high, ...), custom_call_target="tpu_custom_call" | custom-call | tf_op jit(solution)/shard_map/cond/branch_0_fun/gram_y/pallas_call | solution.py:538
  59.9 4.3 %gram_rest.2 = (f32[4,80,256]{2,1,0:T(8,128)S(1)}, f32[4,80,256]{2,1,0:T(8,128)S(1)}, f32[4,80,256]{2,1,0:T(8,128)S(1)}, f32[4,80,256]{2,1,0:T(8,128)S(1)}, f32[...) custom-call(s32[9,12]{1,0:T(8,128)S(1)} %get-tuple-element.23.table_, ...), custom_call_target="tpu_custom_call" | custom-call | tf_op jit(solution)/shard_map/cond/branch_0_fun/gram_rest/pallas_call | solution.py:548
  64.9 2.3 %collective-permute-start.11 = (f32[2,2,48,256]{3,2,1,0:T(8,128)S(1)}, f32[2,2,48,256]{3,2,1,0:T(8,128)S(1)}, u32[]{:S(2)}, u32[]{:S(2)}) collective-permute-start(f32[2,2,48,256]{3,2,1,0:T(8,128)S(1)} %get-tuple-element.44), channel_id=1, source_target_pairs={{0,16},{1,17},{2,18},{3,19},{4,20},{5,21},{6,22},{7,23},{8,24},{9,... | collective-permute-start | bytes 589832 | tf_op jit(solution)/shard_map/cond/branch_0_fun/ppermute | solution.py:482
  67.2 1.5 %collective-permute-start.12 = (f32[2,2,48,256]{3,2,1,0:T(8,128)S(1)}, f32[2,2,48,256]{3,2,1,0:T(8,128)S(1)}, u32[]{:S(2)}, u32[]{:S(2)}) collective-permute-start(f32[2,2,48,256]{3,2,1,0:T(8,128)S(1)} %get-tuple-element.45), channel_id=1, source_target_pairs={{0,24},{1,25},{2,26},{3,27},{4,28},{5,29},{6,30},{7,31},{8,16},{9,... | collective-permute-start | bytes 589832 | tf_op jit(solution)/shard_map/cond/branch_0_fun/ppermute | solution.py:482
  68.6 1.5 %collective-permute-start.4 = (f32[4,80,256]{2,1,0:T(8,128)S(1)}, f32[4,80,256]{2,1,0:T(8,128)S(1)}, u32[]{:S(2)}, u32[]{:S(2)}) collective-permute-start(f32[4,80,256]{2,1,0:T(8,128)S(1)} %get-tuple-element.39), channel_id=1, source_target_pairs={{0,2},{1,3},{2,0},{3,1},{4,6},{5,7},{6,4},{7,5},{8,10},{9,11},{10,... | collective-permute-start | bytes 983048 | tf_op jit(solution)/shard_map/cond/branch_0_fun/ppermute | solution.py:482
  70.2 1.4 %collective-permute-start.5 = (f32[4,80,256]{2,1,0:T(8,128)S(1)}, f32[4,80,256]{2,1,0:T(8,128)S(1)}, u32[]{:S(2)}, u32[]{:S(2)}) collective-permute-start(f32[4,80,256]{2,1,0:T(8,128)S(1)} %get-tuple-element.40), channel_id=1, source_target_pairs={{0,4},{1,5},{2,6},{3,7},{4,0},{5,1},{6,2},{7,3},{8,12},{9,13},{10,... | collective-permute-start | bytes 983048 | tf_op jit(solution)/shard_map/cond/branch_0_fun/ppermute | solution.py:482
  71.6 3.2 %collective-permute-done.10 = f32[2,2,48,256]{3,2,1,0:T(8,128)S(1)} collective-permute-done((f32[2,2,48,256]{3,2,1,0:T(8,128)S(1)}, f32[2,2,48,256]{3,2,1,0:T(8,128)S(1)}, u32[]{:S(2)}, u32[]{:S(2)}) %collective-permute-start.10) | collective-permute-done | bytes 196640 | tf_op jit(solution)/shard_map/cond/branch_0_fun/ppermute | solution.py:482
  74.7 2.5 %collective-permute-start.6 = (f32[4,80,256]{2,1,0:T(8,128)S(1)}, f32[4,80,256]{2,1,0:T(8,128)S(1)}, u32[]{:S(2)}, u32[]{:S(2)}) collective-permute-start(f32[4,80,256]{2,1,0:T(8,128)S(1)} %get-tuple-element.41), channel_id=1, source_target_pairs={{0,6},{1,7},{2,4},{3,5},{4,2},{5,3},{6,0},{7,1},{8,14},{9,15},{10,... | collective-permute-start | bytes 983048 | tf_op jit(solution)/shard_map/cond/branch_0_fun/ppermute | solution.py:482
  77.2 4.7 %collective-permute-done.11 = f32[2,2,48,256]{3,2,1,0:T(8,128)S(1)} collective-permute-done((f32[2,2,48,256]{3,2,1,0:T(8,128)S(1)}, f32[2,2,48,256]{3,2,1,0:T(8,128)S(1)}, u32[]{:S(2)}, u32[]{:S(2)}) %collective-permute-start.11) | collective-permute-done | bytes 196640 | tf_op jit(solution)/shard_map/cond/branch_0_fun/ppermute | solution.py:482
  82.1 1.6 %collective-permute-start.13 = (f32[48,256]{1,0:T(8,128)S(1)}, f32[48,256]{1,0:T(8,128)S(1)}, u32[]{:S(2)}, u32[]{:S(2)}) collective-permute-start(f32[48,256]{1,0:T(8,128)S(1)} %get-tuple-element.84), channel_id=1, source_target_pairs={{0,2},{1,3},{2,0},{3,1},{4,6},{5,7},{6,4},{7,5},{8,10},{9,11},{10,... | collective-permute-start | bytes 147464 | tf_op jit(solution)/shard_map/cond/branch_0_fun/ppermute | solution.py:482
  83.7 1.4 %collective-permute-start.14 = (f32[48,256]{1,0:T(8,128)S(1)}, f32[48,256]{1,0:T(8,128)S(1)}, u32[]{:S(2)}, u32[]{:S(2)}) collective-permute-start(f32[48,256]{1,0:T(8,128)S(1)} %get-tuple-element.82), channel_id=1, source_target_pairs={{0,4},{1,5},{2,6},{3,7},{4,0},{5,1},{6,2},{7,3},{8,12},{9,13},{10,... | collective-permute-start | bytes 147464 | tf_op jit(solution)/shard_map/cond/branch_0_fun/ppermute | solution.py:482
  86.3 3.6 %collective-permute-start.7 = (f32[80,256]{1,0:T(8,128)S(1)}, f32[80,256]{1,0:T(8,128)S(1)}, u32[]{:S(2)}, u32[]{:S(2)}) collective-permute-start(f32[80,256]{1,0:T(8,128)S(1)} %get-tuple-element.81), channel_id=1, source_target_pairs={{0,8},{1,9},{2,10},{3,11},{4,12},{5,13},{6,14},{7,15},{8,0},{9,1},... | collective-permute-start | bytes 245768 | tf_op jit(solution)/shard_map/cond/branch_0_fun/ppermute | solution.py:482
  89.9 0.9 collective-permute-start.8
  90.7 1.6 %collective-permute-start.9 = (f32[80,256]{1,0:T(8,128)S(1)}, f32[80,256]{1,0:T(8,128)S(1)}, u32[]{:S(2)}, u32[]{:S(2)}) collective-permute-start(f32[80,256]{1,0:T(8,128)S(1)} %get-tuple-element.80), channel_id=1, source_target_pairs={{0,24},{1,25},{2,26},{3,27},{4,28},{5,29},{6,30},{7,31},{8,16},{9,... | collective-permute-start | bytes 245768 | tf_op jit(solution)/shard_map/cond/branch_0_fun/ppermute | solution.py:482
  92.9 4.9 %collective-permute-done.8 = f32[80,256]{1,0:T(8,128)S(1)} collective-permute-done((f32[80,256]{1,0:T(8,128)S(1)}, f32[80,256]{1,0:T(8,128)S(1)}, u32[]{:S(2)}, u32[]{:S(2)}) %collective-permute-start.8) | collective-permute-done | bytes 81952 | tf_op jit(solution)/shard_map/cond/branch_0_fun/ppermute | solution.py:482
  (26 shorter events, 3.8 us)
Async XLA Ops:
  6.7 37.3 %collective-permute-start.1 = (f32[12,384,256]{2,1,0:T(8,128)}, f32[12,384,256]{2,1,0:T(8,128)}, u32[]{:S(2)}, u32[]{:S(2)}) collective-permute-start(f32[12,384,256]{2,1,0:T(8,128)} %get-tuple-element.21.blocks_ref), channel_id=1, source_target_pairs={{0,1},{1,0},{2,3},{3,2},{4,5},{5,4},{6,7},{7,6},{8,9},{9,8},{10,11... | collective-permute-start | bytes 14155784 | tf_op jit(solution)/shard_map/cond/branch_0_fun/ppermute | solution.py:482
  7.8 36.2 %all-to-all-start = ((f32[8,296,128]{2,1,0:T(8,128)}), f32[8,296,128]{2,1,0:T(8,128)S(1)}, u32[]{:S(2)}, u32[]{:S(2)}) async-start(f32[8,296,128]{2,1,0:T(8,128)} %get-tuple-element.22), calls=%async_computation | async-start | bytes 2424832 | tf_op jit(solution)/shard_map/cond/branch_0_fun/all_to_all | solution.py:501
  18.0 35.0 %collective-permute-start = (f32[2880,128]{1,0:T(8,128)}, f32[2880,128]{1,0:T(8,128)S(1)}, u32[]{:S(2)}, u32[]{:S(2)}) collective-permute-start(f32[2880,128]{1,0:T(8,128)} %pack_rows.2), channel_id=1, source_target_pairs={{0,2},{1,3},{2,0},{3,1},{4,6},{5,7},{6,4},{7,5},{8,10},{9,11},{10,... | collective-permute-start | bytes 4423688 | tf_op jit(solution)/shard_map/cond/branch_0_fun/ppermute | solution.py:482
  43.9 3.0 %collective-permute-start.2 = (f32[8,296,128]{2,1,0:T(8,128)S(1)}, f32[8,296,128]{2,1,0:T(8,128)S(1)}, u32[]{:S(2)}, u32[]{:S(2)}) collective-permute-start(f32[8,296,128]{2,1,0:T(8,128)S(1)} %all-to-all-done.factor_ref), channel_id=1, source_target_pairs={{0,1},{1,0},{2,3},{3,2},{4,5},{5,4},{6,7},{7,6},{8,9},{9,8},{10,11... | collective-permute-start | bytes 3637256 | tf_op jit(solution)/shard_map/cond/branch_0_fun/ppermute | solution.py:482
  52.9 7.0 %collective-permute-start.3 = (f32[2880,128]{1,0:T(8,128)S(1)}, f32[2880,128]{1,0:T(8,128)S(1)}, u32[]{:S(2)}, u32[]{:S(2)}) collective-permute-start(f32[2880,128]{1,0:T(8,128)S(1)} %collective-permute-done.y_ref), channel_id=1, source_target_pairs={{0,1},{1,0},{2,3},{3,2},{4,5},{5,4},{6,7},{7,6},{8,9},{9,8},{10,11... | collective-permute-start | bytes 4423688 | tf_op jit(solution)/shard_map/cond/branch_0_fun/ppermute | solution.py:482
  64.2 10.6 %collective-permute-start.10 = (f32[2,2,48,256]{3,2,1,0:T(8,128)S(1)}, f32[2,2,48,256]{3,2,1,0:T(8,128)S(1)}, u32[]{:S(2)}, u32[]{:S(2)}) collective-permute-start(f32[2,2,48,256]{3,2,1,0:T(8,128)S(1)} %get-tuple-element.43), channel_id=1, source_target_pairs={{0,8},{1,9},{2,10},{3,11},{4,12},{5,13},{6,14},{7,15},{8,0},{9,1},... | collective-permute-start | bytes 589832 | tf_op jit(solution)/shard_map/cond/branch_0_fun/ppermute | solution.py:482
  64.9 17.1 %collective-permute-start.11 = (f32[2,2,48,256]{3,2,1,0:T(8,128)S(1)}, f32[2,2,48,256]{3,2,1,0:T(8,128)S(1)}, u32[]{:S(2)}, u32[]{:S(2)}) collective-permute-start(f32[2,2,48,256]{3,2,1,0:T(8,128)S(1)} %get-tuple-element.44), channel_id=1, source_target_pairs={{0,16},{1,17},{2,18},{3,19},{4,20},{5,21},{6,22},{7,23},{8,24},{9,... | collective-permute-start | bytes 589832 | tf_op jit(solution)/shard_map/cond/branch_0_fun/ppermute | solution.py:482
  67.2 14.8 %collective-permute-start.12 = (f32[2,2,48,256]{3,2,1,0:T(8,128)S(1)}, f32[2,2,48,256]{3,2,1,0:T(8,128)S(1)}, u32[]{:S(2)}, u32[]{:S(2)}) collective-permute-start(f32[2,2,48,256]{3,2,1,0:T(8,128)S(1)} %get-tuple-element.45), channel_id=1, source_target_pairs={{0,24},{1,25},{2,26},{3,27},{4,28},{5,29},{6,30},{7,31},{8,16},{9,... | collective-permute-start | bytes 589832 | tf_op jit(solution)/shard_map/cond/branch_0_fun/ppermute | solution.py:482
  68.6 16.4 %collective-permute-start.4 = (f32[4,80,256]{2,1,0:T(8,128)S(1)}, f32[4,80,256]{2,1,0:T(8,128)S(1)}, u32[]{:S(2)}, u32[]{:S(2)}) collective-permute-start(f32[4,80,256]{2,1,0:T(8,128)S(1)} %get-tuple-element.39), channel_id=1, source_target_pairs={{0,2},{1,3},{2,0},{3,1},{4,6},{5,7},{6,4},{7,5},{8,10},{9,11},{10,... | collective-permute-start | bytes 983048 | tf_op jit(solution)/shard_map/cond/branch_0_fun/ppermute | solution.py:482
  70.2 15.5 %collective-permute-start.5 = (f32[4,80,256]{2,1,0:T(8,128)S(1)}, f32[4,80,256]{2,1,0:T(8,128)S(1)}, u32[]{:S(2)}, u32[]{:S(2)}) collective-permute-start(f32[4,80,256]{2,1,0:T(8,128)S(1)} %get-tuple-element.40), channel_id=1, source_target_pairs={{0,4},{1,5},{2,6},{3,7},{4,0},{5,1},{6,2},{7,3},{8,12},{9,13},{10,... | collective-permute-start | bytes 983048 | tf_op jit(solution)/shard_map/cond/branch_0_fun/ppermute | solution.py:482
  74.7 11.4 %collective-permute-start.6 = (f32[4,80,256]{2,1,0:T(8,128)S(1)}, f32[4,80,256]{2,1,0:T(8,128)S(1)}, u32[]{:S(2)}, u32[]{:S(2)}) collective-permute-start(f32[4,80,256]{2,1,0:T(8,128)S(1)} %get-tuple-element.41), channel_id=1, source_target_pairs={{0,6},{1,7},{2,4},{3,5},{4,2},{5,3},{6,0},{7,1},{8,14},{9,15},{10,... | collective-permute-start | bytes 983048 | tf_op jit(solution)/shard_map/cond/branch_0_fun/ppermute | solution.py:482
  82.1 8.7 %collective-permute-start.13 = (f32[48,256]{1,0:T(8,128)S(1)}, f32[48,256]{1,0:T(8,128)S(1)}, u32[]{:S(2)}, u32[]{:S(2)}) collective-permute-start(f32[48,256]{1,0:T(8,128)S(1)} %get-tuple-element.84), channel_id=1, source_target_pairs={{0,2},{1,3},{2,0},{3,1},{4,6},{5,7},{6,4},{7,5},{8,10},{9,11},{10,... | collective-permute-start | bytes 147464 | tf_op jit(solution)/shard_map/cond/branch_0_fun/ppermute | solution.py:482
  83.7 8.6 %collective-permute-start.14 = (f32[48,256]{1,0:T(8,128)S(1)}, f32[48,256]{1,0:T(8,128)S(1)}, u32[]{:S(2)}, u32[]{:S(2)}) collective-permute-start(f32[48,256]{1,0:T(8,128)S(1)} %get-tuple-element.82), channel_id=1, source_target_pairs={{0,4},{1,5},{2,6},{3,7},{4,0},{5,1},{6,2},{7,3},{8,12},{9,13},{10,... | collective-permute-start | bytes 147464 | tf_op jit(solution)/shard_map/cond/branch_0_fun/ppermute | solution.py:482
  85.1 7.3 %collective-permute-start.15 = (f32[48,256]{1,0:T(8,128)S(1)}, f32[48,256]{1,0:T(8,128)S(1)}, u32[]{:S(2)}, u32[]{:S(2)}) collective-permute-start(f32[48,256]{1,0:T(8,128)S(1)} %get-tuple-element.83), channel_id=1, source_target_pairs={{0,6},{1,7},{2,4},{3,5},{4,2},{5,3},{6,0},{7,1},{8,14},{9,15},{10,... | collective-permute-start | bytes 147464 | tf_op jit(solution)/shard_map/cond/branch_0_fun/ppermute | solution.py:482
  86.3 6.6 %collective-permute-start.7 = (f32[80,256]{1,0:T(8,128)S(1)}, f32[80,256]{1,0:T(8,128)S(1)}, u32[]{:S(2)}, u32[]{:S(2)}) collective-permute-start(f32[80,256]{1,0:T(8,128)S(1)} %get-tuple-element.81), channel_id=1, source_target_pairs={{0,8},{1,9},{2,10},{3,11},{4,12},{5,13},{6,14},{7,15},{8,0},{9,1},... | collective-permute-start | bytes 245768 | tf_op jit(solution)/shard_map/cond/branch_0_fun/ppermute | solution.py:482
  89.9 7.9 %collective-permute-start.8 = (f32[80,256]{1,0:T(8,128)S(1)}, f32[80,256]{1,0:T(8,128)S(1)}, u32[]{:S(2)}, u32[]{:S(2)}) collective-permute-start(f32[80,256]{1,0:T(8,128)S(1)} %get-tuple-element.79), channel_id=1, source_target_pairs={{0,16},{1,17},{2,18},{3,19},{4,20},{5,21},{6,22},{7,23},{8,24},{9,... | collective-permute-start | bytes 245768 | tf_op jit(solution)/shard_map/cond/branch_0_fun/ppermute | solution.py:482
  90.7 7.1 %collective-permute-start.9 = (f32[80,256]{1,0:T(8,128)S(1)}, f32[80,256]{1,0:T(8,128)S(1)}, u32[]{:S(2)}, u32[]{:S(2)}) collective-permute-start(f32[80,256]{1,0:T(8,128)S(1)} %get-tuple-element.80), channel_id=1, source_target_pairs={{0,24},{1,25},{2,26},{3,27},{4,28},{5,29},{6,30},{7,31},{8,16},{9,... | collective-permute-start | bytes 245768 | tf_op jit(solution)/shard_map/cond/branch_0_fun/ppermute | solution.py:482
  98.1 0.7 copy-start

commit v9 on v8

--- a/solution.py
+++ b/solution.py
@@ -11,7 +11,7 @@
 F32 = jnp.float32
 BF16 = jnp.bfloat16
 XY_FIRST = 80
-VMEM_LIMIT = 24 << 20
+VMEM_LIMIT = 16 << 20
 
 
 def general_body(blocks, orders, pattern, dest, inv_factor):

time: 99 us -> 99 us (level)
  no operation moved by 1% of the time
where the time goes in v9:
time: 99 us; the launch traced here: 98.7 us
  waiting for transfers between devices  38.4 us (39%)
  Pallas kernels  29.3 us (30%)
  starting transfers between devices  29.1 us (29%)
    all_to_all x1, waiting for transfers between devices, paired_rest(): lax.all_to_all(factor_send, 'blk', split_axis=0, concat_axis=0, tiled=True)  24.3 us
    ppermute x16, starting transfers between devices, exchange(): return lax.ppermute(value, axes, perm)  22.5 us
    ppermute x16, waiting for transfers between devices, exchange(): return lax.ppermute(value, axes, perm)  14.1 us
    all_to_all x1, starting transfers between devices, paired_rest(): lax.all_to_all(factor_send, 'blk', split_axis=0, concat_axis=0, tiled=True)  6.63 us
    pallas_call x1, Pallas kernels, paired_rest(): pl.pallas_call(gram_y, out_shape=(shape((depth, width), BF16), shape((dep...  6.36 us
    pallas_call x1, Pallas kernels, paired_body(): pl.pallas_call(plan, out_shape=(shape((n_blk, FACTOR_ROWS, CTW), F32), sh...  5.99 us
    pallas_call x1, Pallas kernels, paired_rest(): pl.pallas_call(gram_own, out_shape=(shape((half, 256, 256), BF16), shape(...  5.98 us
    pallas_call x1, Pallas kernels, paired_rest(): pl.pallas_call(gram_rest, out_shape=(shape(first_shape, F32),) * 4 + (sha...  4.28 us
  transfers between devices with their start and end apart: 17, of which 6 were waited for; matrix products, arithmetic and copies ran while one was open for 0% of the time, Pallas kernels for 19%

profile of v9, /device:TPU:0, one launch (start us, length us, event | category | flops | bytes accessed | tf_op | source)
XLA Modules:
  0.0 98.7 jit_solution(2646770975223764283)
XLA Ops:
  0.0 6.0 %plan.1 = (f32[8,296,128]{2,1,0:T(8,128)}, s32[9,12]{1,0:T(8,128)S(1)}, s32[1]{0:T(128)}) custom-call(s32[96]{0:T(128)} %dest_hbm.1, s32[96]{0:T(128)} %orders_hbm.1, s32[8,96]{1,0:T(8,128)} %bitcast.42, f32[12,384,384]{2,1,0:T(8,128)} %inv_ref.1), custom_call_target="tpu_custom_call" | custom-call | tf_op jit(solution)/shard_map/plan/pallas_call | solution.py:438
  6.6 91.4 %conditional.1 = (f32[128,256]{1,0:T(8,128)S(1)}) conditional(s32[]{:T(128)} %bitcast.17, (s32[9,12]{1,0:T(8,128)S(1)}, f32[12,384,256]{2,1,0:T(8,128)}, f32[8,296,128]{2,1,0:T(8,128)}) %tuple.15, (s32[9,12]{1,0:T(8,128)S(1)}, f32[12,384,256]{2,1,0:T(8,128)}, f32[8,296,128]{2,1,0:T(8,128)}) %tuple.15), branch_computations={%region_0.0_spmd, %region_1.0_spmd} | conditional | flops 557056 | bytes 58426024 | solution.py:467
  6.7 1.1 %collective-permute-start.1 = (f32[12,384,256]{2,1,0:T(8,128)}, f32[12,384,256]{2,1,0:T(8,128)}, u32[]{:S(2)}, u32[]{:S(2)}) collective-permute-start(f32[12,384,256]{2,1,0:T(8,128)} %get-tuple-element.21.blocks_ref), channel_id=1, source_target_pairs={{0,1},{1,0},{2,3},{3,2},{4,5},{5,4},{6,7},{7,6},{8,9},{9,8},{10,11... | collective-permute-start | bytes 14155784 | tf_op jit(solution)/shard_map/cond/branch_0_fun/ppermute | solution.py:482
  7.8 6.6 %all-to-all-start = ((f32[8,296,128]{2,1,0:T(8,128)}), f32[8,296,128]{2,1,0:T(8,128)S(1)}, u32[]{:S(2)}, u32[]{:S(2)}) async-start(f32[8,296,128]{2,1,0:T(8,128)} %get-tuple-element.22), calls=%async_computation | async-start | bytes 2424832 | tf_op jit(solution)/shard_map/cond/branch_0_fun/all_to_all | solution.py:501
  14.4 3.7 %pack_rows.2 = f32[2880,128]{1,0:T(8,128)} custom-call(s32[9,12]{1,0:T(8,128)S(1)} %get-tuple-element.23.table_ref, f32[12,384,256]{2,1,0:T(8,128)} %get-tuple-element.21.blocks_ref), custom_call_target="tpu_custom_call" | custom-call | tf_op jit(solution)/shard_map/cond/branch_0_fun/pack_rows/pallas_call | solution.py:491
  18.1 1.5 %collective-permute-start = (f32[2880,128]{1,0:T(8,128)}, f32[2880,128]{1,0:T(8,128)S(1)}, u32[]{:S(2)}, u32[]{:S(2)}) collective-permute-start(f32[2880,128]{1,0:T(8,128)} %pack_rows.2), channel_id=1, source_target_pairs={{0,2},{1,3},{2,0},{3,1},{4,6},{5,7},{6,4},{7,5},{8,10},{9,11},{10,... | collective-permute-start | bytes 4423688 | tf_op jit(solution)/shard_map/cond/branch_0_fun/ppermute | solution.py:482
  19.6 24.3 %all-to-all-done.factor_ref = f32[8,296,128]{2,1,0:T(8,128)S(1)} async-done(((f32[8,296,128]{2,1,0:T(8,128)}), f32[8,296,128]{2,1,0:T(8,128)S(1)}, u32[]{:S(2)}, u32[]{:S(2)}) %all-to-all-start) | async-done | bytes 1212448 | tf_op jit(solution)/shard_map/cond/branch_0_fun/all_to_all | solution.py:501
  43.9 3.0 %load_columns.2.x_ref = f32[6,2,384,256]{3,2,1,0:T(8,128)S(1)} custom-call(s32[9,12]{1,0:T(8,128)S(1)} %get-tuple-element.23.table_ref, f32[12,384,256]{2,1,0:T(8,128)} %get-tuple-element.21.blocks_ref, f32[12,384,256]{2,1,0:T(8,128)} %collective-permute-done.1.core_ref), custom_call_target="tpu_custom_call" | custom-call | tf_op jit(solution)/shard_map/cond/branch_0_fun/load_columns/pallas_call | solution.py:505
  46.9 6.0 %gram_own.2 = (bf16[6,256,256]{2,1,0:T(8,128)(2,1)S(1)}, bf16[6,256,256]{2,1,0:T(8,128)(2,1)S(1)}, bf16[6,128,384]{2,1,0:T(8,128)(2,1)S(1)}, bf16[6,128,384]{2,1...) custom-call(s32[9,12]{1,0:T(8,128)S(1)} %get-tuple-element.23.table_, ...), custom_call_target="tpu_custom_call" | custom-call | tf_op jit(solution)/shard_map/cond/branch_0_fun/gram_own/pallas_call | solution.py:516
  53.5 6.4 %gram_y.2 = (bf16[2304,256]{1,0:T(8,128)(2,1)S(1)}, bf16[2304,256]{1,0:T(8,128)(2,1)S(1)}, f32[768,256]{1,0:T(8,128)S(1)}) custom-call(s32[9,12]{1,0:T(8,128)S(1)} %get-tuple-element.23.table_ref, f32[2880,128]{1,0:T(8,128)S(1)} %collective-permute-done.y_ref, bf16[6,256,256]{2,1,0:T(8,128)(2,1)S(1)} %get-tuple-element.26.upper_high, ...), custom_call_target="tpu_custom_call" | custom-call | tf_op jit(solution)/shard_map/cond/branch_0_fun/gram_y/pallas_call | solution.py:538
  59.9 4.3 %gram_rest.2 = (f32[4,80,256]{2,1,0:T(8,128)S(1)}, f32[4,80,256]{2,1,0:T(8,128)S(1)}, f32[4,80,256]{2,1,0:T(8,128)S(1)}, f32[4,80,256]{2,1,0:T(8,128)S(1)}, f32[...) custom-call(s32[9,12]{1,0:T(8,128)S(1)} %get-tuple-element.23.table_, ...), custom_call_target="tpu_custom_call" | custom-call | tf_op jit(solution)/shard_map/cond/branch_0_fun/gram_rest/pallas_call | solution.py:548
  64.8 2.4 %collective-permute-start.11 = (f32[2,2,48,256]{3,2,1,0:T(8,128)S(1)}, f32[2,2,48,256]{3,2,1,0:T(8,128)S(1)}, u32[]{:S(2)}, u32[]{:S(2)}) collective-permute-start(f32[2,2,48,256]{3,2,1,0:T(8,128)S(1)} %get-tuple-element.44), channel_id=1, source_target_pairs={{0,16},{1,17},{2,18},{3,19},{4,20},{5,21},{6,22},{7,23},{8,24},{9,... | collective-permute-start | bytes 589832 | tf_op jit(solution)/shard_map/cond/branch_0_fun/ppermute | solution.py:482
  67.2 1.4 %collective-permute-start.12 = (f32[2,2,48,256]{3,2,1,0:T(8,128)S(1)}, f32[2,2,48,256]{3,2,1,0:T(8,128)S(1)}, u32[]{:S(2)}, u32[]{:S(2)}) collective-permute-start(f32[2,2,48,256]{3,2,1,0:T(8,128)S(1)} %get-tuple-element.45), channel_id=1, source_target_pairs={{0,24},{1,25},{2,26},{3,27},{4,28},{5,29},{6,30},{7,31},{8,16},{9,... | collective-permute-start | bytes 589832 | tf_op jit(solution)/shard_map/cond/branch_0_fun/ppermute | solution.py:482
  68.6 1.5 %collective-permute-start.4 = (f32[4,80,256]{2,1,0:T(8,128)S(1)}, f32[4,80,256]{2,1,0:T(8,128)S(1)}, u32[]{:S(2)}, u32[]{:S(2)}) collective-permute-start(f32[4,80,256]{2,1,0:T(8,128)S(1)} %get-tuple-element.39), channel_id=1, source_target_pairs={{0,2},{1,3},{2,0},{3,1},{4,6},{5,7},{6,4},{7,5},{8,10},{9,11},{10,... | collective-permute-start | bytes 983048 | tf_op jit(solution)/shard_map/cond/branch_0_fun/ppermute | solution.py:482
  70.2 1.4 %collective-permute-start.5 = (f32[4,80,256]{2,1,0:T(8,128)S(1)}, f32[4,80,256]{2,1,0:T(8,128)S(1)}, u32[]{:S(2)}, u32[]{:S(2)}) collective-permute-start(f32[4,80,256]{2,1,0:T(8,128)S(1)} %get-tuple-element.40), channel_id=1, source_target_pairs={{0,4},{1,5},{2,6},{3,7},{4,0},{5,1},{6,2},{7,3},{8,12},{9,13},{10,... | collective-permute-start | bytes 983048 | tf_op jit(solution)/shard_map/cond/branch_0_fun/ppermute | solution.py:482
  71.6 3.3 %collective-permute-done.10 = f32[2,2,48,256]{3,2,1,0:T(8,128)S(1)} collective-permute-done((f32[2,2,48,256]{3,2,1,0:T(8,128)S(1)}, f32[2,2,48,256]{3,2,1,0:T(8,128)S(1)}, u32[]{:S(2)}, u32[]{:S(2)}) %collective-permute-start.10) | collective-permute-done | bytes 196640 | tf_op jit(solution)/shard_map/cond/branch_0_fun/ppermute | solution.py:482
  74.8 2.4 %collective-permute-start.6 = (f32[4,80,256]{2,1,0:T(8,128)S(1)}, f32[4,80,256]{2,1,0:T(8,128)S(1)}, u32[]{:S(2)}, u32[]{:S(2)}) collective-permute-start(f32[4,80,256]{2,1,0:T(8,128)S(1)} %get-tuple-element.41), channel_id=1, source_target_pairs={{0,6},{1,7},{2,4},{3,5},{4,2},{5,3},{6,0},{7,1},{8,14},{9,15},{10,... | collective-permute-start | bytes 983048 | tf_op jit(solution)/shard_map/cond/branch_0_fun/ppermute | solution.py:482
  77.2 4.7 %collective-permute-done.11 = f32[2,2,48,256]{3,2,1,0:T(8,128)S(1)} collective-permute-done((f32[2,2,48,256]{3,2,1,0:T(8,128)S(1)}, f32[2,2,48,256]{3,2,1,0:T(8,128)S(1)}, u32[]{:S(2)}, u32[]{:S(2)}) %collective-permute-start.11) | collective-permute-done | bytes 196640 | tf_op jit(solution)/shard_map/cond/branch_0_fun/ppermute | solution.py:482
  82.0 1.4 %collective-permute-start.13 = (f32[48,256]{1,0:T(8,128)S(1)}, f32[48,256]{1,0:T(8,128)S(1)}, u32[]{:S(2)}, u32[]{:S(2)}) collective-permute-start(f32[48,256]{1,0:T(8,128)S(1)} %get-tuple-element.84), channel_id=1, source_target_pairs={{0,2},{1,3},{2,0},{3,1},{4,6},{5,7},{6,4},{7,5},{8,10},{9,11},{10,... | collective-permute-start | bytes 147464 | tf_op jit(solution)/shard_map/cond/branch_0_fun/ppermute | solution.py:482
  83.5 1.6 %collective-permute-start.14 = (f32[48,256]{1,0:T(8,128)S(1)}, f32[48,256]{1,0:T(8,128)S(1)}, u32[]{:S(2)}, u32[]{:S(2)}) collective-permute-start(f32[48,256]{1,0:T(8,128)S(1)} %get-tuple-element.82), channel_id=1, source_target_pairs={{0,4},{1,5},{2,6},{3,7},{4,0},{5,1},{6,2},{7,3},{8,12},{9,13},{10,... | collective-permute-start | bytes 147464 | tf_op jit(solution)/shard_map/cond/branch_0_fun/ppermute | solution.py:482
  86.3 3.5 %collective-permute-start.7 = (f32[80,256]{1,0:T(8,128)S(1)}, f32[80,256]{1,0:T(8,128)S(1)}, u32[]{:S(2)}, u32[]{:S(2)}) collective-permute-start(f32[80,256]{1,0:T(8,128)S(1)} %get-tuple-element.81), channel_id=1, source_target_pairs={{0,8},{1,9},{2,10},{3,11},{4,12},{5,13},{6,14},{7,15},{8,0},{9,1},... | collective-permute-start | bytes 245768 | tf_op jit(solution)/shard_map/cond/branch_0_fun/ppermute | solution.py:482
  89.8 1.0 collective-permute-start.8
  90.8 1.5 %collective-permute-start.9 = (f32[80,256]{1,0:T(8,128)S(1)}, f32[80,256]{1,0:T(8,128)S(1)}, u32[]{:S(2)}, u32[]{:S(2)}) collective-permute-start(f32[80,256]{1,0:T(8,128)S(1)} %get-tuple-element.80), channel_id=1, source_target_pairs={{0,24},{1,25},{2,26},{3,27},{4,28},{5,29},{6,30},{7,31},{8,16},{9,... | collective-permute-start | bytes 245768 | tf_op jit(solution)/shard_map/cond/branch_0_fun/ppermute | solution.py:482
  92.9 4.8 %collective-permute-done.8 = f32[80,256]{1,0:T(8,128)S(1)} collective-permute-done((f32[80,256]{1,0:T(8,128)S(1)}, f32[80,256]{1,0:T(8,128)S(1)}, u32[]{:S(2)}, u32[]{:S(2)}) %collective-permute-start.8) | collective-permute-done | bytes 81952 | tf_op jit(solution)/shard_map/cond/branch_0_fun/ppermute | solution.py:482
  (26 shorter events, 3.9 us)
Async XLA Ops:
  6.7 37.3 %collective-permute-start.1 = (f32[12,384,256]{2,1,0:T(8,128)}, f32[12,384,256]{2,1,0:T(8,128)}, u32[]{:S(2)}, u32[]{:S(2)}) collective-permute-start(f32[12,384,256]{2,1,0:T(8,128)} %get-tuple-element.21.blocks_ref), channel_id=1, source_target_pairs={{0,1},{1,0},{2,3},{3,2},{4,5},{5,4},{6,7},{7,6},{8,9},{9,8},{10,11... | collective-permute-start | bytes 14155784 | tf_op jit(solution)/shard_map/cond/branch_0_fun/ppermute | solution.py:482
  7.8 36.2 %all-to-all-start = ((f32[8,296,128]{2,1,0:T(8,128)}), f32[8,296,128]{2,1,0:T(8,128)S(1)}, u32[]{:S(2)}, u32[]{:S(2)}) async-start(f32[8,296,128]{2,1,0:T(8,128)} %get-tuple-element.22), calls=%async_computation | async-start | bytes 2424832 | tf_op jit(solution)/shard_map/cond/branch_0_fun/all_to_all | solution.py:501
  18.1 34.9 %collective-permute-start = (f32[2880,128]{1,0:T(8,128)}, f32[2880,128]{1,0:T(8,128)S(1)}, u32[]{:S(2)}, u32[]{:S(2)}) collective-permute-start(f32[2880,128]{1,0:T(8,128)} %pack_rows.2), channel_id=1, source_target_pairs={{0,2},{1,3},{2,0},{3,1},{4,6},{5,7},{6,4},{7,5},{8,10},{9,11},{10,... | collective-permute-start | bytes 4423688 | tf_op jit(solution)/shard_map/cond/branch_0_fun/ppermute | solution.py:482
  43.9 3.0 %collective-permute-start.2 = (f32[8,296,128]{2,1,0:T(8,128)S(1)}, f32[8,296,128]{2,1,0:T(8,128)S(1)}, u32[]{:S(2)}, u32[]{:S(2)}) collective-permute-start(f32[8,296,128]{2,1,0:T(8,128)S(1)} %all-to-all-done.factor_ref), channel_id=1, source_target_pairs={{0,1},{1,0},{2,3},{3,2},{4,5},{5,4},{6,7},{7,6},{8,9},{9,8},{10,11... | collective-permute-start | bytes 3637256 | tf_op jit(solution)/shard_map/cond/branch_0_fun/ppermute | solution.py:482
  52.9 7.0 %collective-permute-start.3 = (f32[2880,128]{1,0:T(8,128)S(1)}, f32[2880,128]{1,0:T(8,128)S(1)}, u32[]{:S(2)}, u32[]{:S(2)}) collective-permute-start(f32[2880,128]{1,0:T(8,128)S(1)} %collective-permute-done.y_ref), channel_id=1, source_target_pairs={{0,1},{1,0},{2,3},{3,2},{4,5},{5,4},{6,7},{7,6},{8,9},{9,8},{10,11... | collective-permute-start | bytes 4423688 | tf_op jit(solution)/shard_map/cond/branch_0_fun/ppermute | solution.py:482
  64.2 10.6 %collective-permute-start.10 = (f32[2,2,48,256]{3,2,1,0:T(8,128)S(1)}, f32[2,2,48,256]{3,2,1,0:T(8,128)S(1)}, u32[]{:S(2)}, u32[]{:S(2)}) collective-permute-start(f32[2,2,48,256]{3,2,1,0:T(8,128)S(1)} %get-tuple-element.43), channel_id=1, source_target_pairs={{0,8},{1,9},{2,10},{3,11},{4,12},{5,13},{6,14},{7,15},{8,0},{9,1},... | collective-permute-start | bytes 589832 | tf_op jit(solution)/shard_map/cond/branch_0_fun/ppermute | solution.py:482
  64.8 17.1 %collective-permute-start.11 = (f32[2,2,48,256]{3,2,1,0:T(8,128)S(1)}, f32[2,2,48,256]{3,2,1,0:T(8,128)S(1)}, u32[]{:S(2)}, u32[]{:S(2)}) collective-permute-start(f32[2,2,48,256]{3,2,1,0:T(8,128)S(1)} %get-tuple-element.44), channel_id=1, source_target_pairs={{0,16},{1,17},{2,18},{3,19},{4,20},{5,21},{6,22},{7,23},{8,24},{9,... | collective-permute-start | bytes 589832 | tf_op jit(solution)/shard_map/cond/branch_0_fun/ppermute | solution.py:482
  67.2 14.7 %collective-permute-start.12 = (f32[2,2,48,256]{3,2,1,0:T(8,128)S(1)}, f32[2,2,48,256]{3,2,1,0:T(8,128)S(1)}, u32[]{:S(2)}, u32[]{:S(2)}) collective-permute-start(f32[2,2,48,256]{3,2,1,0:T(8,128)S(1)} %get-tuple-element.45), channel_id=1, source_target_pairs={{0,24},{1,25},{2,26},{3,27},{4,28},{5,29},{6,30},{7,31},{8,16},{9,... | collective-permute-start | bytes 589832 | tf_op jit(solution)/shard_map/cond/branch_0_fun/ppermute | solution.py:482
  68.6 16.4 %collective-permute-start.4 = (f32[4,80,256]{2,1,0:T(8,128)S(1)}, f32[4,80,256]{2,1,0:T(8,128)S(1)}, u32[]{:S(2)}, u32[]{:S(2)}) collective-permute-start(f32[4,80,256]{2,1,0:T(8,128)S(1)} %get-tuple-element.39), channel_id=1, source_target_pairs={{0,2},{1,3},{2,0},{3,1},{4,6},{5,7},{6,4},{7,5},{8,10},{9,11},{10,... | collective-permute-start | bytes 983048 | tf_op jit(solution)/shard_map/cond/branch_0_fun/ppermute | solution.py:482
  70.2 15.4 %collective-permute-start.5 = (f32[4,80,256]{2,1,0:T(8,128)S(1)}, f32[4,80,256]{2,1,0:T(8,128)S(1)}, u32[]{:S(2)}, u32[]{:S(2)}) collective-permute-start(f32[4,80,256]{2,1,0:T(8,128)S(1)} %get-tuple-element.40), channel_id=1, source_target_pairs={{0,4},{1,5},{2,6},{3,7},{4,0},{5,1},{6,2},{7,3},{8,12},{9,13},{10,... | collective-permute-start | bytes 983048 | tf_op jit(solution)/shard_map/cond/branch_0_fun/ppermute | solution.py:482
  74.8 11.4 %collective-permute-start.6 = (f32[4,80,256]{2,1,0:T(8,128)S(1)}, f32[4,80,256]{2,1,0:T(8,128)S(1)}, u32[]{:S(2)}, u32[]{:S(2)}) collective-permute-start(f32[4,80,256]{2,1,0:T(8,128)S(1)} %get-tuple-element.41), channel_id=1, source_target_pairs={{0,6},{1,7},{2,4},{3,5},{4,2},{5,3},{6,0},{7,1},{8,14},{9,15},{10,... | collective-permute-start | bytes 983048 | tf_op jit(solution)/shard_map/cond/branch_0_fun/ppermute | solution.py:482
  82.0 8.8 %collective-permute-start.13 = (f32[48,256]{1,0:T(8,128)S(1)}, f32[48,256]{1,0:T(8,128)S(1)}, u32[]{:S(2)}, u32[]{:S(2)}) collective-permute-start(f32[48,256]{1,0:T(8,128)S(1)} %get-tuple-element.84), channel_id=1, source_target_pairs={{0,2},{1,3},{2,0},{3,1},{4,6},{5,7},{6,4},{7,5},{8,10},{9,11},{10,... | collective-permute-start | bytes 147464 | tf_op jit(solution)/shard_map/cond/branch_0_fun/ppermute | solution.py:482
  83.5 8.8 %collective-permute-start.14 = (f32[48,256]{1,0:T(8,128)S(1)}, f32[48,256]{1,0:T(8,128)S(1)}, u32[]{:S(2)}, u32[]{:S(2)}) collective-permute-start(f32[48,256]{1,0:T(8,128)S(1)} %get-tuple-element.82), channel_id=1, source_target_pairs={{0,4},{1,5},{2,6},{3,7},{4,0},{5,1},{6,2},{7,3},{8,12},{9,13},{10,... | collective-permute-start | bytes 147464 | tf_op jit(solution)/shard_map/cond/branch_0_fun/ppermute | solution.py:482
  85.0 7.2 %collective-permute-start.15 = (f32[48,256]{1,0:T(8,128)S(1)}, f32[48,256]{1,0:T(8,128)S(1)}, u32[]{:S(2)}, u32[]{:S(2)}) collective-permute-start(f32[48,256]{1,0:T(8,128)S(1)} %get-tuple-element.83), channel_id=1, source_target_pairs={{0,6},{1,7},{2,4},{3,5},{4,2},{5,3},{6,0},{7,1},{8,14},{9,15},{10,... | collective-permute-start | bytes 147464 | tf_op jit(solution)/shard_map/cond/branch_0_fun/ppermute | solution.py:482
  86.3 6.6 %collective-permute-start.7 = (f32[80,256]{1,0:T(8,128)S(1)}, f32[80,256]{1,0:T(8,128)S(1)}, u32[]{:S(2)}, u32[]{:S(2)}) collective-permute-start(f32[80,256]{1,0:T(8,128)S(1)} %get-tuple-element.81), channel_id=1, source_target_pairs={{0,8},{1,9},{2,10},{3,11},{4,12},{5,13},{6,14},{7,15},{8,0},{9,1},... | collective-permute-start | bytes 245768 | tf_op jit(solution)/shard_map/cond/branch_0_fun/ppermute | solution.py:482
  89.8 7.9 %collective-permute-start.8 = (f32[80,256]{1,0:T(8,128)S(1)}, f32[80,256]{1,0:T(8,128)S(1)}, u32[]{:S(2)}, u32[]{:S(2)}) collective-permute-start(f32[80,256]{1,0:T(8,128)S(1)} %get-tuple-element.79), channel_id=1, source_target_pairs={{0,16},{1,17},{2,18},{3,19},{4,20},{5,21},{6,22},{7,23},{8,24},{9,... | collective-permute-start | bytes 245768 | tf_op jit(solution)/shard_map/cond/branch_0_fun/ppermute | solution.py:482
  90.8 6.9 %collective-permute-start.9 = (f32[80,256]{1,0:T(8,128)S(1)}, f32[80,256]{1,0:T(8,128)S(1)}, u32[]{:S(2)}, u32[]{:S(2)}) collective-permute-start(f32[80,256]{1,0:T(8,128)S(1)} %get-tuple-element.80), channel_id=1, source_target_pairs={{0,24},{1,25},{2,26},{3,27},{4,28},{5,29},{6,30},{7,31},{8,16},{9,... | collective-permute-start | bytes 245768 | tf_op jit(solution)/shard_map/cond/branch_0_fun/ppermute | solution.py:482
  98.1 0.7 copy-start
